TPU v7x, 32 devices: a whole 2x2x4 slice. The times are simulated.
32 devices in a mesh: fsdp: 8 (over z, x), seq: 4 (over y, core).
Axes of the slice: x: 2, y: 2, z: 4, core: 2. Of those that a mesh axis runs over, the one named last changes fastest.
Arguments:
- tokens: bfloat16 [16384, 768], P(('fsdp', 'seq')), may hold values from -6 to 6
- read_memory: bfloat16 [8, 10, 768], P('fsdp'), may hold values from -6 to 6
- write_memory: bfloat16 [8, 10, 768], P('fsdp'), may hold values from -6 to 6
- lengths: int32 [8], P('fsdp'), may hold values from 1024 to 2048, as said below
- qkv_weight: bfloat16 [768, 2304], P('fsdp'), may hold values from -0.21875 to 0.21875
- qv_bias: bfloat16 [1536], P('fsdp'), may hold values from -1.5 to 1.5
- out_weight: bfloat16 [768, 768], P('fsdp'), may hold values from -6 to 6
- out_bias: bfloat16 [768], P('fsdp'), may hold values from -1.5 to 1.5
- norm1_gain: bfloat16 [768], P('fsdp'), may hold values from 0.5 to 1.5
- norm1_bias: bfloat16 [768], P('fsdp'), may hold values from -1.5 to 1.5
- up_weight: bfloat16 [768, 3072], P('fsdp'), may hold values from -0.21875 to 0.21875
- up_bias: bfloat16 [3072], P('fsdp'), may hold values from -1.5 to 1.5
- down_weight: bfloat16 [3072, 768], P('fsdp'), may hold values from -0.109375 to 0.109375
- down_bias: bfloat16 [768], P('fsdp'), may hold values from -1.5 to 1.5
- norm2_gain: bfloat16 [768], P('fsdp'), may hold values from 0.5 to 1.5
- norm2_bias: bfloat16 [768], P('fsdp'), may hold values from -1.5 to 1.5
- cotangent: bfloat16 [16384, 768], P(('fsdp', 'seq')), may hold values from -6 to 6
Outputs:
- output: bfloat16 [16384, 768], P(('fsdp', 'seq'))
- input_grad: float32 [16384, 768], P(('fsdp', 'seq'))
- read_grad: float32 [8, 10, 768], P('fsdp')
- write_grad: float32 [8, 10, 768], P('fsdp')
- qkv_weight_grad: float32 [768, 2304], P('fsdp')
- qv_bias_grad: float32 [1536], P('fsdp')
- out_weight_grad: float32 [768, 768], P('fsdp')
- out_bias_grad: float32 [768], P('fsdp')
- norm1_gain_grad: float32 [768], P('fsdp')
- norm1_bias_grad: float32 [768], P('fsdp')
- up_weight_grad: float32 [768, 3072], P('fsdp')
- up_bias_grad: float32 [3072], P('fsdp')
- down_weight_grad: float32 [3072, 768], P('fsdp')
- down_bias_grad: float32 [768], P('fsdp')
- norm2_gain_grad: float32 [768], P('fsdp')
- norm2_bias_grad: float32 [768], P('fsdp')
Inputs may be any that keep to these rules, and one draw needn't show every extreme that they name: `lengths`: valid length of each slot in positions, counting its 10 read and 10 write memory tokens; in every draw some slot has length 2048 and some slot 1024.
All inputs are finite; a program needn't handle non-finite values.
Results may differ from a plain program's by a relative error of at most 0.017.
Values may be sent and summed in bfloat16 or wider, within the bound.
A program may use at most 128 MiB of HBM per device.

v0:
```python
from functools import partial

import jax
import jax.numpy as jnp
from jax import lax
from jax.sharding import PartitionSpec as P

HEAD = 64
MEM = 10


norm_epsilon = 1e-06
masked_score = -1e30


def normalize(values, gain_vec, shift_vec):
    centre = values - jnp.mean(values, axis=-1, keepdims=True)
    factor = lax.rsqrt(jnp.mean(centre * centre, axis=-1, keepdims=True) + norm_epsilon)
    return centre * factor * gain_vec + shift_vec


def over_rows(left, right):
    return lax.dot_general(
        left, right, (((0,), (0,)), ((), ())), preferred_element_type=jnp.float32
    )


def by_columns(left, right):
    return lax.dot_general(
        left, right, (((1,), (1,)), ((), ())), preferred_element_type=jnp.float32
    )


def column_sums(values):
    return jnp.sum(values, axis=0, dtype=jnp.float32)


def per_device(
    tokens,
    read_memory,
    write_memory,
    lengths,
    qkv_weight,
    qv_bias,
    out_weight,
    out_bias,
    norm1_gain,
    norm1_bias,
    up_weight,
    up_bias,
    down_weight,
    down_bias,
    norm2_gain,
    norm2_bias,
    cotangent,
):
    seq_count = lax.axis_size("seq")
    local_rows = tokens.shape[0]
    model_width = tokens.shape[1]
    slot_rows = local_rows * seq_count
    head_cols = model_width // seq_count
    head_count = head_cols // HEAD
    block_rows = min(512, slot_rows)
    block_count = slot_rows // block_rows
    factor = HEAD ** (-0.5)
    length = lengths[0]
    places = lax.axis_index("seq") * local_rows + jnp.arange(local_rows, dtype=jnp.int32)
    in_slot = (places < length)[:, None]
    memory_slots = jnp.arange(MEM, dtype=jnp.int32)
    pick_read = places[:, None] == memory_slots[None, :]
    pick_write = places[:, None] == length - MEM + memory_slots[None, :]
    is_memory = jnp.any(pick_read | pick_write, axis=1)[:, None]
    read_float = pick_read.astype(jnp.float32)
    write_float = pick_write.astype(jnp.float32)
    memory_rows = jnp.dot(
        read_float.astype(jnp.bfloat16), read_memory[0], preferred_element_type=jnp.float32
    ) + jnp.dot(
        write_float.astype(jnp.bfloat16), write_memory[0], preferred_element_type=jnp.float32
    )
    layer_in = jnp.where(is_memory, memory_rows.astype(jnp.bfloat16), tokens)
    qkv_full, qv_full, out_full, out_bias_full, gain_one, shift_one = (
        lax.all_gather(qkv_weight, "fsdp", axis=0, tiled=True),
        lax.all_gather(qv_bias, "fsdp", axis=0, tiled=True),
        lax.all_gather(out_weight, "fsdp", axis=0, tiled=True),
        lax.all_gather(out_bias, "fsdp", axis=0, tiled=True),
        lax.all_gather(norm1_gain, "fsdp", axis=0, tiled=True),
        lax.all_gather(norm1_bias, "fsdp", axis=0, tiled=True),
    )
    projected = jnp.dot(layer_in, qkv_full, preferred_element_type=jnp.float32)
    qv_vec = qv_full.astype(jnp.float32)
    query_tok = (projected[:, :model_width] + qv_vec[:model_width]).astype(jnp.bfloat16)
    keys_tok = projected[:, model_width : 2 * model_width].astype(jnp.bfloat16)
    values_tok = (projected[:, 2 * model_width :] + qv_vec[model_width:]).astype(jnp.bfloat16)
    heads_query, heads_key, heads_value = (
        lax.all_to_all(query_tok, "seq", split_axis=1, concat_axis=0, tiled=True),
        lax.all_to_all(keys_tok, "seq", split_axis=1, concat_axis=0, tiled=True),
        lax.all_to_all(values_tok, "seq", split_axis=1, concat_axis=0, tiled=True),
    )
    heads_query = heads_query.reshape(slot_rows, head_count, HEAD)
    heads_key = heads_key.reshape(slot_rows, head_count, HEAD)
    heads_value = heads_value.reshape(slot_rows, head_count, HEAD)
    key_in_slot = jnp.arange(slot_rows, dtype=jnp.int32) < length

    def scores_for(query_block):
        scores = (
            jnp.einsum("qhd,khd->hqk", query_block, heads_key, preferred_element_type=jnp.float32)
            * factor
        )
        return jnp.where(key_in_slot[None, None, :], scores, masked_score)

    def forward_block(block_index):
        query_block = lax.dynamic_slice_in_dim(heads_query, block_index * block_rows, block_rows, 0)
        scores = scores_for(query_block)
        row_max = jnp.max(scores, axis=-1, keepdims=True)
        exponent = jnp.exp(scores - row_max)
        row_sum = jnp.sum(exponent, axis=-1, keepdims=True)
        probs_low = (exponent / row_sum).astype(jnp.bfloat16)
        mixed_block = jnp.einsum(
            "hqk,khd->qhd", probs_low, heads_value, preferred_element_type=jnp.float32
        )
        return (mixed_block.astype(jnp.bfloat16), row_max, row_sum)

    mixed_blocks, row_maxes, row_sums = lax.map(
        forward_block, jnp.arange(block_count, dtype=jnp.int32)
    )
    mixed_heads = mixed_blocks.reshape(slot_rows, head_cols)
    attended = lax.all_to_all(mixed_heads, "seq", split_axis=0, concat_axis=1, tiled=True)
    branch = jnp.dot(attended, out_full, preferred_element_type=jnp.float32) + out_bias_full.astype(
        jnp.float32
    )
    resid_one = layer_in.astype(jnp.float32) + branch
    middle, norm_one_back = jax.vjp(
        normalize, resid_one, gain_one.astype(jnp.float32), shift_one.astype(jnp.float32)
    )
    up_full, up_bias_full, down_full, down_bias_full, gain_two, shift_two = (
        lax.all_gather(up_weight, "fsdp", axis=0, tiled=True),
        lax.all_gather(up_bias, "fsdp", axis=0, tiled=True),
        lax.all_gather(down_weight, "fsdp", axis=0, tiled=True),
        lax.all_gather(down_bias, "fsdp", axis=0, tiled=True),
        lax.all_gather(norm2_gain, "fsdp", axis=0, tiled=True),
        lax.all_gather(norm2_bias, "fsdp", axis=0, tiled=True),
    )
    middle_low = middle.astype(jnp.bfloat16)
    up_pre = jnp.dot(middle_low, up_full, preferred_element_type=jnp.float32) + up_bias_full.astype(
        jnp.float32
    )
    gelu_out, gelu_back = jax.vjp(partial(jax.nn.gelu, approximate=False), up_pre)
    hidden = gelu_out.astype(jnp.bfloat16)
    down_pre = jnp.dot(
        hidden, down_full, preferred_element_type=jnp.float32
    ) + down_bias_full.astype(jnp.float32)
    final, norm_two_back = jax.vjp(
        normalize, middle + down_pre, gain_two.astype(jnp.float32), shift_two.astype(jnp.float32)
    )
    output = jnp.where(in_slot, final, 0.0).astype(jnp.bfloat16)
    grad_final = jnp.where(in_slot, cotangent.astype(jnp.float32), 0.0)
    down_back, up_back = (
        lax.all_gather(down_weight, "fsdp", axis=0, tiled=True),
        lax.all_gather(up_weight, "fsdp", axis=0, tiled=True),
    )
    grad_resid_two, grad_gain_two, grad_shift_two = norm_two_back(grad_final)
    grad_down = grad_resid_two.astype(jnp.bfloat16)
    grad_down_bias = column_sums(grad_down)
    grad_down_weight = over_rows(hidden, grad_down)
    grad_hidden = by_columns(grad_down, down_back)
    (grad_up_pre,) = gelu_back(grad_hidden)
    grad_up = grad_up_pre.astype(jnp.bfloat16)
    grad_up_bias = column_sums(grad_up)
    grad_up_weight = over_rows(middle_low, grad_up)
    grad_middle = grad_resid_two + by_columns(grad_up, up_back)
    grad_resid_one, grad_gain_one, grad_shift_one = norm_one_back(grad_middle)
    out_back, qkv_back = (
        lax.all_gather(out_weight, "fsdp", axis=0, tiled=True),
        lax.all_gather(qkv_weight, "fsdp", axis=0, tiled=True),
    )
    grad_branch = grad_resid_one.astype(jnp.bfloat16)
    grad_out_bias = column_sums(grad_branch)
    grad_out_weight = over_rows(attended, grad_branch)
    grad_attended = by_columns(grad_branch, out_back).astype(jnp.bfloat16)
    grad_heads = lax.all_to_all(grad_attended, "seq", split_axis=1, concat_axis=0, tiled=True)
    grad_heads = grad_heads.reshape(slot_rows, head_count, HEAD)

    def backward_block(carry, block_item):
        key_sum, value_sum = carry
        block_index, row_max, row_sum = block_item
        query_block = lax.dynamic_slice_in_dim(heads_query, block_index * block_rows, block_rows, 0)
        grad_block = lax.dynamic_slice_in_dim(grad_heads, block_index * block_rows, block_rows, 0)
        scores = scores_for(query_block)
        attn_probs = jnp.exp(scores - row_max) / row_sum
        probs_low = attn_probs.astype(jnp.bfloat16)
        grad_probs = jnp.einsum(
            "qhd,khd->hqk", grad_block, heads_value, preferred_element_type=jnp.float32
        )
        row_delta = jnp.sum(grad_probs * attn_probs, axis=-1, keepdims=True)
        grad_scores = (attn_probs * (grad_probs - row_delta)).astype(jnp.bfloat16)
        grad_query = (
            jnp.einsum("hqk,khd->qhd", grad_scores, heads_key, preferred_element_type=jnp.float32)
            * factor
        )
        key_sum = (
            key_sum
            + jnp.einsum(
                "hqk,qhd->khd", grad_scores, query_block, preferred_element_type=jnp.float32
            )
            * factor
        )
        value_sum = value_sum + jnp.einsum(
            "hqk,qhd->khd", probs_low, grad_block, preferred_element_type=jnp.float32
        )
        return ((key_sum, value_sum), grad_query.astype(jnp.bfloat16))

    zero_heads = jnp.zeros((slot_rows, head_count, HEAD), jnp.float32)
    (key_total, value_total), query_blocks = lax.scan(
        backward_block,
        (zero_heads, zero_heads),
        (jnp.arange(block_count, dtype=jnp.int32), row_maxes, row_sums),
    )
    grad_query_heads = query_blocks.reshape(slot_rows, head_cols)
    grad_key_heads = key_total.reshape(slot_rows, head_cols).astype(jnp.bfloat16)
    grad_value_heads = value_total.reshape(slot_rows, head_cols).astype(jnp.bfloat16)
    grad_query_tok, grad_key_tok, grad_value_tok = (
        lax.all_to_all(grad_query_heads, "seq", split_axis=0, concat_axis=1, tiled=True),
        lax.all_to_all(grad_key_heads, "seq", split_axis=0, concat_axis=1, tiled=True),
        lax.all_to_all(grad_value_heads, "seq", split_axis=0, concat_axis=1, tiled=True),
    )
    grad_projected = jnp.concatenate([grad_query_tok, grad_key_tok, grad_value_tok], axis=1)
    grad_qv_bias = jnp.concatenate([column_sums(grad_query_tok), column_sums(grad_value_tok)])
    grad_qkv_weight = over_rows(layer_in, grad_projected)
    grad_layer_in = grad_resid_one + by_columns(grad_projected, qkv_back)
    input_grad = jnp.where(is_memory, 0.0, grad_layer_in)
    grad_read = lax.dot_general(
        read_float,
        grad_layer_in,
        (((0,), (0,)), ((), ())),
        precision=lax.Precision.HIGHEST,
        preferred_element_type=jnp.float32,
    )
    grad_write = lax.dot_general(
        write_float,
        grad_layer_in,
        (((0,), (0,)), ((), ())),
        precision=lax.Precision.HIGHEST,
        preferred_element_type=jnp.float32,
    )
    (
        shard_qkv,
        shard_qv,
        shard_out_w,
        shard_out_b,
        shard_gain_one,
        shard_shift_one,
        shard_up_w,
        shard_up_b,
        shard_down_w,
        shard_down_b,
        shard_gain_two,
        shard_shift_two,
    ) = (
        lax.psum_scatter(grad_qkv_weight, "fsdp", scatter_dimension=0, tiled=True),
        lax.psum_scatter(grad_qv_bias, "fsdp", scatter_dimension=0, tiled=True),
        lax.psum_scatter(grad_out_weight, "fsdp", scatter_dimension=0, tiled=True),
        lax.psum_scatter(grad_out_bias, "fsdp", scatter_dimension=0, tiled=True),
        lax.psum_scatter(grad_gain_one, "fsdp", scatter_dimension=0, tiled=True),
        lax.psum_scatter(grad_shift_one, "fsdp", scatter_dimension=0, tiled=True),
        lax.psum_scatter(grad_up_weight, "fsdp", scatter_dimension=0, tiled=True),
        lax.psum_scatter(grad_up_bias, "fsdp", scatter_dimension=0, tiled=True),
        lax.psum_scatter(grad_down_weight, "fsdp", scatter_dimension=0, tiled=True),
        lax.psum_scatter(grad_down_bias, "fsdp", scatter_dimension=0, tiled=True),
        lax.psum_scatter(grad_gain_two, "fsdp", scatter_dimension=0, tiled=True),
        lax.psum_scatter(grad_shift_two, "fsdp", scatter_dimension=0, tiled=True),
    )
    (
        sum_qkv,
        sum_qv,
        sum_out_w,
        sum_out_b,
        sum_gain_one,
        sum_shift_one,
        sum_up_w,
        sum_up_b,
        sum_down_w,
        sum_down_b,
        sum_gain_two,
        sum_shift_two,
        read_total,
        write_total,
    ) = (
        lax.psum(shard_qkv.astype(jnp.bfloat16), "seq").astype(jnp.float32),
        lax.psum(shard_qv.astype(jnp.bfloat16), "seq").astype(jnp.float32),
        lax.psum(shard_out_w.astype(jnp.bfloat16), "seq").astype(jnp.float32),
        lax.psum(shard_out_b.astype(jnp.bfloat16), "seq").astype(jnp.float32),
        lax.psum(shard_gain_one.astype(jnp.bfloat16), "seq").astype(jnp.float32),
        lax.psum(shard_shift_one.astype(jnp.bfloat16), "seq").astype(jnp.float32),
        lax.psum(shard_up_w.astype(jnp.bfloat16), "seq").astype(jnp.float32),
        lax.psum(shard_up_b.astype(jnp.bfloat16), "seq").astype(jnp.float32),
        lax.psum(shard_down_w.astype(jnp.bfloat16), "seq").astype(jnp.float32),
        lax.psum(shard_down_b.astype(jnp.bfloat16), "seq").astype(jnp.float32),
        lax.psum(shard_gain_two.astype(jnp.bfloat16), "seq").astype(jnp.float32),
        lax.psum(shard_shift_two.astype(jnp.bfloat16), "seq").astype(jnp.float32),
        lax.psum(grad_read.astype(jnp.bfloat16), "seq").astype(jnp.float32),
        lax.psum(grad_write.astype(jnp.bfloat16), "seq").astype(jnp.float32),
    )
    return (
        output,
        input_grad,
        read_total[None],
        write_total[None],
        sum_qkv,
        sum_qv,
        sum_out_w,
        sum_out_b,
        sum_gain_one,
        sum_shift_one,
        sum_up_w,
        sum_up_b,
        sum_down_w,
        sum_down_b,
        sum_gain_two,
        sum_shift_two,
    )


def solution(mesh):
    in_specs = (
        P(("fsdp", "seq"), None),
        P("fsdp", None, None),
        P("fsdp", None, None),
        P("fsdp"),
        P("fsdp", None),
        P("fsdp"),
        P("fsdp", None),
        P("fsdp"),
        P("fsdp"),
        P("fsdp"),
        P("fsdp", None),
        P("fsdp"),
        P("fsdp", None),
        P("fsdp"),
        P("fsdp"),
        P("fsdp"),
        P(("fsdp", "seq"), None),
    )
    out_specs = (
        P(("fsdp", "seq"), None),
        P(("fsdp", "seq"), None),
        P("fsdp", None, None),
        P("fsdp", None, None),
        P("fsdp", None),
        P("fsdp"),
        P("fsdp", None),
        P("fsdp"),
        P("fsdp"),
        P("fsdp"),
        P("fsdp", None),
        P("fsdp"),
        P("fsdp", None),
        P("fsdp"),
        P("fsdp"),
        P("fsdp"),
    )
    return jax.shard_map(
        per_device, mesh=mesh, in_specs=in_specs, out_specs=out_specs, check_vma=False
    )
```

profile of v0, /device:TPU:9, one launch (start us, length us, event | category | flops | bytes accessed | tf_op | source)
XLA Modules:
  0.0 1021.1 jit_solution(4488948586990560364)
XLA Ops:
  18.6 28.7 %all-reduce.16 = (bf16[1536]{0:T(1024)(128)(2,1)S(1)}, bf16[768]{0:T(1024)(128)(2,1)S(1)}, bf16[768]{0:T(1024)(128)(2,1)S(1)}, bf16[768]{0:T(1024)(128)(2,1)S(1)...) all-reduce(bf16[1536]{0:T(1024)(128)(2,1)S(1)} %dynamic-update-slic, ...), channel_id=1, replica_groups=mesh['fsdp'=8,'seq'=4] {'fsdp'}, use_global_device_ids=true, to_apply=%add | all-reduce | flops 6144 | bytes 24576
  49.5 26.2 %all-gather.6.cloned.1.call-done = bf16[768,2304]{1,0:T(8,128)(2,1)} async-done(((bf16[96,2304]{1,0:T(8,128)(2,1)}), bf16[768,2304]{1,0:T(8,128)(2,1)}) %all-gather.6.cloned.1.call-update) | async-done | bytes 3538960 | tf_op jit(solution)/shard_map/all_gather | solution.py:82
  83.4 5.4 all-to-all-start
  89.9 9.6 all-to-all-done
  106.5 8.2 all-to-all-done.2
  124.4 5.4 all-to-all-done.1
  134.3 44.2 %while.30 = (s32[]{:T(128)}, bf16[4,512,3,64]{1,3,2,0:T(8,128)(2,1)}, f32[4,3,512,1]{2,1,3,0:T(4,128)S(1)}, f32[4,3,512,1]{2,1,3,0:T(4,128)S(1)}, s32[4]{0:T(128...) while((s32[]{:T(128)}, ...), condition=%wide.region_4.5_spmd.clone, body=%wide.region_1.4_spmd.clone.sunk | while | flops 843152384 | bytes 39787204 | solution.py:123
  182.9 21.0 %all-gather = bf16[8,1,384]{2,1,0:T(2,128)(2,1)S(1)} all-gather(bf16[1,1,384]{2,1,0:T(2,128)(2,1)S(1)} %reshape.204), channel_id=1, replica_groups=mesh['fsdp'=8,'seq'=4] {'fsdp'}, dimensions={0}, use_global_device_ids=true | all-gather | bytes 6912 | tf_op jit(solution)/shard_map/all_gather | solution.py:137
  207.9 21.3 %multiply_convert_fusion.1 = (bf16[512,3072]{1,0:T(8,128)(2,1)}, f32[512,3072]{1,0:T(8,128)}, f32[512,3072]{1,0:T(8,128)}) fusion(f32[3072]{0:T(1024)S(1)} %bitcast.154, bf16[768,3072]{1,0:T(8,128)(2,1)} %all-gather.10.cloned.1.call-done, f32[512,768]{1,0:T(8,128)} %copy-done.7, f32[768]{0:T(1024)S(1)} %convert_element_type.216, ...), kind=kOutput, calls=%fused_computation.49 | convolution fusion | flops 2521694208 | bytes 22042624 | tf_op jit(solution)/shard_map/dot_general | solution.py:144
  229.2 48.9 %all-gather.12.cloned.1.call-done = bf16[3072,768]{1,0:T(8,128)(2,1)} async-done(((bf16[384,768]{1,0:T(8,128)(2,1)}), bf16[3072,768]{1,0:T(8,128)(2,1)}) %all-gather.12.cloned.1.call-update) | async-done | bytes 4718608 | tf_op jit(solution)/shard_map/all_gather | solution.py:138
  278.1 6.1 fusion.79
  288.5 8.9 convert_reduce_fusion
  305.6 5.8 all-to-all-start.4
  314.9 7.5 all-to-all-done.4
  328.8 115.5 %while.31 = (s32[]{:T(128)}, f32[2048,3,64]{0,2,1:T(8,128)S(1)}, f32[2048,3,64]{0,2,1:T(8,128)}, bf16[4,512,3,64]{1,3,2,0:T(8,128)(2,1)}, s32[4]{0:T(128)S(1)}, ...) while((s32[]{:T(128)}, f32[2048,3,64]{0,2,1:T(8,128)S(1)}, ...), condition=%wide.region_15.16_spmd.clone, body=%wide.region_13.15_spmd.clone.sunk | while | flops 2046886400 | bytes 204722992 | solution.py:213
  347.6 6.3 fusion.145
  376.0 6.3 fusion.145
  405.0 6.3 fusion.145
  434.0 6.3 fusion.145
  452.6 8.5 all-to-all-done.6
  461.0 13.9 %all_to_all.134 = bf16[4,512,192]{1,2,0:T(8,128)(2,1)S(1)} all-to-all(bf16[4,512,192]{1,2,0:T(8,128)(2,1)S(1)} %copy.93), channel_id=1, replica_groups=mesh['fsdp'=8,'seq'=4] {'seq'}, dimensions={0} | all-to-all | bytes 1572864 | tf_op jit(solution)/shard_map/all_to_all | solution.py:224
  474.9 14.3 %all_to_all.135 = bf16[4,512,192]{1,2,0:T(8,128)(2,1)S(1)} all-to-all(bf16[4,512,192]{1,2,0:T(8,128)(2,1)S(1)} %bitcast.149), channel_id=1, replica_groups=mesh['fsdp'=8,'seq'=4] {'seq'}, dimensions={0} | all-to-all | bytes 1572864 | tf_op jit(solution)/shard_map/all_to_all | solution.py:222
  489.2 6.4 fusion.51
  496.7 8.3 fusion.82
  506.4 7.2 fusion.69
  516.4 28.7 %all-reduce.15 = (bf16[1536]{0:T(1024)(128)(2,1)S(1)}, bf16[768]{0:T(1024)(128)(2,1)S(1)}, bf16[768]{0:T(1024)(128)(2,1)S(1)}, bf16[768]{0:T(1024)(128)(2,1)S(1)...) all-reduce(f32[1536]{0:T(1024)S(1)} %pad_maximum_fusion.3, ...), channel_id=3, replica_groups=mesh['fsdp'=8,'seq'=4] {'fsdp'}, use_global_device_ids=true, to_apply=%region_22.23.clone | all-reduce | flops 9216 | bytes 55296
  547.5 76.0 %reduce-scatter.5.cloned.1.call-done = f32[96,2304]{1,0:T(8,128)} async-done(((f32[768,2304]{1,0:T(8,128)}), f32[96,2304]{1,0:T(8,128)}) %reduce-scatter.5.cloned.1.call-update) | async-done | bytes 884752 | tf_op jit(solution)/shard_map/reduce_scatter | solution.py:259
  625.4 164.3 %reduce-scatter.11.cloned.1.call-done = f32[384,768]{1,0:T(8,128)} async-done(((f32[3072,768]{1,0:T(8,128)}), f32[384,768]{1,0:T(8,128)}) %reduce-scatter.11.cloned.1.call-update) | async-done | bytes 1179664 | tf_op jit(solution)/shard_map/reduce_scatter | solution.py:267
  791.8 164.3 %reduce-scatter.9.cloned.1.call-done = f32[96,3072]{1,0:T(8,128)} async-done(((f32[768,3072]{1,0:T(8,128)}), f32[96,3072]{1,0:T(8,128)}) %reduce-scatter.9.cloned.1.call-update) | async-done | bytes 1179664 | tf_op jit(solution)/shard_map/reduce_scatter | solution.py:265
  958.3 5.6 broadcast_select_fusion
  965.2 13.0 %all-reduce.17 = (bf16[1,10,768]{2,1,0:T(8,128)(2,1)S(1)}, bf16[1,10,768]{2,1,0:T(8,128)(2,1)S(1)}, bf16[192]{0:T(256)(128)(2,1)S(1)}, bf16[96]{0:T(256)(128)(2,...) all-reduce(bf16[1,10,768]{2,1,0:T(8,128)(2,1)S(1)} %fusion.49, ...), channel_id=1, replica_groups=mesh['fsdp'=8,'seq'=4] {'seq'}, use_global_device_ids=true, to_apply=%region_16.17 | all-reduce | flops 16512 | bytes 66048 | tf_op jit(solution)/shard_map/psum | solution.py:300
  983.7 24.5 %all-reduce.21.cloned.1.call-done = (bf16[96,2304]{1,0:T(8,128)(2,1)}, bf16[96,768]{1,0:T(8,128)(2,1)}, bf16[96,3072]{1,0:T(8,128)(2,1)}, bf16[384,768]{1,0:T(8,128)(2,1)}) async-done(((bf16[96,2304]{1,0:T(8,128)(2,1)}, bf16[96,768]{1,0:T(8,128)(2,1)}, bf16[96,3072]{1,0:T(8,128)(2,1)}, bf16[384,768]{1,0:T(8,128)(2,1)}), (bf16[96,2304]{1,0:T(8,128)(2,1)}, bf16[96,768]{1,0:T(8,128)(2,1)}, ...) | async-done | bytes 1769488 | tf_op jit(solution)/shard_map/psum | solution.py:288
  (308 shorter events, 233.9 us)
Async XLA Ops:
  7.2 40.2 %copy-start = (bf16[1,10,768]{2,1,0:T(8,128)(2,1)S(1)}, bf16[1,10,768]{2,1,0:T(8,128)(2,1)}, u32[]{:S(2)}) copy-start(bf16[1,10,768]{2,1,0:T(8,128)(2,1)} %param.22) | copy-start | bytes 46084
  7.2 68.5 %all-gather.6.cloned.1.call-start = ((), (), s32[]{:S(2)}) async-start(), calls=%async_computation.12 | async-start | bytes 3981312 | tf_op jit(solution)/shard_map/all_gather | solution.py:82
  7.9 196.0 %all-gather.8.cloned.1.call-start = ((), (), s32[]{:S(2)}) async-start(), calls=%async_computation.13 | async-start | bytes 1327104 | tf_op jit(solution)/shard_map/all_gather | solution.py:84
  8.7 199.2 %all-gather.10.cloned.1.call-start = ((), (), s32[]{:S(2)}) async-start(), calls=%async_computation.14 | async-start | bytes 5308416 | tf_op jit(solution)/shard_map/all_gather | solution.py:136
  47.2 32.5 %copy-start.37 = (s32[10]{0:T(128)}, s32[10]{0:T(128)S(1)}, u32[]{:S(2)}) copy-start(s32[10]{0:T(128)S(1)} %iota_add_fusion.1) | copy-start | bytes 124
  47.3 32.4 %copy-start.43 = (pred[512]{0:T(512)(128)(4,1)}, pred[512]{0:T(512)(128)(4,1)S(1)}, u32[]{:S(2)}) copy-start(pred[512]{0:T(512)(128)(4,1)S(1)} %fusion.54) | copy-start | bytes 1540
  49.5 30.3 %copy-start.17 = (bf16[512,768]{1,0:T(8,128)(2,1)}, bf16[512,768]{1,0:T(8,128)(2,1)S(1)}, u32[]{:S(2)}) copy-start(bf16[512,768]{1,0:T(8,128)(2,1)S(1)} %fusion.47) | copy-start | bytes 2359300
  83.4 16.2 %all-to-all-start = ((bf16[512,4,192]{0,2,1:T(8,128)(2,1)}), bf16[512,4,192]{0,2,1:T(8,128)(2,1)S(1)}, u32[]{:S(2)}, u32[]{:S(2)}) async-start(bf16[512,4,192]{0,2,1:T(8,128)(2,1)} %bitcast.4), calls=%async_computation | async-start | bytes 1572864 | tf_op jit(solution)/shard_map/all_to_all | solution.py:95
  99.5 15.2 %all-to-all-start.2 = ((bf16[512,4,192]{0,2,1:T(8,128)(2,1)}), bf16[512,4,192]{0,2,1:T(8,128)(2,1)S(1)}, u32[]{:S(2)}, u32[]{:S(2)}) async-start(bf16[512,4,192]{0,2,1:T(8,128)(2,1)} %bitcast.8), calls=%async_computation.2 | async-start | bytes 1572864 | tf_op jit(solution)/shard_map/all_to_all | solution.py:97
  114.7 15.0 %all-to-all-start.1 = ((bf16[512,4,192]{0,2,1:T(8,128)(2,1)}), bf16[512,4,192]{0,2,1:T(8,128)(2,1)S(1)}, u32[]{:S(2)}, u32[]{:S(2)}) async-start(bf16[512,4,192]{0,2,1:T(8,128)(2,1)} %bitcast.6), calls=%async_computation.1 | async-start | bytes 1572864 | tf_op jit(solution)/shard_map/all_to_all | solution.py:96
  119.0 159.1 %all-gather.12.cloned.1.call-start = ((), (), s32[]{:S(2)}) async-start(), calls=%async_computation.15 | async-start | bytes 5308416 | tf_op jit(solution)/shard_map/all_gather | solution.py:138
  134.3 48.5 %copy-start.45 = (bf16[384]{0:T(512)(128)(2,1)S(1)}, bf16[384]{0:T(512)(128)(2,1)}, u32[]{:S(2)}) copy-start(bf16[384]{0:T(512)(128)(2,1)} %param.32) | copy-start | bytes 2308
  178.5 29.3 %copy-start.4 = (bf16[2048,3,64]{0,2,1:T(8,128)(2,1)}, bf16[2048,3,64]{0,2,1:T(8,128)(2,1)S(1)}, u32[]{:S(2)}) copy-start(bf16[2048,3,64]{0,2,1:T(8,128)(2,1)S(1)} %get-tuple-element.654) | copy-start | bytes 2359300
  178.5 29.3 %copy-start.6 = (bf16[2048,3,64]{0,2,1:T(8,128)(2,1)}, bf16[2048,3,64]{0,2,1:T(8,128)(2,1)S(1)}, u32[]{:S(2)}) copy-start(bf16[2048,3,64]{0,2,1:T(8,128)(2,1)S(1)} %get-tuple-element.655) | copy-start | bytes 2359300
  178.5 25.4 %all-to-all-start.3 = ((bf16[4,512,192]{1,2,0:T(8,128)(2,1)}), bf16[4,512,192]{1,2,0:T(8,128)(2,1)S(1)}, u32[]{:S(2)}, u32[]{:S(2)}) async-start(bf16[4,512,192]{1,2,0:T(8,128)(2,1)} %bitcast.10), calls=%async_computation.3 | async-start | bytes 1572864 | tf_op jit(solution)/shard_map/all_to_all | solution.py:127
  182.8 118.2 %copy-start.30 = (f32[768]{0:T(1024)}, f32[768]{0:T(1024)S(1)}, u32[]{:S(2)}) copy-start(f32[768]{0:T(1024)S(1)} %convert_element_type.215) | copy-start | bytes 9220
  182.9 95.2 %copy-start.39 = (f32[768]{0:T(1024)}, f32[768]{0:T(1024)S(1)}, u32[]{:S(2)}) copy-start(f32[768]{0:T(1024)S(1)} %convert_element_type.216) | copy-start | bytes 9220
  206.4 94.6 %copy-start.24 = (f32[512]{0:T(512)}, f32[512]{0:T(512)S(1)}, u32[]{:S(2)}) copy-start(f32[512]{0:T(512)S(1)} %broadcast_multiply_fusion.1) | copy-start | bytes 6148
  207.9 93.2 %copy-start.33 = (f32[512]{0:T(512)}, f32[512]{0:T(512)S(1)}, u32[]{:S(2)}) copy-start(f32[512]{0:T(512)S(1)} %fusion.65) | copy-start | bytes 6148
  207.9 70.2 %copy-start.8 = (f32[512,768]{1,0:T(8,128)S(1)}, f32[512,768]{1,0:T(8,128)}, u32[]{:S(2)}) copy-start(f32[512,768]{1,0:T(8,128)} %copy-done.7) | copy-start | bytes 4718596
  305.6 16.7 %all-to-all-start.4 = ((bf16[512,4,192]{0,2,1:T(8,128)(2,1)}), bf16[512,4,192]{0,2,1:T(8,128)(2,1)}, u32[]{:S(2)}, u32[]{:S(2)}) async-start(bf16[512,4,192]{0,2,1:T(8,128)(2,1)} %bitcast.15), calls=%async_computation.4 | async-start | bytes 1572864 | tf_op jit(solution)/shard_map/all_to_all | solution.py:180
  311.5 234.2 %reduce-scatter.7.cloned.1.call-start = ((), (), s32[]{:S(2)}) async-start(), calls=%async_computation.17 | async-start | bytes 2654208 | tf_op jit(solution)/shard_map/reduce_scatter | solution.py:261
  446.0 15.1 %all-to-all-start.6 = ((bf16[4,512,192]{1,2,0:T(8,128)(2,1)}), bf16[4,512,192]{1,2,0:T(8,128)(2,1)S(1)}, u32[]{:S(2)}, u32[]{:S(2)}) async-start(bf16[4,512,192]{1,2,0:T(8,128)(2,1)} %copy.92), calls=%async_computation.6 | async-start | bytes 1572864 | tf_op jit(solution)/shard_map/all_to_all | solution.py:223
  450.2 173.2 %reduce-scatter.5.cloned.1.call-start = ((), (), s32[]{:S(2)}) async-start(), calls=%async_computation.16 | async-start | bytes 7962624 | tf_op jit(solution)/shard_map/reduce_scatter | solution.py:259
  450.3 24.7 %copy-start.14 = (bf16[4,512,3,64]{1,3,2,0:T(8,128)(2,1)S(1)}, bf16[4,512,3,64]{1,3,2,0:T(8,128)(2,1)}, u32[]{:S(2)}) copy-start(bf16[4,512,3,64]{1,3,2,0:T(8,128)(2,1)} %get-tuple-element.132) | copy-start | bytes 2359300
  495.6 294.1 %reduce-scatter.11.cloned.1.call-start = ((), (), s32[]{:S(2)}) async-start(), calls=%async_computation.19 | async-start | bytes 10616832 | tf_op jit(solution)/shard_map/reduce_scatter | solution.py:267
  505.0 451.1 %reduce-scatter.9.cloned.1.call-start = ((), (), s32[]{:S(2)}) async-start(), calls=%async_computation.18 | async-start | bytes 10616832 | tf_op jit(solution)/shard_map/reduce_scatter | solution.py:265
  513.7 494.6 %all-reduce.21.cloned.1.call-start = ((), (), s32[]{:S(2)}) async-start(), calls=%async_computation.20 | async-start | bytes 3538944 | tf_op jit(solution)/shard_map/psum | solution.py:288
  545.7 412.6 %copy-start.11 = (f32[512,768]{1,0:T(8,128)S(1)}, f32[512,768]{1,0:T(8,128)}, u32[]{:S(2)}) copy-start(f32[512,768]{1,0:T(8,128)} %copy-done.10) | copy-start | bytes 4718596
  545.7 412.6 %copy-start.36 = (f32[512]{0:T(512)S(1)}, f32[512]{0:T(512)}, u32[]{:S(2)}) copy-start(f32[512]{0:T(512)} %copy-done.35) | copy-start | bytes 6148
  545.7 412.6 %copy-start.44 = (pred[512]{0:T(512)(128)(4,1)S(1)}, pred[512]{0:T(512)(128)(4,1)}, u32[]{:S(2)}) copy-start(pred[512]{0:T(512)(128)(4,1)} %copy-done.43) | copy-start | bytes 1540
  963.9 50.4 %copy-start.1 = (bf16[1,10,768]{2,1,0:T(8,128)(2,1)S(1)}, bf16[1,10,768]{2,1,0:T(8,128)(2,1)}, u32[]{:S(2)}) copy-start(bf16[1,10,768]{2,1,0:T(8,128)(2,1)} %param.22) | copy-start | bytes 46084
  (40 other events, 197.3 us)
Sparse Core Ops, SparseCore 0:
  10.2 65.4 all-gather.5
  77.9 39.5 all-gather.7
  119.7 78.0 all-gather.9
  199.9 78.1 all-gather.11
  315.5 66.1 reduce-scatter.6
  495.7 127.6 reduce-scatter.4
  627.4 162.1 reduce-scatter.10
  793.7 162.3 reduce-scatter.8
  960.1 48.1 all-reduce.20
where the time goes:
time: 1030 us; the launch traced here: 1020 us
  waiting for transfers between devices  546 us (53%)
  matrix products  195 us (19%)
  blocking collectives  119 us (12%)
  other arithmetic  57.2 us (6%)
  local copies, waits for them, and re-layouts  50.3 us (5%)
  starting transfers between devices  28.8 us (3%)
  between operations  18.6 us (2%)
    reduce_scatter x1, waiting for transfers between devices, per_device(): lax.psum_scatter(grad_up_weight, 'fsdp', scatter_dimension=0, tiled=True)  164 us
    reduce_scatter x1, waiting for transfers between devices, per_device(): lax.psum_scatter(grad_down_weight, 'fsdp', scatter_dimension=0, tiled=True)  164 us
    reduce_scatter x1, waiting for transfers between devices, per_device(): lax.psum_scatter(grad_qkv_weight, 'fsdp', scatter_dimension=0, tiled=True)  76 us
    unnamed x2, blocking collectives  57.4 us
    all_gather x1, waiting for transfers between devices, per_device(): lax.all_gather(down_weight, 'fsdp', axis=0, tiled=True)  48.9 us
    all_gather x1, waiting for transfers between devices, per_device(): lax.all_gather(qkv_weight, 'fsdp', axis=0, tiled=True)  26.2 us
    dot_general x8, matrix products, scores_for(): jnp.einsum('qhd,khd->hqk', query_block, heads_key, preferred_element_type...  25.4 us
    dot_general x4, matrix products, over_rows(): lax.dot_general(left, right, (((0,), (0,)), ((), ())), preferred_element_...  25.3 us
  transfers between devices with their start and end apart: 15, of which 11 were waited for; matrix products, arithmetic and copies ran while one was open for 25% of the time, Pallas kernels for 0%

commit v1 on v0

v1 whole, which is shorter than its diff:
```python
from functools import partial

import jax
import jax.numpy as jnp
from jax import lax
from jax.experimental import pallas as pl
from jax.experimental.pallas import tpu as pltpu
from jax.sharding import PartitionSpec as P

HEAD = 64
MEM = 10
WIDE = 128
VMEM_BYTES = 64000 * 1024

norm_epsilon = 1e-06
masked_score = -1e30
low = jnp.bfloat16
full = jnp.float32

NN = (((1,), (0,)), ((), ()))
NT = (((1,), (1,)), ((), ()))
TN = (((0,), (0,)), ((), ()))
TT = (((0,), (1,)), ((), ()))


def mul(left, right, dims=NN):
    return lax.dot_general(left, right, dims, preferred_element_type=full)


def three_parts(value):
    high = value.astype(low)
    rest = value - high.astype(full)
    middle = rest.astype(low)
    return high, middle, (rest - middle.astype(full)).astype(low)


def stack_rows(rows, columns):
    place = lax.broadcasted_iota(jnp.int32, (HEAD, columns), 0)
    block = jnp.zeros((HEAD, columns), full)
    for index, row in enumerate(rows):
        block = jnp.where(place == index, row, block)
    return block.astype(low)


def project_heads(length, rows_ref, weight_ref, bias_ref, q_x, k_t, v_x, k_wide, v_wide):
    slot_rows = rows_ref.shape[0]
    head_cols = k_t.shape[0]
    heads = head_cols // HEAD
    bias = jnp.transpose(bias_ref[...])[:, 0:1]
    step = 512
    for start in range(0, slot_rows, step):
        lanes = slice(start, start + step)
        made = mul(weight_ref[...], rows_ref[lanes, :], TT) + bias[: 3 * head_cols]
        query = made[:head_cols].astype(low) * jnp.asarray(HEAD**-0.5, low)
        k_t[:, lanes] = made[head_cols : 2 * head_cols].astype(low)
        value = made[2 * head_cols :].astype(low)
        place = start + lax.broadcasted_iota(jnp.int32, (1, step), 1)
        key_bias = jnp.where(place < length, 0.0, masked_score)
        one = jnp.ones((1, step), full)
        query_extra = stack_rows([one], step)
        key_extra = stack_rows([key_bias, one, one, one], step)
        value_extra = stack_rows([one, one, one], step)
        for h in range(heads):
            own = slice(h * HEAD, (h + 1) * HEAD)
            q_x[h, :HEAD, lanes] = query[own]
            q_x[h, HEAD:, lanes] = query_extra
            v_x[h, :HEAD, lanes] = value[own]
            v_x[h, HEAD:, lanes] = value_extra
            k_wide[h, lanes, :] = jnp.transpose(
                jnp.concatenate([k_t[own, lanes], key_extra], axis=0)
            )
            v_wide[h, lanes, :] = jnp.transpose(v_x[h, :, lanes])


def attend_block(h, lanes, q_x, k_wide, v_x, mixed, mixed_low, row_stats):
    scores = mul(k_wide[h], q_x[h, :, lanes])
    row_max = jnp.max(scores, axis=0, keepdims=True)
    probs = jnp.exp(scores - row_max).astype(low)
    total = mul(v_x[h, : HEAD + 16], probs)
    row_sum = total[HEAD : HEAD + 1]
    own = pl.ds(h * HEAD, HEAD)
    result = total[:HEAD] / row_sum
    mixed[own, lanes] = result
    mixed_low[own, lanes] = result.astype(low)
    row_stats[h, :, lanes] = jnp.broadcast_to(row_max + jnp.log(row_sum), (8, result.shape[1]))


def forward_kernel(
    length_ref, rows_ref, weight_ref, bias_ref, q_x, k_t, k_wide, v_wide, mixed, mixed_low, row_stats, v_x
):
    project_heads(length_ref[0], rows_ref, weight_ref, bias_ref, q_x, k_t, v_x, k_wide, v_wide)
    heads = q_x.shape[0]
    block = 512
    blocks = q_x.shape[2] // block

    def step(index, carry):
        h = index // blocks
        start = pl.multiple_of(lax.rem(index, blocks) * block, block)
        attend_block(h, pl.ds(start, block), q_x, k_wide, v_x, mixed, mixed_low, row_stats)
        return carry

    lax.fori_loop(0, heads * blocks, step, 0)


def attention_forward(length, rows, weight, bias):
    slot_rows = rows.shape[0]
    head_cols = weight.shape[1] // 3
    heads = head_cols // HEAD
    vmem = pl.BlockSpec(memory_space=pltpu.VMEM)
    return pl.pallas_call(
        forward_kernel,
        in_specs=[pl.BlockSpec(memory_space=pltpu.SMEM), vmem, vmem, vmem],
        out_specs=[vmem] * 7,
        out_shape=[
            jax.ShapeDtypeStruct((heads, WIDE, slot_rows), low),
            jax.ShapeDtypeStruct((head_cols, slot_rows), low),
            jax.ShapeDtypeStruct((heads, slot_rows, WIDE), low),
            jax.ShapeDtypeStruct((heads, slot_rows, WIDE), low),
            jax.ShapeDtypeStruct((head_cols, slot_rows), full),
            jax.ShapeDtypeStruct((head_cols, slot_rows), low),
            jax.ShapeDtypeStruct((heads, 8, slot_rows), full),
        ],
        scratch_shapes=[pltpu.VMEM((heads, WIDE, slot_rows), low)],
        compiler_params=pltpu.CompilerParams(vmem_limit_bytes=VMEM_BYTES),
        name="attention_forward",
    )(length, rows, weight, bias)


def prepare_backward(h, q_x, do_x, grad_t, mixed, row_stats):
    slot_rows = grad_t.shape[1]
    own = slice(h * HEAD, (h + 1) * HEAD)
    grad = grad_t[own, :]
    delta = jnp.sum(grad.astype(full) * mixed[own, :], axis=0, keepdims=True)
    parts = [part.astype(full) for part in three_parts(-delta)]
    do_x[h, :HEAD, :] = grad
    do_x[h, HEAD:, :] = stack_rows(parts, slot_rows)
    parts = [part.astype(full) for part in three_parts(-row_stats[h, 0:1, :])]
    q_x[h, HEAD:, :] = stack_rows([jnp.ones((1, slot_rows), full)] + parts, slot_rows)


def attend_back_block(h, lanes, first, q_x, do_x, k_t, k_wide, v_wide, grad_q, grad_k, grad_v):
    own = pl.ds(h * HEAD, HEAD)
    probs = jnp.exp(mul(k_wide[h], q_x[h, :, lanes]))
    grad_scores = (probs * mul(v_wide[h], do_x[h, :, lanes])).astype(low)
    value_part = mul(do_x[h, :HEAD, lanes], probs.astype(low), NT)
    key_part = mul(q_x[h, :HEAD, lanes], grad_scores, NT)

    @pl.when(first)
    def _():
        grad_v[...] = value_part
        grad_k[...] = key_part

    @pl.when(jnp.logical_not(first))
    def _():
        grad_v[...] += value_part
        grad_k[...] += key_part

    grad_q[own, lanes] = (mul(k_t[own, :], grad_scores) * HEAD**-0.5).astype(low)


def backward_kernel(
    q_in, k_t, k_wide, v_wide, mixed, row_stats, grad_t, rows_ref, weight_ref,
    partial_out, weight_out, sums_out, q_x, do_x, grads, grad_k, grad_v,
):
    heads, _, slot_rows = q_in.shape
    head_cols = heads * HEAD
    q_x[:, :HEAD, :] = q_in[:, :HEAD, :]
    for h in range(heads):
        prepare_backward(h, q_x, do_x, grad_t, mixed, row_stats)
    block = 512
    blocks = slot_rows // block

    def step(index, carry):
        h = index // blocks
        turn = lax.rem(index, blocks)
        start = pl.multiple_of(turn * block, block)
        attend_back_block(
            h, pl.ds(start, block), turn == 0, q_x, do_x, k_t, k_wide, v_wide,
            grads, grad_k, grad_v,
        )

        @pl.when(turn == blocks - 1)
        def _():
            grads[pl.ds(head_cols + h * HEAD, HEAD), :] = grad_k[...].astype(low)
            grads[pl.ds(2 * head_cols + h * HEAD, HEAD), :] = grad_v[...].astype(low)

        return carry

    lax.fori_loop(0, heads * blocks, step, 0)
    for start in range(0, slot_rows, block):
        partial_out[start : start + block, :] = mul(
            grads[:, start : start + block], weight_ref[...], TT
        ).astype(partial_out.dtype)
    weight_out[...] = jnp.transpose(mul(grads[...], rows_ref[...])).astype(weight_out.dtype)
    sums_out[...] = jnp.broadcast_to(
        jnp.sum(grads[...].astype(full), axis=1, keepdims=True), sums_out.shape
    )


def attention_backward(q_x, k_t, k_wide, v_wide, mixed, row_stats, grad_t, rows, weight):
    heads, _, slot_rows = q_x.shape
    width, all_cols = weight.shape
    vmem = pl.BlockSpec(memory_space=pltpu.VMEM)
    return pl.pallas_call(
        backward_kernel,
        in_specs=[vmem] * 9,
        out_specs=[vmem] * 3,
        out_shape=[
            jax.ShapeDtypeStruct((slot_rows, width), low),
            jax.ShapeDtypeStruct((width, all_cols), low),
            jax.ShapeDtypeStruct((all_cols, WIDE), full),
        ],
        scratch_shapes=[
            pltpu.VMEM((heads, WIDE, slot_rows), low),
            pltpu.VMEM((heads, WIDE, slot_rows), low),
            pltpu.VMEM((all_cols, slot_rows), low),
            pltpu.VMEM((HEAD, slot_rows), full),
            pltpu.VMEM((HEAD, slot_rows), full),
        ],
        compiler_params=pltpu.CompilerParams(vmem_limit_bytes=VMEM_BYTES),
        name="attention_backward",
    )(q_x, k_t, k_wide, v_wide, mixed, row_stats, grad_t, rows, weight)


def normalize(values, gain_vec, shift_vec):
    centre = values - jnp.mean(values, axis=-1, keepdims=True)
    factor = lax.rsqrt(jnp.mean(centre * centre, axis=-1, keepdims=True) + norm_epsilon)
    return centre * factor * gain_vec + shift_vec


def column_sums(values):
    return jnp.sum(values, axis=0, dtype=full)


def per_device(
    tokens, read_memory, write_memory, lengths, qkv_weight, qv_bias, out_weight, out_bias, norm1_gain,
    norm1_bias, up_weight, up_bias, down_weight, down_bias, norm2_gain, norm2_bias, cotangent,
):
    seq_count = lax.axis_size("seq")
    fsdp_count = lax.axis_size("fsdp")
    seq_place = lax.axis_index("seq")
    local_rows, width = tokens.shape
    head_cols = width // seq_count
    shard = width // fsdp_count
    length = lengths[0]
    places = seq_place * local_rows + jnp.arange(local_rows, dtype=jnp.int32)
    in_slot = (places < length)[:, None]
    memory_slots = jnp.arange(MEM, dtype=jnp.int32)
    pick_read = places[:, None] == memory_slots[None, :]
    pick_write = places[:, None] == length - MEM + memory_slots[None, :]
    is_memory = jnp.any(pick_read | pick_write, axis=1)[:, None]
    picks = jnp.concatenate([pick_read, pick_write], axis=1).astype(full)
    memory = jnp.concatenate([read_memory[0], write_memory[0]], axis=0)
    layer_in = jnp.where(is_memory, mul(picks.astype(low), memory).astype(low), tokens)

    rows = lax.all_gather(layer_in, "seq", axis=0, tiled=True)
    own_shard = lax.dynamic_slice_in_dim(
        qkv_weight.reshape(shard, 3, seq_count, head_cols), seq_place, 1, 2
    ).reshape(shard, 3 * head_cols)
    weight = lax.all_gather(own_shard, "fsdp", axis=0, tiled=True)
    vectors = (qv_bias, out_bias, norm1_gain, norm1_bias, up_bias, down_bias, norm2_gain, norm2_bias)
    packed = lax.all_gather(jnp.concatenate(vectors).reshape(1, -1), "fsdp", axis=0, tiled=True).astype(full)
    whole, start = [], 0
    for vector in vectors:
        whole.append(packed[:, start : start + vector.shape[0]].reshape(-1))
        start += vector.shape[0]
    qv_vec, out_vec, gain_one, shift_one, up_vec, down_vec, gain_two, shift_two = whole
    own_qv = lax.dynamic_slice_in_dim(qv_vec.reshape(2, seq_count, head_cols), seq_place, 1, 1)
    bias = jnp.concatenate(
        [own_qv[0, 0], jnp.zeros((head_cols,), full), own_qv[1, 0], jnp.zeros((-3 * head_cols % WIDE,), full)]
    )
    bias = jnp.broadcast_to(bias, (8, bias.shape[0]))
    out_full = lax.all_gather(out_weight, "fsdp", axis=0, tiled=True)
    up_full = lax.all_gather(up_weight, "fsdp", axis=0, tiled=True)
    down_full = lax.all_gather(down_weight, "fsdp", axis=0, tiled=True)

    q_x, k_t, k_wide, v_wide, mixed, mixed_low, row_stats = attention_forward(lengths, rows, weight, bias)
    attended = lax.all_to_all(mixed_low, "seq", split_axis=1, concat_axis=0, tiled=True)
    resid_one = layer_in.astype(full) + mul(attended, out_full, TN) + out_vec
    middle, norm_one_back = jax.vjp(normalize, resid_one, gain_one, shift_one)
    middle_low = middle.astype(low)
    up_pre = mul(middle_low, up_full) + up_vec
    gelu_out, gelu_back = jax.vjp(partial(jax.nn.gelu, approximate=False), up_pre)
    hidden = gelu_out.astype(low)
    down_pre = mul(hidden, down_full) + down_vec
    final, norm_two_back = jax.vjp(normalize, middle + down_pre, gain_two, shift_two)
    output = jnp.where(in_slot, final, 0.0).astype(low)
    grad_final = jnp.where(in_slot, cotangent.astype(full), 0.0)
    grad_resid_two, grad_gain_two, grad_shift_two = norm_two_back(grad_final)
    grad_down = grad_resid_two.astype(low)
    grad_down_weight = mul(hidden, grad_down, TN)
    (grad_up_pre,) = gelu_back(mul(grad_down, down_full, NT))
    grad_up = grad_up_pre.astype(low)
    grad_up_weight = mul(middle_low, grad_up, TN)
    grad_middle = grad_resid_two + mul(grad_up, up_full, NT)
    grad_resid_one, grad_gain_one, grad_shift_one = norm_one_back(grad_middle)
    grad_branch = grad_resid_one.astype(low)
    grad_out_weight = mul(attended, grad_branch)
    grad_attended = mul(out_full, grad_branch, NT).astype(low)
    grad_t = lax.all_to_all(grad_attended, "seq", split_axis=0, concat_axis=1, tiled=True)
    partial_in, weight_part, sums = attention_backward(
        q_x, k_t, k_wide, v_wide, mixed, row_stats, grad_t, rows, weight
    )
    from_heads = lax.psum_scatter(partial_in, "seq", scatter_dimension=0, tiled=True).astype(full)
    grad_layer_in = grad_resid_one + from_heads
    input_grad = jnp.where(is_memory, 0.0, grad_layer_in)
    grad_memory = lax.dot_general(
        picks, grad_layer_in, TN, precision=lax.Precision.HIGHEST, preferred_element_type=full
    )
    grad_memory = lax.psum(grad_memory.astype(low), "seq").astype(full)

    sums = sums[:, 0]
    own_sums = jnp.stack([sums[:head_cols], sums[2 * head_cols :]])[:, None]
    zero_qv = jnp.zeros((2, seq_count, head_cols), full)
    qv_grad = lax.dynamic_update_slice_in_dim(zero_qv, own_sums, seq_place, 1).reshape(-1)
    vector_grads = [
        qv_grad, column_sums(grad_branch), grad_gain_one, grad_shift_one, column_sums(grad_up),
        column_sums(grad_down), grad_gain_two, grad_shift_two,
    ]
    packed_grad = jnp.concatenate([v.reshape(fsdp_count, -1) for v in vector_grads], axis=1)
    packed_sum = lax.psum(packed_grad, ("fsdp", "seq"))
    own_vectors = lax.dynamic_index_in_dim(packed_sum, lax.axis_index("fsdp"), 0, False)
    vector_outs, start = [], 0
    for vector in vectors:
        vector_outs.append(own_vectors[start : start + vector.shape[0]])
        start += vector.shape[0]
    qv_out, out_b_out, gain_one_out, shift_one_out, up_b_out, down_b_out, gain_two_out, shift_two_out = vector_outs

    def both_axes(part):
        piece = lax.psum_scatter(part.astype(low), "fsdp", scatter_dimension=0, tiled=True)
        return lax.psum(piece, "seq").astype(full)

    qkv_piece = lax.psum_scatter(weight_part, "fsdp", scatter_dimension=0, tiled=True)
    qkv_parts = lax.all_gather(qkv_piece, "seq", axis=0).reshape(seq_count, shard, 3, head_cols)
    qkv_out = jnp.transpose(qkv_parts, (1, 2, 0, 3)).reshape(shard, 3 * width).astype(full)
    return (
        output, input_grad, grad_memory[None, :MEM], grad_memory[None, MEM:], qkv_out, qv_out,
        both_axes(grad_out_weight), out_b_out, gain_one_out, shift_one_out,
        both_axes(grad_up_weight), up_b_out, both_axes(grad_down_weight), down_b_out,
        gain_two_out, shift_two_out,
    )


def solution(mesh):
    rows, piece = P(("fsdp", "seq"), None), P("fsdp")
    matrix, memory = P("fsdp", None), P("fsdp", None, None)
    in_specs = (
        rows, memory, memory, piece, matrix, piece, matrix, piece, piece, piece, matrix, piece, matrix,
        piece, piece, piece, rows,
    )
    out_specs = (
        rows, rows, memory, memory, matrix, piece, matrix, piece, piece, piece, matrix, piece, matrix,
        piece, piece, piece,
    )
    return jax.shard_map(per_device, mesh=mesh, in_specs=in_specs, out_specs=out_specs, check_vma=False)
```

time: 1030 us -> 768 us (0.75)
  matrix products: 195 us -> 61.6 us
  waiting for transfers between devices: 546 us -> 432 us
  Pallas kernels: 0 us -> 75.1 us
  other arithmetic: 57.2 us -> 11.8 us
  local copies, waits for them, and re-layouts: 50.3 us -> 20.4 us
  starting transfers between devices: 28.8 us -> 15.5 us
    dot_general x44 -> x11, matrix products: 195 us -> 61.6 us  [the longest x10 59.5 us: mul(): return lax.dot_general(left, right, dims, preferred_element_type=full)]
    reduce_scatter x4 -> x5, waiting for transfers between devices: 405 us -> 292 us  [the longest x3 252 us: both_axes(): lax.psum_scatter(part.astype(low), 'fsdp', scatter_dimension=0, tiled=True)]
    pallas_call x0 -> x2, Pallas kernels: none -> 75.1 us  [the longest x1 47.2 us: attention_backward(): pl.pallas_call(backward_kernel, in_specs=[vmem] * 9, out_specs=[vmem] * 3...]
    unnamed x2 -> x0, blocking collectives: 57.4 us -> none
    all_gather x1 -> x3, blocking collectives: 21 us -> 62.1 us  [the longest x1 31.4 us: per_device(): weight = lax.all_gather(own_shard, 'fsdp', axis=0, tiled=True)]
    psum x1 -> x2, blocking collectives: 13 us -> 51.2 us  [the longest x1 39.9 us: per_device(): packed_sum = lax.psum(packed_grad, ('fsdp', 'seq'))]
    all_to_all x6 -> x1, waiting for transfers between devices: 39.2 us -> 9.99 us  [per_device(): lax.all_to_all(mixed_low, 'seq', split_axis=1, concat_axis=0, tiled=True)]
    convert_element_type x30 -> x4, other arithmetic: 34.3 us -> 5.98 us  [the longest x3 5.97 us: both_axes(): return lax.psum(piece, 'seq').astype(full)]
  transfers between devices with their start and end apart: 15 -> 11, of which waited for: 11 -> 8; matrix products, arithmetic and copies ran while one was open for 25% -> 7% of each run, Pallas kernels for 0% -> 4%
where the time goes in v1:
time: 768 us; the launch traced here: 761 us
  waiting for transfers between devices  432 us (56%)
  blocking collectives  128 us (17%)
  Pallas kernels  75.1 us (10%)
  matrix products  61.6 us (8%)
  local copies, waits for them, and re-layouts  20.4 us (3%)
  between operations  15.9 us (2%)
  starting transfers between devices  15.5 us (2%)
  other arithmetic  11.8 us (2%)
    reduce_scatter x3, waiting for transfers between devices, both_axes(): lax.psum_scatter(part.astype(low), 'fsdp', scatter_dimension=0, tiled=True)  252 us
    all_gather x1, waiting for transfers between devices, per_device(): down_full = lax.all_gather(down_weight, 'fsdp', axis=0, tiled=True)  60.5 us
    dot_general x10, matrix products, mul(): return lax.dot_general(left, right, dims, preferred_element_type=full)  59.5 us
    pallas_call x1, Pallas kernels, attention_backward(): pl.pallas_call(backward_kernel, in_specs=[vmem] * 9, out_specs=[vmem] * 3...  47.2 us
    reduce_scatter x1, waiting for transfers between devices, per_device(): lax.psum_scatter(partial_in, 'seq', scatter_dimension=0, tiled=True)  40.5 us
    all_gather x1, waiting for transfers between devices, per_device(): up_full = lax.all_gather(up_weight, 'fsdp', axis=0, tiled=True)  40.4 us
    psum x1, blocking collectives, per_device(): packed_sum = lax.psum(packed_grad, ('fsdp', 'seq'))  39.9 us
    all_gather x1, blocking collectives, per_device(): weight = lax.all_gather(own_shard, 'fsdp', axis=0, tiled=True)  31.4 us
  transfers between devices with their start and end apart: 11, of which 8 were waited for; matrix products, arithmetic and copies ran while one was open for 7% of the time, Pallas kernels for 4%

profile of v1, /device:TPU:9, one launch (start us, length us, event | category | flops | bytes accessed | tf_op | source)
XLA Modules:
  0.0 760.7 jit_solution(3322971212278135689)
XLA Ops:
  8.2 2.5 fusion.8
  12.9 22.1 %all-gather.2 = bf16[8,1,1152]{2,1,0:T(2,128)(2,1)S(1)} all-gather(bf16[1,1,1152]{2,1,0:T(2,128)(2,1)S(1)} %reshape.187), channel_id=2, replica_groups=mesh['fsdp'=8,'seq'=4] {'fsdp'}, dimensions={0}, use_global_device_ids=true | all-gather | bytes 20736 | tf_op jit(solution)/shard_map/all_gather | solution.py:262
  36.5 31.4 %all_gather.25.weight_ref = bf16[768,576]{1,0:T(8,128)(2,1)} all-gather(bf16[96,576]{1,0:T(8,128)(2,1)S(1)} %copy.68), channel_id=1, replica_groups=mesh['fsdp'=8,'seq'=4] {'fsdp'}, dimensions={0}, use_global_device_ids=true | all-gather | bytes 995328 | tf_op jit(solution)/shard_map/all_gather | solution.py:260
  68.5 27.9 %attention_forward.1 = (bf16[3,128,2048]{2,1,0:T(8,128)(2,1)}, bf16[192,2048]{1,0:T(8,128)(2,1)}, bf16[3,2048,128]{2,1,0:T(8,128)(2,1)}, bf16[3,2048,128]{2,1,0:...) custom-call(s32[1]{0:T(128)} %copy.89.length_ref, ...), custom_call_target="tpu_custom_call" | custom-call | tf_op jit(solution)/shard_map/attention_forward/pallas_call | solution.py:110
  96.3 2.1 copy.83
  98.4 14.9 %all-to-all-start = ((bf16[192,4,512]{2,0,1:T(8,128)(2,1)}), bf16[192,4,512]{2,0,1:T(8,128)(2,1)S(1)}, u32[]{:S(2)}, u32[]{:S(2)}) async-start(bf16[192,4,512]{2,0,1:T(8,128)(2,1)} %bitcast.60), calls=%async_computation | async-start | bytes 1572864 | tf_op jit(solution)/shard_map/all_to_all | solution.py:278
  114.1 10.0 %all-to-all-done = bf16[192,4,512]{2,0,1:T(8,128)(2,1)S(1)} async-done(((bf16[192,4,512]{2,0,1:T(8,128)(2,1)}), bf16[192,4,512]{2,0,1:T(8,128)(2,1)S(1)}, u32[]{:S(2)}, u32[]{:S(2)}) %all-to-all-start) | async-done | bytes 786464 | tf_op jit(solution)/shard_map/all_to_all | solution.py:278
  125.0 2.4 fusion.28
  127.8 40.4 %all-gather.12.cloned.1.call-done = bf16[768,3072]{1,0:T(8,128)(2,1)} async-done(((bf16[96,3072]{1,0:T(8,128)(2,1)}), bf16[768,3072]{1,0:T(8,128)(2,1)}) %all-gather.12.cloned.1.call-update) | async-done | bytes 4718608 | tf_op jit(solution)/shard_map/all_gather | solution.py:274
  168.2 19.6 %multiply_convert_fusion = (bf16[512,3072]{1,0:T(8,128)(2,1)}, f32[512,3072]{1,0:T(8,128)}, f32[512,3072]{1,0:T(8,128)}) fusion(f32[3072]{0:T(1024)S(1)} %add.149, bf16[768,3072]{1,0:T(8,128)(2,1)} %all-gather.12.cloned.1.call-done, f32[512,768]{1,0:T(8,128)S(1)} %get-tuple-element.160, f32[768]{0:T(1024)S(1)} %add.146, f32[768]{0:T(1024)S(1)} %mul.147, ...), kind=kOutput, calls=%fused_computation.4 | convolution fusion | flops 2521694208 | bytes 22042624 | tf_op jit(solution)/shard_map/dot_general | solution.py:27
  187.8 60.5 %all-gather.14.cloned.1.call-done = bf16[3072,768]{1,0:T(8,128)(2,1)} async-done(((bf16[384,768]{1,0:T(8,128)(2,1)}), bf16[3072,768]{1,0:T(8,128)(2,1)}) %all-gather.14.cloned.1.call-update) | async-done | bytes 4718608 | tf_op jit(solution)/shard_map/all_gather | solution.py:275
  248.3 6.1 fusion.29
  258.2 8.5 %convert_reduce_fusion = (f32[3072]{0:T(1024)S(1)}, bf16[512,3072]{1,0:T(8,128)(2,1)S(1)}) fusion(f32[512,3072]{1,0:T(8,128)} %get-tuple-element.138, f32[512,3072]{1,0:T(8,128)} %get-tuple-element.161, f32[3072]{0:T(1024)S(1)} %add.149, bf16[512,768]{1,0:T(8,128)(2,1)S(1)} %get-tuple-element.128, bf16[3072,768]{1,0:T(8,128)(2,1)S(1)} %copy-done.22), kind=kOutput, calls=%fused_computation.2 | convolution fusion | flops 2442654720 | bytes 21258240 | tf_op jit(solution)/shard_map/dot_general | solution.py:27
  266.7 3.2 multiply_reduce_fusion.1
  274.0 14.9 %all_to_all.38 = bf16[4,192,512]{2,1,0:T(8,128)(2,1)S(1)} all-to-all(bf16[4,192,512]{2,1,0:T(8,128)(2,1)S(1)} %bitcast.66), channel_id=1, replica_groups=mesh['fsdp'=8,'seq'=4] {'seq'}, dimensions={0} | all-to-all | bytes 1572864 | tf_op jit(solution)/shard_map/all_to_all | solution.py:300
  290.0 47.2 %attention_backward.1 = (bf16[2048,768]{1,0:T(8,128)(2,1)}, bf16[768,576]{1,0:T(8,128)(2,1)}, f32[576,128]{1,0:T(8,128)}) custom-call(bf16[3,128,2048]{2,1,0:T(8,128)(2,1)} %get-tuple-element.27.q_in, bf16[192,2048]{1,0:T(8,128)(2,1)} %get-tuple-element.28.k_t, bf16[3,2048,128]{2,1,0:T(8,128)(2,1)} %get-tuple-element.29.k_wide, ...), custom_call_target="tpu_custom_call" | custom-call | tf_op jit(solution)/shard_map/attention_backward/pallas_call | solution.py:204
  337.2 3.0 convolution_convert_fusion.2
  340.3 6.7 convolution_convert_fusion.1
  348.2 6.7 convolution_convert_fusion
  356.5 39.9 %psum.36 = f32[8,1152]{1,0:T(8,128)S(1)} all-reduce(f32[8,1152]{1,0:T(8,128)S(1)} %concatenate.19), channel_id=1, replica_groups=mesh['fsdp'=8,'seq'=4] {'fsdp','seq'}, use_global_device_ids=true, to_apply=%region_19.20 | all-reduce | flops 9216 | bytes 73728 | tf_op jit(solution)/shard_map/psum | solution.py:321
  398.3 8.6 %all-gather.1 = bf16[384,576]{1,0:T(8,128)(2,1)S(1)} all-gather(bf16[96,576]{1,0:T(8,128)(2,1)} %reduce-scatter.8.cloned.1.call-done), channel_id=3, replica_groups=mesh['fsdp'=8,'seq'=4] {'seq'}, dimensions={0}, use_global_device_ids=true | all-gather | bytes 552960 | tf_op jit(solution)/shard_map/all_gather | solution.py:334
  407.8 1.8 copy.73
  409.6 3.0 reshape.180
  412.6 52.0 %reduce-scatter.10.cloned.1.call-done = bf16[96,768]{1,0:T(8,128)(2,1)} async-done(((bf16[768,768]{1,0:T(8,128)(2,1)}), bf16[96,768]{1,0:T(8,128)(2,1)}) %reduce-scatter.10.cloned.1.call-update) | async-done | bytes 147472 | tf_op jit(solution)/shard_map/reduce_scatter | solution.py:330
  464.6 100.6 %reduce-scatter.12.cloned.1.call-done = bf16[96,3072]{1,0:T(8,128)(2,1)} async-done(((bf16[768,3072]{1,0:T(8,128)(2,1)}), bf16[96,3072]{1,0:T(8,128)(2,1)}) %reduce-scatter.12.cloned.1.call-update) | async-done | bytes 589840 | tf_op jit(solution)/shard_map/reduce_scatter | solution.py:330
  565.1 99.3 %reduce-scatter.14.cloned.1.call-done = bf16[384,768]{1,0:T(8,128)(2,1)} async-done(((bf16[3072,768]{1,0:T(8,128)(2,1)}), bf16[384,768]{1,0:T(8,128)(2,1)}) %reduce-scatter.14.cloned.1.call-update) | async-done | bytes 589840 | tf_op jit(solution)/shard_map/reduce_scatter | solution.py:330
  664.4 40.5 %reduce-scatter.6.cloned.1.call-done = bf16[512,768]{1,0:T(8,128)(2,1)} async-done(((bf16[2048,768]{1,0:T(8,128)(2,1)}), bf16[512,768]{1,0:T(8,128)(2,1)}) %reduce-scatter.6.cloned.1.call-update) | async-done | bytes 786448 | tf_op jit(solution)/shard_map/reduce_scatter | solution.py:304
  704.9 2.0 convolution_convert_fusion.5
  706.9 11.3 %psum.35 = bf16[20,768]{1,0:T(8,128)(2,1)S(1)} all-reduce(bf16[20,768]{1,0:T(8,128)(2,1)S(1)} %convolution_convert_fusion.5), channel_id=1, replica_groups=mesh['fsdp'=8,'seq'=4] {'seq'}, use_global_device_ids=true, to_apply=%region_10.11 | all-reduce | flops 15360 | bytes 61440 | tf_op jit(solution)/shard_map/psum | solution.py:310
  720.9 26.5 %all-reduce.3.cloned.1.call-done = (bf16[96,768]{1,0:T(8,128)(2,1)}, bf16[96,3072]{1,0:T(8,128)(2,1)}, bf16[384,768]{1,0:T(8,128)(2,1)}) async-done(((bf16[96,768]{1,0:T(8,128)(2,1)}, bf16[96,3072]{1,0:T(8,128)(2,1)}, bf16[384,768]{1,0:T(8,128)(2,1)}), (bf16[96,768]{1,0:T(8,128)(2,1)}, bf16[96,3072]{1,0:T(8,128)(2,1)}, bf16[384,768]{1,0:T(8,128)(2,1)})) %all-reduce.3.cloned.1.call-update) | async-done | bytes 1327120 | tf_op jit(solution)/shard_map/psum | solution.py:331
  749.1 2.2 convert_element_type.117
  751.3 2.2 convert_element_type.119
  (148 shorter events, 25.0 us)
Async XLA Ops:
  7.2 5.5 copy-start.15
  7.2 5.5 copy-start.16
  7.2 5.5 copy-start.17
  7.2 5.5 copy-start.18
  7.2 5.5 copy-start.14
  7.2 5.5 copy-start.19
  7.2 5.5 copy-start.20
  7.3 5.5 copy-start.21
  7.3 27.8 %copy-start.12 = (bf16[96,2304]{1,0:T(8,128)(2,1)S(1)}, bf16[96,2304]{1,0:T(8,128)(2,1)}, u32[]{:S(2)}) copy-start(bf16[96,2304]{1,0:T(8,128)(2,1)} %param.21) | copy-start | bytes 1327108
  7.3 60.6 %all-gather.8.cloned.1.call-start = ((), (), s32[]{:S(2)}) async-start(), calls=%async_computation.7 | async-start | bytes 3932160 | tf_op jit(solution)/shard_map/all_gather | solution.py:256
  10.7 103.5 %all-gather.10.cloned.1.call-start = ((), (), s32[]{:S(2)}) async-start(), calls=%async_computation.8 | async-start | bytes 1327104 | tf_op jit(solution)/shard_map/all_gather | solution.py:273
  11.4 156.8 %all-gather.12.cloned.1.call-start = ((), (), s32[]{:S(2)}) async-start(), calls=%async_computation.9 | async-start | bytes 5308416 | tf_op jit(solution)/shard_map/all_gather | solution.py:274
  12.1 236.2 %all-gather.14.cloned.1.call-start = ((), (), s32[]{:S(2)}) async-start(), calls=%async_computation.10 | async-start | bytes 5308416 | tf_op jit(solution)/shard_map/all_gather | solution.py:275
  68.5 56.6 %copy-start.5 = (bf16[512,768]{1,0:T(8,128)(2,1)S(1)}, bf16[512,768]{1,0:T(8,128)(2,1)}, u32[]{:S(2)}) copy-start(bf16[512,768]{1,0:T(8,128)(2,1)} %fusion.8) | copy-start | bytes 2359300
  98.4 25.7 %all-to-all-start = ((bf16[192,4,512]{2,0,1:T(8,128)(2,1)}), bf16[192,4,512]{2,0,1:T(8,128)(2,1)S(1)}, u32[]{:S(2)}, u32[]{:S(2)}) async-start(bf16[192,4,512]{2,0,1:T(8,128)(2,1)} %bitcast.60), calls=%async_computation | async-start | bytes 1572864 | tf_op jit(solution)/shard_map/all_to_all | solution.py:278
  113.3 284.9 %reduce-scatter.8.cloned.1.call-start = ((), (), s32[]{:S(2)}) async-start(), calls=%async_computation.12 | async-start | bytes 1105920 | tf_op jit(solution)/shard_map/reduce_scatter | solution.py:333
  127.5 142.5 %copy-start.2 = (f32[512,768]{1,0:T(8,128)}, f32[512,768]{1,0:T(8,128)S(1)}, u32[]{:S(2)}) copy-start(f32[512,768]{1,0:T(8,128)S(1)} %get-tuple-element.160) | copy-start | bytes 4718596
  248.3 6.4 copy-start.4
  257.3 9.4 %slice-start = ((s8[4718592]{0:T(1024)(128)(4,1)}), s8[4194304]{0:T(1024)(128)(4,1)S(1)}, s32[]{:S(2)}) async-start(s8[4718592]{0:T(1024)(128)(4,1)} %bitcast.82), calls=%async_computation.17 | async-start | bytes 8388608
  257.5 9.2 %copy-start.9 = (bf16[512,768]{1,0:T(8,128)(2,1)}, bf16[512,768]{1,0:T(8,128)(2,1)S(1)}, u32[]{:S(2)}) copy-start(bf16[512,768]{1,0:T(8,128)(2,1)S(1)} %get-tuple-element.128) | copy-start | bytes 2359300
  258.2 8.5 %slice-start.1 = ((s8[4718592]{0:T(1024)(128)(4,1)}), s8[524288]{0:T(1024)(128)(4,1)S(1)}, s32[]{:S(2)}) async-start(s8[4718592]{0:T(1024)(128)(4,1)} %bitcast.82), calls=%async_computation.18 | async-start | bytes 1048576
  266.7 3.2 copy-start.24
  269.9 3.0 copy-start.23
  290.0 47.3 %copy-start.8 = (bf16[192,4,512]{2,0,1:T(8,128)(2,1)S(1)}, bf16[192,4,512]{2,0,1:T(8,128)(2,1)}, u32[]{:S(2)}) copy-start(bf16[192,4,512]{2,0,1:T(8,128)(2,1)} %copy-done.7) | copy-start | bytes 2359300
  337.2 3.2 copy-start.3
  337.2 127.4 %reduce-scatter.10.cloned.1.call-start = ((), (), s32[]{:S(2)}) async-start(), calls=%async_computation.13 | async-start | bytes 1327104 | tf_op jit(solution)/shard_map/reduce_scatter | solution.py:330
  340.3 224.8 %reduce-scatter.12.cloned.1.call-start = ((), (), s32[]{:S(2)}) async-start(), calls=%async_computation.14 | async-start | bytes 5308416 | tf_op jit(solution)/shard_map/reduce_scatter | solution.py:330
  347.1 317.3 %reduce-scatter.14.cloned.1.call-start = ((), (), s32[]{:S(2)}) async-start(), calls=%async_computation.15 | async-start | bytes 5308416 | tf_op jit(solution)/shard_map/reduce_scatter | solution.py:330
  354.9 349.9 %reduce-scatter.6.cloned.1.call-start = ((), (), s32[]{:S(2)}) async-start(), calls=%async_computation.11 | async-start | bytes 3932160 | tf_op jit(solution)/shard_map/reduce_scatter | solution.py:304
  355.7 391.8 %all-reduce.3.cloned.1.call-start = ((), (), s32[]{:S(2)}) async-start(), calls=%async_computation.16 | async-start | bytes 2654208 | tf_op jit(solution)/shard_map/psum | solution.py:331
  407.8 297.1 %copy-start.1 = (f32[512,768]{1,0:T(8,128)S(1)}, f32[512,768]{1,0:T(8,128)}, u32[]{:S(2)}) copy-start(f32[512,768]{1,0:T(8,128)} %copy-done) | copy-start | bytes 4718596
  704.9 14.6 %copy-start.6 = (bf16[512,768]{1,0:T(8,128)(2,1)S(1)}, bf16[512,768]{1,0:T(8,128)(2,1)}, u32[]{:S(2)}) copy-start(bf16[512,768]{1,0:T(8,128)(2,1)} %reduce-scatter.6.cloned.1.call-done) | copy-start | bytes 2359300
  (6 other events, 8.1 us)
Sparse Core Ops, SparseCore 0:
  10.8 30.0 all-gather.7
  43.1 45.7 all-gather.9
  91.0 77.1 all-gather.11
  170.2 78.0 all-gather.13
  337.3 59.8 reduce-scatter.7
  401.4 63.0 reduce-scatter.9
  468.6 96.4 reduce-scatter.11
  569.2 95.1 reduce-scatter.13
  667.1 37.7 reduce-scatter.5
  707.3 40.0 all-reduce.2

commit v2 on v1

--- a/solution.py
+++ b/solution.py
@@ -42,34 +42,37 @@
     return block.astype(low)
 
 
+def project_block(start, length, rows_ref, weight_ref, bias_q, bias_v, q_x, k_t, v_x, k_wide, v_wide, step):
+    head_cols = k_t.shape[0]
+    lanes = pl.ds(start, step)
+    made = mul(weight_ref[...], rows_ref[lanes, :], TT)
+    query = (made[:head_cols] + bias_q).astype(low) * jnp.asarray(HEAD**-0.5, low)
+    k_t[:, lanes] = made[head_cols : 2 * head_cols].astype(low)
+    value = (made[2 * head_cols :] + bias_v).astype(low)
+    place = start + lax.broadcasted_iota(jnp.int32, (1, step), 1)
+    key_bias = jnp.where(place < length, 0.0, masked_score)
+    one = jnp.ones((1, step), full)
+    query_extra = stack_rows([one], step)
+    key_extra = stack_rows([key_bias, one, one, one], step)
+    value_extra = stack_rows([one, one, one], step)
+    for h in range(head_cols // HEAD):
+        own = slice(h * HEAD, (h + 1) * HEAD)
+        q_x[h, :HEAD, lanes] = query[own]
+        q_x[h, HEAD:, lanes] = query_extra
+        v_x[h, :HEAD, lanes] = value[own]
+        v_x[h, HEAD:, lanes] = value_extra
+        k_wide[h, lanes, :] = jnp.transpose(jnp.concatenate([k_t[own, lanes], key_extra], axis=0))
+        v_wide[h, lanes, :] = jnp.transpose(v_x[h, :, lanes])
+
+
 def project_heads(length, rows_ref, weight_ref, bias_ref, q_x, k_t, v_x, k_wide, v_wide):
-    slot_rows = rows_ref.shape[0]
     head_cols = k_t.shape[0]
-    heads = head_cols // HEAD
     bias = jnp.transpose(bias_ref[...])[:, 0:1]
-    step = 512
-    for start in range(0, slot_rows, step):
-        lanes = slice(start, start + step)
-        made = mul(weight_ref[...], rows_ref[lanes, :], TT) + bias[: 3 * head_cols]
-        query = made[:head_cols].astype(low) * jnp.asarray(HEAD**-0.5, low)
-        k_t[:, lanes] = made[head_cols : 2 * head_cols].astype(low)
-        value = made[2 * head_cols :].astype(low)
-        place = start + lax.broadcasted_iota(jnp.int32, (1, step), 1)
-        key_bias = jnp.where(place < length, 0.0, masked_score)
-        one = jnp.ones((1, step), full)
-        query_extra = stack_rows([one], step)
-        key_extra = stack_rows([key_bias, one, one, one], step)
-        value_extra = stack_rows([one, one, one], step)
-        for h in range(heads):
-            own = slice(h * HEAD, (h + 1) * HEAD)
-            q_x[h, :HEAD, lanes] = query[own]
-            q_x[h, HEAD:, lanes] = query_extra
-            v_x[h, :HEAD, lanes] = value[own]
-            v_x[h, HEAD:, lanes] = value_extra
-            k_wide[h, lanes, :] = jnp.transpose(
-                jnp.concatenate([k_t[own, lanes], key_extra], axis=0)
-            )
-            v_wide[h, lanes, :] = jnp.transpose(v_x[h, :, lanes])
+    for start in range(0, rows_ref.shape[0], 512):
+        project_block(
+            start, length, rows_ref, weight_ref, bias[:head_cols], bias[2 * head_cols : 3 * head_cols],
+            q_x, k_t, v_x, k_wide, v_wide, 512,
+        )
 
 
 def attend_block(h, lanes, q_x, k_wide, v_x, mixed, mixed_low, row_stats):
@@ -222,6 +225,476 @@
     )(q_x, k_t, k_wide, v_wide, mixed, row_stats, grad_t, rows, weight)
 
 
+MESH = pl.DeviceIdType.MESH
+OWN, RELATIONS = 0, 7
+UP_W, OUT_W, DOWN_W, QKV_W = 0, 1, 2, 3
+
+
+def offset_of(relation):
+    return (0, -1, -2, -3, 1, 2, 3)[relation]
+
+
+class Place:
+    def __init__(self):
+        self.f, self.s = lax.axis_index("fsdp"), lax.axis_index("seq")
+        self.z, self.x = self.f // 2, lax.rem(self.f, 2)
+        self.y, self.c = self.s // 2, lax.rem(self.s, 2)
+        self.core = (self.f, 2 * self.y + 1 - self.c)
+        self.across_y = (self.f, 2 * (1 - self.y) + self.c)
+        self.diagonal = (self.f, 2 * (1 - self.y) + 1 - self.c)
+        self.across_x = (2 * self.z + 1 - self.x, self.s)
+        self.above = (self.f + 2, self.s)
+        self.below = (self.f - 2, self.s)
+
+    def has(self, relation):
+        offset = offset_of(relation)
+        return (self.z + offset >= 0) & (self.z + offset <= 3)
+
+    def source(self, relation, column):
+        own_column = self.f + 2 * offset_of(relation)
+        return own_column if column == 0 else own_column + 1 - 2 * self.x
+
+    def member(self, turn):
+        flip_y = 1 - turn // 2
+        flip_c = lax.rem(turn, 2) if not isinstance(turn, int) else turn % 2
+        flip_c = flip_c + (1 - 2 * flip_c) * (turn // 2)
+        return 2 * lax.rem(self.y + flip_y, 2) + lax.rem(self.c + flip_c, 2)
+
+
+def remote(src, dst, send, recv, where):
+    return pltpu.make_async_remote_copy(
+        src_ref=src, dst_ref=dst, send_sem=send, recv_sem=recv, device_id=where, device_id_type=MESH
+    )
+
+
+def greet(place, everyone):
+    barrier = pltpu.get_barrier_semaphore()
+    near = [place.core, place.across_y, place.diagonal, place.across_x]
+    for where in near:
+        pl.semaphore_signal(barrier, inc=1, device_id=where, device_id_type=MESH)
+
+    @pl.when(place.z > 0)
+    def _():
+        pl.semaphore_signal(barrier, inc=1, device_id=place.below, device_id_type=MESH)
+
+    @pl.when(place.z < 3)
+    def _():
+        pl.semaphore_signal(barrier, inc=1, device_id=place.above, device_id_type=MESH)
+
+    ends = jnp.where((place.z == 0) | (place.z == 3), 1, 2)
+    pl.semaphore_wait(barrier, len(near) + ends)
+
+
+class Gather:
+    def __init__(self, place, own, whole, sems):
+        self.place, self.own, self.whole = place, own, whole
+        (self.z_send, self.z_recv, self.x_send, self.x_recv, self.c_send, self.c_recv,
+         self.y_send, self.y_recv, self.d_send, self.d_recv) = sems
+
+    def piece(self, array, source, quarter=None):
+        c = self.place.c
+        ref = self.whole[array]
+        if array == QKV_W:
+            return ref.at[source]
+        if array == DOWN_W:
+            rows = ref.shape[0] // 8
+            part = rows // 4
+            quarter = self.place.s if quarter is None else quarter
+            return ref.at[pl.ds(pl.multiple_of(source * rows + quarter * part, part), part)]
+        rows, columns = ref.shape[0] // 8, ref.shape[1] // 2
+        return ref.at[
+            pl.ds(pl.multiple_of(source * rows, rows), rows),
+            pl.ds(pl.multiple_of(c * columns, columns), columns),
+        ]
+
+    def own_piece(self, array):
+        ref = self.own[array]
+        if array == QKV_W:
+            return ref
+        if array == DOWN_W:
+            part = ref.shape[0] // 4
+            return ref.at[pl.ds(pl.multiple_of(self.place.s * part, part), part)]
+        columns = ref.shape[1] // 2
+        return ref.at[:, pl.ds(pl.multiple_of(self.place.c * columns, columns), columns)]
+
+    def along_z(self, array, relation, way):
+        here = self.piece(array, self.place.source(relation, 0))
+        src = self.own_piece(array) if relation == OWN else here
+        step = abs(offset_of(relation))
+        where = self.place.above if way == 0 else self.place.below
+        return remote(src, here, self.z_send.at[array, way, step], self.z_recv.at[array, way, step], where)
+
+    def z_ways(self, relation):
+        place = self.place
+        ways = []
+        if offset_of(relation) <= 0:
+            ways.append((0, place.has(relation) & (place.z < 3)))
+        if offset_of(relation) >= 0:
+            ways.append((1, place.has(relation) & (place.z > 0)))
+        return ways
+
+    def wait_z(self, array, relation):
+        way = 0 if offset_of(relation) < 0 else 1
+        step = abs(offset_of(relation)) - 1
+        here = self.piece(array, self.place.source(relation, 0))
+        where = self.place.below if way == 0 else self.place.above
+        remote(
+            here, here, self.z_send.at[array, way, step], self.z_recv.at[array, way, step], where
+        ).wait_recv()
+
+    def over_x(self, array, relation):
+        here = self.piece(array, self.place.source(relation, 0))
+        src = self.own_piece(array) if relation == OWN else here
+        return remote(
+            src, here, self.x_send.at[array, relation], self.x_recv.at[array, relation], self.place.across_x
+        )
+
+    def from_x(self, array, relation):
+        here = self.piece(array, self.place.source(relation, 1))
+        return remote(
+            here, here, self.x_send.at[array, relation], self.x_recv.at[array, relation], self.place.across_x
+        )
+
+    def to_core(self, array, relation, column):
+        here = self.piece(array, self.place.source(relation, column))
+        return remote(
+            here, here, self.c_send.at[array, relation, column], self.c_recv.at[array, relation, column],
+            self.place.core,
+        )
+
+    def over_y(self, relation, column):
+        here = self.piece(DOWN_W, self.place.source(relation, column))
+        return remote(
+            here, here, self.y_send.at[relation, column], self.y_recv.at[relation, column], self.place.across_y
+        )
+
+    def far_quarter(self, relation, column):
+        return self.piece(
+            DOWN_W, self.place.source(relation, column), 2 * (1 - self.place.y) + self.place.c
+        )
+
+    def from_y(self, relation, column):
+        here = self.far_quarter(relation, column)
+        return remote(
+            here, here, self.y_send.at[relation, column], self.y_recv.at[relation, column], self.place.across_y
+        )
+
+    def far_to_core(self, relation, column):
+        here = self.far_quarter(relation, column)
+        return remote(
+            here, here, self.d_send.at[relation, column], self.d_recv.at[relation, column], self.place.core
+        )
+
+    def when(self, relation, action):
+        if relation == OWN:
+            action()
+        else:
+            pl.when(self.place.has(relation))(action)
+
+    def arrive_z(self, array, relation):
+        def action():
+            if relation != OWN:
+                self.wait_z(array, relation)
+            for way, holds in self.z_ways(relation):
+                pl.when(holds)(lambda way=way: self.along_z(array, relation, way).start())
+            self.over_x(array, relation).start()
+            if array != QKV_W and relation != OWN:
+                self.to_core(array, relation, 0).start()
+                if array == DOWN_W:
+                    self.over_y(relation, 0).start()
+
+        self.when(relation, action)
+
+    def arrive_x(self, array, relation):
+        def action():
+            self.from_x(array, relation).wait_recv()
+            if array != QKV_W:
+                self.to_core(array, relation, 1).start()
+                if array == DOWN_W:
+                    self.over_y(relation, 1).start()
+
+        self.when(relation, action)
+
+    def arrive_y(self, relation, column):
+        def action():
+            self.from_y(relation, column).wait_recv()
+            self.far_to_core(relation, column).start()
+
+        if (relation, column) != (OWN, 0):
+            self.when(relation, action)
+
+    def finish(self, array):
+        for relation in range(RELATIONS):
+            def action():
+                self.over_x(array, relation).wait_send()
+                for way, holds in self.z_ways(relation):
+                    pl.when(holds)(lambda way=way: self.along_z(array, relation, way).wait_send())
+                if array == QKV_W:
+                    return
+                for column in range(2):
+                    if (relation, column) == (OWN, 0):
+                        continue
+                    self.to_core(array, relation, column).wait()
+                    if array == DOWN_W:
+                        self.over_y(relation, column).wait_send()
+                        self.far_to_core(relation, column).wait()
+
+            self.when(relation, action)
+
+
+def front_kernel(
+    length_ref, rows_in, qkv_in, up_in, down_in, out_in,
+    rows_ref, weight_ref, pieces, q_x, k_t, k_wide, v_wide, mixed, row_stats, up_full, down_full, out_full,
+    attended,
+    v_x, mixed_low, row_send, row_recv, far_send, far_recv, mix_send, mix_recv, local_sem, *gather_sems,
+):
+    place = Place()
+    slot_rows, width = rows_ref.shape
+    local_rows = rows_in.shape[0]
+    head_cols = k_t.shape[0]
+    heads = head_cols // HEAD
+    own_shards = {UP_W: up_in, DOWN_W: down_in, OUT_W: out_in, QKV_W: qkv_in}
+    whole = {UP_W: up_full, DOWN_W: down_full, OUT_W: out_full, QKV_W: pieces}
+    gather = Gather(place, own_shards, whole, gather_sems)
+    greet(place, None)
+
+    halves = 2
+    part = local_rows // halves
+
+    def rows_of(member, half):
+        return pl.ds(pl.multiple_of(member * local_rows + half * part, part), part)
+
+    def send_rows(half, index):
+        where = (place.core, place.across_y)[index]
+        return remote(
+            rows_in.at[pl.ds(half * part, part)], rows_ref.at[rows_of(place.s, half)],
+            row_send.at[index, half], row_recv.at[index, half], where,
+        )
+
+    def rows_from(half, index):
+        member = (2 * place.y + 1 - place.c, 2 * (1 - place.y) + place.c)[index]
+        here = rows_ref.at[rows_of(member, half)]
+        where = (place.core, place.across_y)[index]
+        return remote(here, here, row_send.at[index, half], row_recv.at[index, half], where)
+
+    def pass_rows(half, arriving):
+        flip = place.c if not arriving else 1 - place.c
+        here = rows_ref.at[rows_of(2 * (1 - place.y) + flip, half)]
+        return remote(here, here, far_send.at[half], far_recv.at[half], place.core)
+
+    for half in range(halves):
+        send_rows(half, 1).start()
+        send_rows(half, 0).start()
+    gather.arrive_z(QKV_W, OWN)
+
+    def own_copies():
+        copies = []
+        for index, array in enumerate((UP_W, DOWN_W, OUT_W)):
+            rows = own_shards[array].shape[0]
+            copies.append(pltpu.make_async_copy(
+                own_shards[array], whole[array].at[pl.ds(pl.multiple_of(place.f * rows, rows), rows)],
+                local_sem.at[index],
+            ))
+        copies.append(pltpu.make_async_copy(qkv_in, pieces.at[place.f], local_sem.at[3]))
+        copies.append(pltpu.make_async_copy(
+            rows_in, rows_ref.at[pl.ds(pl.multiple_of(place.s * local_rows, local_rows), local_rows)],
+            local_sem.at[4],
+        ))
+        return copies
+
+    for copy in own_copies():
+        copy.start()
+
+    for relation in (1, 4):
+        gather.arrive_z(QKV_W, relation)
+    gather.arrive_z(UP_W, OWN)
+    for relation in (2, 5):
+        gather.arrive_z(QKV_W, relation)
+    gather.arrive_z(OUT_W, OWN)
+    gather.arrive_z(DOWN_W, OWN)
+    rows_from(0, 1).wait_recv()
+    pass_rows(0, False).start()
+    for relation in (3, 6):
+        gather.arrive_z(QKV_W, relation)
+    for relation in (1, 4):
+        gather.arrive_z(UP_W, relation)
+    for relation in range(RELATIONS):
+        gather.arrive_x(QKV_W, relation)
+    for copy in own_copies()[3:]:
+        copy.wait()
+
+    shard = weight_ref.shape[0] // 8
+    for source in range(8):
+        weight_ref[source * shard : (source + 1) * shard, :] = pieces[source, :shard, :]
+    bias_q = jnp.transpose(pieces[place.s, shard : shard + 16, :].astype(full))[:head_cols, 0:1]
+    bias_v = jnp.transpose(pieces[4 + place.s, shard : shard + 16, :].astype(full))[:head_cols, 0:1]
+    length = length_ref[0]
+
+    def project(member):
+        start = pl.multiple_of(member * local_rows, local_rows)
+        project_block(
+            start, length, rows_ref, weight_ref, bias_q, bias_v, q_x, k_t, v_x, k_wide, v_wide, local_rows
+        )
+
+    project(place.s)
+    for half in range(halves):
+        rows_from(half, 0).wait_recv()
+    project(2 * place.y + 1 - place.c)
+    rows_from(1, 1).wait_recv()
+    pass_rows(1, False).start()
+    project(2 * (1 - place.y) + place.c)
+    for relation in (1, 4):
+        gather.arrive_z(OUT_W, relation)
+        gather.arrive_z(DOWN_W, relation)
+    for half in range(halves):
+        pass_rows(half, True).wait_recv()
+    project(2 * (1 - place.y) + 1 - place.c)
+
+    def chores(step):
+        if step == 0:
+            gather.arrive_x(UP_W, OWN)
+            for relation in (2, 5):
+                gather.arrive_z(UP_W, relation)
+        elif step == 2:
+            for relation in (2, 5):
+                gather.arrive_z(OUT_W, relation)
+                gather.arrive_z(DOWN_W, relation)
+            gather.arrive_x(OUT_W, OWN)
+            gather.arrive_x(DOWN_W, OWN)
+        elif step == 4:
+            for relation in (1, 4):
+                gather.arrive_x(UP_W, relation)
+                gather.arrive_y(relation, 0)
+            gather.arrive_y(OWN, 1)
+        elif step == 6:
+            for relation in (3, 6):
+                gather.arrive_z(UP_W, relation)
+            for relation in (1, 4):
+                gather.arrive_x(OUT_W, relation)
+                gather.arrive_x(DOWN_W, relation)
+        elif step == 8:
+            for relation in (3, 6):
+                gather.arrive_z(OUT_W, relation)
+                gather.arrive_z(DOWN_W, relation)
+            for relation in (2, 5):
+                gather.arrive_x(UP_W, relation)
+                gather.arrive_y(relation, 0)
+        elif step == 10:
+            for relation in (2, 5):
+                gather.arrive_x(OUT_W, relation)
+                gather.arrive_x(DOWN_W, relation)
+            for relation in (1, 4):
+                gather.arrive_y(relation, 1)
+
+    def send_mixed(h, turn, arriving=False):
+        member = place.member(turn)
+        own = pl.ds(pl.multiple_of(h * HEAD, HEAD), HEAD)
+        lanes = pl.ds(pl.multiple_of(member * local_rows, local_rows), local_rows)
+        owner = member if arriving else place.s
+        there = attended.at[pl.ds(pl.multiple_of(owner * head_cols + h * HEAD, HEAD), HEAD)]
+        return remote(
+            mixed_low.at[own, lanes], there, mix_send.at[h, turn], mix_recv.at[h, turn], (place.f, member)
+        )
+
+    def keep_mixed(h):
+        own = pl.ds(pl.multiple_of(h * HEAD, HEAD), HEAD)
+        lanes = pl.ds(pl.multiple_of(place.s * local_rows, local_rows), local_rows)
+        there = attended.at[pl.ds(pl.multiple_of(place.s * head_cols + h * HEAD, HEAD), HEAD)]
+        return pltpu.make_async_copy(mixed_low.at[own, lanes], there, mix_send.at[h, 3])
+
+    turns = slot_rows // local_rows
+
+    def pass_on(index):
+        h, turn = index // turns, lax.rem(index, turns)
+
+        @pl.when(turn < turns - 1)
+        def _():
+            send_mixed(h, turn).start()
+
+        @pl.when(turn == turns - 1)
+        def _():
+            keep_mixed(h).start()
+
+    def step(index, carry):
+        for when in range(0, 12, 2):
+            pl.when(index == when)(lambda when=when: chores(when))
+        h, turn = index // turns, lax.rem(index, turns)
+        start = pl.multiple_of(place.member(turn) * local_rows, local_rows)
+        attend_block(h, pl.ds(start, local_rows), q_x, k_wide, v_x, mixed, mixed_low, row_stats)
+
+        @pl.when(index > 0)
+        def _():
+            pass_on(index - 1)
+
+        return carry
+
+    lax.fori_loop(0, heads * turns, step, 0)
+    pass_on(heads * turns - 1)
+    for relation in (3, 6):
+        gather.arrive_x(UP_W, relation)
+        gather.arrive_x(OUT_W, relation)
+        gather.arrive_x(DOWN_W, relation)
+    for relation in (3, 6):
+        gather.arrive_y(relation, 0)
+    for relation in (2, 5, 3, 6):
+        gather.arrive_y(relation, 1)
+    for array in (UP_W, OUT_W, DOWN_W, QKV_W):
+        gather.finish(array)
+    for copy in own_copies()[:3]:
+        copy.wait()
+    for half in range(halves):
+        for index in range(2):
+            send_rows(half, index).wait_send()
+        pass_rows(half, False).wait_send()
+    for h in range(heads):
+        for turn in range(turns - 1):
+            send_mixed(h, turn).wait_send()
+            send_mixed(h, turn, True).wait_recv()
+        keep_mixed(h).wait()
+
+
+def front(lengths, layer_in, qkv_piece, up_weight, down_weight, out_weight):
+    local_rows, width = layer_in.shape
+    slot_rows = local_rows * 4
+    head_cols = width // 4
+    heads = head_cols // HEAD
+    vmem = pl.BlockSpec(memory_space=pltpu.VMEM)
+    anywhere = pl.BlockSpec(memory_space=pl.ANY)
+    dma = pltpu.SemaphoreType.DMA
+    hidden = up_weight.shape[1]
+    return pl.pallas_call(
+        front_kernel,
+        in_specs=[pl.BlockSpec(memory_space=pltpu.SMEM)] + [vmem] * 5,
+        out_specs=[vmem] * 9 + [anywhere] * 4,
+        out_shape=[
+            jax.ShapeDtypeStruct((slot_rows, width), low),
+            jax.ShapeDtypeStruct((width, 3 * head_cols), low),
+            jax.ShapeDtypeStruct((8,) + qkv_piece.shape, low),
+            jax.ShapeDtypeStruct((heads, WIDE, slot_rows), low),
+            jax.ShapeDtypeStruct((head_cols, slot_rows), low),
+            jax.ShapeDtypeStruct((heads, slot_rows, WIDE), low),
+            jax.ShapeDtypeStruct((heads, slot_rows, WIDE), low),
+            jax.ShapeDtypeStruct((head_cols, slot_rows), full),
+            jax.ShapeDtypeStruct((heads, 8, slot_rows), full),
+            jax.ShapeDtypeStruct((width, hidden), low),
+            jax.ShapeDtypeStruct((hidden, width), low),
+            jax.ShapeDtypeStruct((width, width), low),
+            jax.ShapeDtypeStruct((width, local_rows), low),
+        ],
+        scratch_shapes=[
+            pltpu.VMEM((heads, WIDE, slot_rows), low),
+            pltpu.VMEM((head_cols, slot_rows), low),
+            dma((2, 2)), dma((2, 2)), dma((2,)), dma((2,)), dma((heads, 4)), dma((heads, 4)), dma((5,)),
+            dma((4, 2, 3)), dma((4, 2, 3)), dma((4, 7)), dma((4, 7)), dma((3, 7, 2)), dma((3, 7, 2)),
+            dma((7, 2)), dma((7, 2)), dma((7, 2)), dma((7, 2)),
+        ],
+        compiler_params=pltpu.CompilerParams(
+            vmem_limit_bytes=VMEM_BYTES, collective_id=0, has_side_effects=True
+        ),
+        name="front",
+    )(lengths, layer_in, qkv_piece, up_weight, down_weight, out_weight)
+
+
 def normalize(values, gain_vec, shift_vec):
     centre = values - jnp.mean(values, axis=-1, keepdims=True)
     factor = lax.rsqrt(jnp.mean(centre * centre, axis=-1, keepdims=True) + norm_epsilon)
@@ -253,29 +726,38 @@
     memory = jnp.concatenate([read_memory[0], write_memory[0]], axis=0)
     layer_in = jnp.where(is_memory, mul(picks.astype(low), memory).astype(low), tokens)
 
-    rows = lax.all_gather(layer_in, "seq", axis=0, tiled=True)
     own_shard = lax.dynamic_slice_in_dim(
         qkv_weight.reshape(shard, 3, seq_count, head_cols), seq_place, 1, 2
     ).reshape(shard, 3 * head_cols)
-    weight = lax.all_gather(own_shard, "fsdp", axis=0, tiled=True)
     vectors = (qv_bias, out_bias, norm1_gain, norm1_bias, up_bias, down_bias, norm2_gain, norm2_bias)
-    packed = lax.all_gather(jnp.concatenate(vectors).reshape(1, -1), "fsdp", axis=0, tiled=True).astype(full)
+    packed = jnp.concatenate(vectors)
+    on_block = (fsdp_count, seq_count) == (8, 4)
+    if on_block:
+        spare = jnp.zeros((14, 3 * head_cols), low)
+        piece = jnp.concatenate([own_shard, packed.reshape(2, -1), spare], axis=0)
+        (rows, weight, pieces, q_x, k_t, k_wide, v_wide, mixed, row_stats, up_full, down_full, out_full,
+         attended) = front(lengths, layer_in, piece, up_weight, down_weight, out_weight)
+        packed = pieces[:, shard : shard + 2].reshape(fsdp_count, -1).astype(full)
+    else:
+        rows = lax.all_gather(layer_in, "seq", axis=0, tiled=True)
+        weight = lax.all_gather(own_shard, "fsdp", axis=0, tiled=True)
+        packed = lax.all_gather(packed.reshape(1, -1), "fsdp", axis=0, tiled=True).astype(full)
     whole, start = [], 0
     for vector in vectors:
         whole.append(packed[:, start : start + vector.shape[0]].reshape(-1))
         start += vector.shape[0]
     qv_vec, out_vec, gain_one, shift_one, up_vec, down_vec, gain_two, shift_two = whole
-    own_qv = lax.dynamic_slice_in_dim(qv_vec.reshape(2, seq_count, head_cols), seq_place, 1, 1)
-    bias = jnp.concatenate(
-        [own_qv[0, 0], jnp.zeros((head_cols,), full), own_qv[1, 0], jnp.zeros((-3 * head_cols % WIDE,), full)]
-    )
-    bias = jnp.broadcast_to(bias, (8, bias.shape[0]))
-    out_full = lax.all_gather(out_weight, "fsdp", axis=0, tiled=True)
-    up_full = lax.all_gather(up_weight, "fsdp", axis=0, tiled=True)
-    down_full = lax.all_gather(down_weight, "fsdp", axis=0, tiled=True)
-
-    q_x, k_t, k_wide, v_wide, mixed, mixed_low, row_stats = attention_forward(lengths, rows, weight, bias)
-    attended = lax.all_to_all(mixed_low, "seq", split_axis=1, concat_axis=0, tiled=True)
+    if not on_block:
+        own_qv = lax.dynamic_slice_in_dim(qv_vec.reshape(2, seq_count, head_cols), seq_place, 1, 1)
+        bias = jnp.concatenate(
+            [own_qv[0, 0], jnp.zeros((head_cols,), full), own_qv[1, 0], jnp.zeros((-3 * head_cols % WIDE,), full)]
+        )
+        bias = jnp.broadcast_to(bias, (8, bias.shape[0]))
+        out_full = lax.all_gather(out_weight, "fsdp", axis=0, tiled=True)
+        up_full = lax.all_gather(up_weight, "fsdp", axis=0, tiled=True)
+        down_full = lax.all_gather(down_weight, "fsdp", axis=0, tiled=True)
+        q_x, k_t, k_wide, v_wide, mixed, mixed_low, row_stats = attention_forward(lengths, rows, weight, bias)
+        attended = lax.all_to_all(mixed_low, "seq", split_axis=1, concat_axis=0, tiled=True)
     resid_one = layer_in.astype(full) + mul(attended, out_full, TN) + out_vec
     middle, norm_one_back = jax.vjp(normalize, resid_one, gain_one, shift_one)
     middle_low = middle.astype(low)

time: 768 us -> 638 us (0.83)
  waiting for transfers between devices: 432 us -> 320 us
  Pallas kernels: 75.1 us -> 124 us
  blocking collectives: 128 us -> 79.2 us
  starting transfers between devices: 15.5 us -> 0.24 us
    all_gather x4 -> x0, waiting for transfers between devices: 101 us -> none  [the longest x1 60.5 us: per_device(): down_full = lax.all_gather(down_weight, 'fsdp', axis=0, tiled=True)]
    all_gather x2 -> x0, blocking collectives: 53.5 us -> none  [the longest x1 31.4 us: per_device(): weight = lax.all_gather(own_shard, 'fsdp', axis=0, tiled=True)]
    pallas_call x1, Pallas kernels: 27.9 us -> 77 us  [front(): pl.pallas_call(front_kernel, in_specs=[pl.BlockSpec(memory_space=pltpu.SM...]
    all_to_all x1 -> x0, starting transfers between devices: 14.9 us -> none  [per_device(): lax.all_to_all(mixed_low, 'seq', split_axis=1, concat_axis=0, tiled=True)]
    all_to_all x1 -> x0, waiting for transfers between devices: 9.99 us -> none  [per_device(): lax.all_to_all(mixed_low, 'seq', split_axis=1, concat_axis=0, tiled=True)]
  transfers between devices with their start and end apart: 11 -> 6, of which waited for: 8 -> 6; matrix products, arithmetic and copies ran while one was open for 7% -> 5% of each run, Pallas kernels for 4% -> 0%
where the time goes in v2:
time: 638 us; the launch traced here: 632 us
  waiting for transfers between devices  320 us (50%)
  Pallas kernels  124 us (19%)
  blocking collectives  79.2 us (12%)
  matrix products  57.5 us (9%)
  local copies, waits for them, and re-layouts  19.6 us (3%)
  other arithmetic  15.7 us (2%)
  between operations  15.3 us (2%)
    reduce_scatter x3, waiting for transfers between devices, both_axes(): lax.psum_scatter(part.astype(low), 'fsdp', scatter_dimension=0, tiled=True)  252 us
    pallas_call x1, Pallas kernels, front(): pl.pallas_call(front_kernel, in_specs=[pl.BlockSpec(memory_space=pltpu.SM...  77 us
    dot_general x10, matrix products, mul(): return lax.dot_general(left, right, dims, preferred_element_type=full)  55.5 us
    pallas_call x1, Pallas kernels, attention_backward(): pl.pallas_call(backward_kernel, in_specs=[vmem] * 9, out_specs=[vmem] * 3...  47.1 us
    psum x1, blocking collectives, per_device(): packed_sum = lax.psum(packed_grad, ('fsdp', 'seq'))  44.5 us
    reduce_scatter x1, waiting for transfers between devices, per_device(): lax.psum_scatter(partial_in, 'seq', scatter_dimension=0, tiled=True)  40.3 us
    psum x1, waiting for transfers between devices, both_axes(): return lax.psum(piece, 'seq').astype(full)  26.5 us
    all_to_all x1, blocking collectives, per_device(): lax.all_to_all(grad_attended, 'seq', split_axis=0, concat_axis=1, tiled=T...  13.8 us
  transfers between devices with their start and end apart: 6, of which 6 were waited for; matrix products, arithmetic and copies ran while one was open for 5% of the time, Pallas kernels for 0%

profile of v2, /device:TPU:9, one launch (start us, length us, event | category | flops | bytes accessed | tf_op | source)
XLA Modules:
  0.0 631.9 jit_solution(13440617047433758042)
XLA Ops:
  7.9 5.5 concatenate.17
  13.4 1.6 reshape.170
  16.7 2.5 fusion.8.rows_in
  19.1 77.0 %front.1 = (bf16[2048,768]{1,0:T(8,128)(2,1)}, bf16[768,576]{1,0:T(8,128)(2,1)}, bf16[8,112,576]{2,1,0:T(8,128)(2,1)}, bf16[3,128,2048]{2,1,0:T(8,128)(2,1)}, bf...) custom-call(s32[1]{0:T(128)} %copy.75.length_ref, ...), custom_call_target="tpu_custom_call" | custom-call | tf_op jit(solution)/shard_map/front/pallas_call | solution.py:665
  97.6 2.8 fusion.27
  100.8 18.6 %multiply_convert_fusion = (bf16[512,3072]{1,0:T(8,128)(2,1)S(1)}, f32[512,3072]{1,0:T(8,128)}, f32[512,3072]{1,0:T(8,128)}) fusion(f32[3072]{0:T(1024)S(1)} %add.148, bf16[768,3072]{1,0:T(8,128)(2,1)S(1)} %copy-done.7, f32[512,768]{1,0:T(8,128)S(1)} %get-tuple-element.170, f32[768]{0:T(1024)S(1)} %add.145, f32[768]{0:T(1024)S(1)} %mul.147, ...), kind=kOutput, calls=%fused_computation.4 | convolution fusion | flops 2521694208 | bytes 22042624 | tf_op jit(solution)/shard_map/dot_general | solution.py:27
  119.4 2.8 fusion.28
  122.6 1.9 multiply_reduce_fusion
  124.5 3.0 fusion.24
  127.7 8.5 %convert_reduce_fusion = (f32[3072]{0:T(1024)S(1)}, bf16[512,3072]{1,0:T(8,128)(2,1)S(1)}) fusion(f32[512,3072]{1,0:T(8,128)} %get-tuple-element.150, f32[512,3072]{1,0:T(8,128)} %get-tuple-element.171, f32[3072]{0:T(1024)S(1)} %add.148, bf16[512,768]{1,0:T(8,128)(2,1)S(1)} %get-tuple-element.140, bf16[3072,768]{1,0:T(8,128)(2,1)} %get-tuple-element.36), kind=kOutput, calls=%fused_computation.2 | convolution fusion | flops 2442654720 | bytes 21258240 | tf_op jit(solution)/shard_map/dot_general | solution.py:27
  136.3 3.2 multiply_reduce_fusion.1
  141.6 13.8 %all_to_all.19 = bf16[4,192,512]{2,1,0:T(8,128)(2,1)S(1)} all-to-all(bf16[4,192,512]{2,1,0:T(8,128)(2,1)S(1)} %bitcast.53), channel_id=1, replica_groups=mesh['fsdp'=8,'seq'=4] {'seq'}, dimensions={0} | all-to-all | bytes 1572864 | tf_op jit(solution)/shard_map/all_to_all | solution.py:782
  155.4 1.0 copy.70
  156.3 47.1 %attention_backward.1 = (bf16[2048,768]{1,0:T(8,128)(2,1)}, bf16[768,576]{1,0:T(8,128)(2,1)}, f32[576,128]{1,0:T(8,128)}) custom-call(bf16[3,128,2048]{2,1,0:T(8,128)(2,1)} %get-tuple-element.37.q_in, bf16[192,2048]{1,0:T(8,128)(2,1)} %get-tuple-element.38.k_t, bf16[3,2048,128]{2,1,0:T(8,128)(2,1)} %get-tuple-element.39.k_wide, ...), custom_call_target="tpu_custom_call" | custom-call | tf_op jit(solution)/shard_map/attention_backward/pallas_call | solution.py:207
  203.5 3.3 convolution_convert_fusion.2
  206.9 6.4 %convolution_convert_fusion.1 = bf16[768,3072]{1,0:T(8,128)(2,1)} fusion(bf16[512,3072]{1,0:T(8,128)(2,1)} %copy-done.9, f32[512,768]{1,0:T(8,128)S(1)} %copy-done.3, f32[768]{0:T(1024)S(1)} %add.145, f32[768]{0:T(1024)S(1)} %mul.147, f32[512]{0:T(512)S(1)} %fusion.15, f32[512]{0:T(512)S(1)} %broadcast_multiply_fusion.1), kind=kOutput, calls=%fused_computation.19 | convolution fusion | flops 2420244480 | bytes 9447424 | tf_op jit(solution)/shard_map/dot_general | solution.py:27
  213.4 6.7 %convolution_convert_fusion = bf16[3072,768]{1,0:T(8,128)(2,1)} fusion(bf16[512,3072]{1,0:T(8,128)(2,1)} %copy-done.10, bf16[512,768]{1,0:T(8,128)(2,1)S(1)} %get-tuple-element.140), kind=kOutput, calls=%fused_computation.18 | convolution fusion | flops 2418278400 | bytes 8650752 | tf_op jit(solution)/shard_map/dot_general | solution.py:27
  221.6 44.5 %psum.36 = f32[8,1152]{1,0:T(8,128)S(1)} all-reduce(f32[8,1152]{1,0:T(8,128)S(1)} %concatenate.19), channel_id=1, replica_groups=mesh['fsdp'=8,'seq'=4] {'fsdp','seq'}, use_global_device_ids=true, to_apply=%region_19.20 | all-reduce | flops 9216 | bytes 73728 | tf_op jit(solution)/shard_map/psum | solution.py:803
  268.7 9.7 %all-gather = bf16[384,576]{1,0:T(8,128)(2,1)S(1)} all-gather(bf16[96,576]{1,0:T(8,128)(2,1)} %reduce-scatter.8.cloned.1.call-done), channel_id=2, replica_groups=mesh['fsdp'=8,'seq'=4] {'seq'}, dimensions={0}, use_global_device_ids=true | all-gather | bytes 552960 | tf_op jit(solution)/shard_map/all_gather | solution.py:816
  279.2 1.8 copy.65
  281.0 3.0 reshape.181
  284.0 52.1 %reduce-scatter.10.cloned.1.call-done = bf16[96,768]{1,0:T(8,128)(2,1)} async-done(((bf16[768,768]{1,0:T(8,128)(2,1)}), bf16[96,768]{1,0:T(8,128)(2,1)}) %reduce-scatter.10.cloned.1.call-update) | async-done | bytes 147472 | tf_op jit(solution)/shard_map/reduce_scatter | solution.py:812
  336.1 100.9 %reduce-scatter.12.cloned.1.call-done = bf16[96,3072]{1,0:T(8,128)(2,1)} async-done(((bf16[768,3072]{1,0:T(8,128)(2,1)}), bf16[96,3072]{1,0:T(8,128)(2,1)}) %reduce-scatter.12.cloned.1.call-update) | async-done | bytes 589840 | tf_op jit(solution)/shard_map/reduce_scatter | solution.py:812
  437.1 99.0 %reduce-scatter.14.cloned.1.call-done = bf16[384,768]{1,0:T(8,128)(2,1)} async-done(((bf16[3072,768]{1,0:T(8,128)(2,1)}), bf16[384,768]{1,0:T(8,128)(2,1)}) %reduce-scatter.14.cloned.1.call-update) | async-done | bytes 589840 | tf_op jit(solution)/shard_map/reduce_scatter | solution.py:812
  536.1 40.3 %reduce-scatter.6.cloned.1.call-done = bf16[512,768]{1,0:T(8,128)(2,1)} async-done(((bf16[2048,768]{1,0:T(8,128)(2,1)}), bf16[512,768]{1,0:T(8,128)(2,1)}) %reduce-scatter.6.cloned.1.call-update) | async-done | bytes 786448 | tf_op jit(solution)/shard_map/reduce_scatter | solution.py:786
  576.4 2.0 convolution_convert_fusion.5
  578.4 11.3 %psum.35 = bf16[20,768]{1,0:T(8,128)(2,1)S(1)} all-reduce(bf16[20,768]{1,0:T(8,128)(2,1)S(1)} %convolution_convert_fusion.5), channel_id=1, replica_groups=mesh['fsdp'=8,'seq'=4] {'seq'}, use_global_device_ids=true, to_apply=%region_10.11 | all-reduce | flops 15360 | bytes 61440 | tf_op jit(solution)/shard_map/psum | solution.py:792
  591.0 1.4 fusion.10
  592.4 26.5 %all-reduce.3.cloned.1.call-done = (bf16[96,768]{1,0:T(8,128)(2,1)}, bf16[96,3072]{1,0:T(8,128)(2,1)}, bf16[384,768]{1,0:T(8,128)(2,1)}) async-done(((bf16[96,768]{1,0:T(8,128)(2,1)}, bf16[96,3072]{1,0:T(8,128)(2,1)}, bf16[384,768]{1,0:T(8,128)(2,1)}), (bf16[96,768]{1,0:T(8,128)(2,1)}, bf16[96,3072]{1,0:T(8,128)(2,1)}, bf16[384,768]{1,0:T(8,128)(2,1)})) %all-reduce.3.cloned.1.call-update) | async-done | bytes 1327120 | tf_op jit(solution)/shard_map/psum | solution.py:813
  618.9 1.6 convert_element_type.115
  620.6 2.2 convert_element_type.117
  622.8 2.2 convert_element_type.119
  (104 shorter events, 12.6 us)
Async XLA Ops:
  7.2 261.5 %reduce-scatter.8.cloned.1.call-start = ((), (), s32[]{:S(2)}) async-start(), calls=%async_computation.7 | async-start | bytes 1105920 | tf_op jit(solution)/shard_map/reduce_scatter | solution.py:815
  97.6 3.2 copy-start.7
  97.6 21.7 %slice-start.2 = ((s8[4718592]{0:T(1024)(128)(4,1)}), s8[4194304]{0:T(1024)(128)(4,1)S(1)}, s32[]{:S(2)}) async-start(s8[4718592]{0:T(1024)(128)(4,1)} %bitcast.62), calls=%async_computation.14 | async-start | bytes 8388608
  100.4 39.0 %copy-start.2 = (f32[512,768]{1,0:T(8,128)}, f32[512,768]{1,0:T(8,128)S(1)}, u32[]{:S(2)}) copy-start(f32[512,768]{1,0:T(8,128)S(1)} %get-tuple-element.170) | copy-start | bytes 4718596
  100.8 18.6 %slice-start.3 = ((s8[4718592]{0:T(1024)(128)(4,1)}), s8[524288]{0:T(1024)(128)(4,1)S(1)}, s32[]{:S(2)}) async-start(s8[4718592]{0:T(1024)(128)(4,1)} %bitcast.62), calls=%async_computation.15 | async-start | bytes 1048576
  119.4 2.8 copy-start.10
  124.5 11.7 %slice-start = ((s8[4718592]{0:T(1024)(128)(4,1)}), s8[4194304]{0:T(1024)(128)(4,1)S(1)}, s32[]{:S(2)}) async-start(s8[4718592]{0:T(1024)(128)(4,1)} %bitcast.60), calls=%async_computation.12 | async-start | bytes 8388608
  127.7 8.5 %slice-start.1 = ((s8[4718592]{0:T(1024)(128)(4,1)}), s8[524288]{0:T(1024)(128)(4,1)S(1)}, s32[]{:S(2)}) async-start(s8[4718592]{0:T(1024)(128)(4,1)} %bitcast.60), calls=%async_computation.13 | async-start | bytes 1048576
  136.2 3.2 copy-start.9
  139.5 1.3 copy-start.8
  140.1 15.2 %copy-start = (f32[512,768]{1,0:T(8,128)}, f32[512,768]{1,0:T(8,128)S(1)}, u32[]{:S(2)}) copy-start(f32[512,768]{1,0:T(8,128)S(1)} %get-tuple-element.146) | copy-start | bytes 4718596
  140.4 16.0 %copy-start.5 = (bf16[512,768]{1,0:T(8,128)(2,1)}, bf16[512,768]{1,0:T(8,128)(2,1)S(1)}, u32[]{:S(2)}) copy-start(bf16[512,768]{1,0:T(8,128)(2,1)S(1)} %get-tuple-element.144) | copy-start | bytes 2359300
  203.5 3.4 copy-start.3
  203.5 132.7 %reduce-scatter.10.cloned.1.call-start = ((), (), s32[]{:S(2)}) async-start(), calls=%async_computation.8 | async-start | bytes 1327104 | tf_op jit(solution)/shard_map/reduce_scatter | solution.py:812
  206.8 230.2 %reduce-scatter.12.cloned.1.call-start = ((), (), s32[]{:S(2)}) async-start(), calls=%async_computation.9 | async-start | bytes 5308416 | tf_op jit(solution)/shard_map/reduce_scatter | solution.py:812
  213.3 322.7 %reduce-scatter.14.cloned.1.call-start = ((), (), s32[]{:S(2)}) async-start(), calls=%async_computation.10 | async-start | bytes 5308416 | tf_op jit(solution)/shard_map/reduce_scatter | solution.py:812
  220.1 1.1 copy-start.6
  220.1 356.2 %reduce-scatter.6.cloned.1.call-start = ((), (), s32[]{:S(2)}) async-start(), calls=%async_computation.6 | async-start | bytes 3932160 | tf_op jit(solution)/shard_map/reduce_scatter | solution.py:786
  220.7 398.2 %all-reduce.3.cloned.1.call-start = ((), (), s32[]{:S(2)}) async-start(), calls=%async_computation.11 | async-start | bytes 2654208 | tf_op jit(solution)/shard_map/psum | solution.py:813
  279.2 297.2 %copy-start.1 = (f32[512,768]{1,0:T(8,128)S(1)}, f32[512,768]{1,0:T(8,128)}, u32[]{:S(2)}) copy-start(f32[512,768]{1,0:T(8,128)} %copy-done) | copy-start | bytes 4718596
  576.4 14.6 %copy-start.4 = (bf16[512,768]{1,0:T(8,128)(2,1)S(1)}, bf16[512,768]{1,0:T(8,128)(2,1)}, u32[]{:S(2)}) copy-start(bf16[512,768]{1,0:T(8,128)(2,1)} %reduce-scatter.6.cloned.1.call-done) | copy-start | bytes 2359300
Sparse Core Ops, SparseCore 0:
  203.6 65.0 reduce-scatter.7
  273.0 63.0 reduce-scatter.9
  340.2 96.7 reduce-scatter.11
  441.0 95.0 reduce-scatter.13
  538.6 37.7 reduce-scatter.5
  578.8 40.1 all-reduce.2

commit v3 on v2

--- a/solution.py
+++ b/solution.py
@@ -46,9 +46,6 @@
     head_cols = k_t.shape[0]
     lanes = pl.ds(start, step)
     made = mul(weight_ref[...], rows_ref[lanes, :], TT)
-    query = (made[:head_cols] + bias_q).astype(low) * jnp.asarray(HEAD**-0.5, low)
-    k_t[:, lanes] = made[head_cols : 2 * head_cols].astype(low)
-    value = (made[2 * head_cols :] + bias_v).astype(low)
     place = start + lax.broadcasted_iota(jnp.int32, (1, step), 1)
     key_bias = jnp.where(place < length, 0.0, masked_score)
     one = jnp.ones((1, step), full)
@@ -57,9 +54,12 @@
     value_extra = stack_rows([one, one, one], step)
     for h in range(head_cols // HEAD):
         own = slice(h * HEAD, (h + 1) * HEAD)
-        q_x[h, :HEAD, lanes] = query[own]
+        base = 3 * h * HEAD
+        query = (made[base : base + HEAD] + bias_q[own]).astype(low)
+        q_x[h, :HEAD, lanes] = query * jnp.asarray(HEAD**-0.5, low)
         q_x[h, HEAD:, lanes] = query_extra
-        v_x[h, :HEAD, lanes] = value[own]
+        k_t[own, lanes] = made[base + HEAD : base + 2 * HEAD].astype(low)
+        v_x[h, :HEAD, lanes] = (made[base + 2 * HEAD : base + 3 * HEAD] + bias_v[own]).astype(low)
         v_x[h, HEAD:, lanes] = value_extra
         k_wide[h, lanes, :] = jnp.transpose(jnp.concatenate([k_t[own, lanes], key_extra], axis=0))
         v_wide[h, lanes, :] = jnp.transpose(v_x[h, :, lanes])
@@ -70,7 +70,7 @@
     bias = jnp.transpose(bias_ref[...])[:, 0:1]
     for start in range(0, rows_ref.shape[0], 512):
         project_block(
-            start, length, rows_ref, weight_ref, bias[:head_cols], bias[2 * head_cols : 3 * head_cols],
+            start, length, rows_ref, weight_ref, bias[:head_cols], bias[head_cols:],
             q_x, k_t, v_x, k_wide, v_wide, 512,
         )
 
@@ -129,24 +129,21 @@
     )(length, rows, weight, bias)
 
 
-def prepare_backward(h, q_x, do_x, grad_t, mixed, row_stats):
-    slot_rows = grad_t.shape[1]
-    own = slice(h * HEAD, (h + 1) * HEAD)
-    grad = grad_t[own, :]
-    delta = jnp.sum(grad.astype(full) * mixed[own, :], axis=0, keepdims=True)
+def attend_back(h, lanes, q_x, q_here, do_x, grad_t, mixed, row_stats, k_t, k_wide, v_wide, grads, grad_k, grad_v, first):
+    own = pl.ds(pl.multiple_of(h * HEAD, HEAD), HEAD)
+    grad = grad_t[own, lanes]
+    columns = grad.shape[1]
+    delta = jnp.sum(grad.astype(full) * mixed[own, lanes], axis=0, keepdims=True)
     parts = [part.astype(full) for part in three_parts(-delta)]
-    do_x[h, :HEAD, :] = grad
-    do_x[h, HEAD:, :] = stack_rows(parts, slot_rows)
-    parts = [part.astype(full) for part in three_parts(-row_stats[h, 0:1, :])]
-    q_x[h, HEAD:, :] = stack_rows([jnp.ones((1, slot_rows), full)] + parts, slot_rows)
-
-
-def attend_back_block(h, lanes, first, q_x, do_x, k_t, k_wide, v_wide, grad_q, grad_k, grad_v):
-    own = pl.ds(h * HEAD, HEAD)
-    probs = jnp.exp(mul(k_wide[h], q_x[h, :, lanes]))
-    grad_scores = (probs * mul(v_wide[h], do_x[h, :, lanes])).astype(low)
-    value_part = mul(do_x[h, :HEAD, lanes], probs.astype(low), NT)
-    key_part = mul(q_x[h, :HEAD, lanes], grad_scores, NT)
+    do_x[:HEAD, :] = grad
+    do_x[HEAD:, :] = stack_rows(parts, columns)
+    parts = [part.astype(full) for part in three_parts(-row_stats[h, 0:1, lanes])]
+    q_here[:HEAD, :] = q_x[h, :HEAD, lanes]
+    q_here[HEAD:, :] = stack_rows([jnp.ones((1, columns), full)] + parts, columns)
+    probs = jnp.exp(mul(k_wide[h], q_here[...]))
+    grad_scores = (probs * mul(v_wide[h], do_x[...])).astype(low)
+    value_part = mul(grad, probs.astype(low), NT)
+    key_part = mul(q_here[:HEAD, :], grad_scores, NT)
 
     @pl.when(first)
     def _():
@@ -158,18 +155,15 @@
         grad_v[...] += value_part
         grad_k[...] += key_part
 
-    grad_q[own, lanes] = (mul(k_t[own, :], grad_scores) * HEAD**-0.5).astype(low)
+    query_part = mul(k_t[own, :], grad_scores) * HEAD**-0.5
+    grads[pl.ds(pl.multiple_of(3 * h * HEAD, HEAD), HEAD), lanes] = query_part.astype(low)
 
 
 def backward_kernel(
     q_in, k_t, k_wide, v_wide, mixed, row_stats, grad_t, rows_ref, weight_ref,
-    partial_out, weight_out, sums_out, q_x, do_x, grads, grad_k, grad_v,
+    partial_out, weight_out, sums_out, q_here, do_x, grads, grad_k, grad_v,
 ):
     heads, _, slot_rows = q_in.shape
-    head_cols = heads * HEAD
-    q_x[:, :HEAD, :] = q_in[:, :HEAD, :]
-    for h in range(heads):
-        prepare_backward(h, q_x, do_x, grad_t, mixed, row_stats)
     block = 512
     blocks = slot_rows // block
 
@@ -177,15 +171,16 @@
         h = index // blocks
         turn = lax.rem(index, blocks)
         start = pl.multiple_of(turn * block, block)
-        attend_back_block(
-            h, pl.ds(start, block), turn == 0, q_x, do_x, k_t, k_wide, v_wide,
-            grads, grad_k, grad_v,
+        attend_back(
+            h, pl.ds(start, block), q_in, q_here, do_x, grad_t, mixed, row_stats, k_t, k_wide, v_wide, grads, grad_k,
+            grad_v, turn == 0,
         )
 
         @pl.when(turn == blocks - 1)
         def _():
-            grads[pl.ds(head_cols + h * HEAD, HEAD), :] = grad_k[...].astype(low)
-            grads[pl.ds(2 * head_cols + h * HEAD, HEAD), :] = grad_v[...].astype(low)
+            base = pl.multiple_of(3 * h * HEAD, HEAD)
+            grads[pl.ds(base + HEAD, HEAD), :] = grad_k[...].astype(low)
+            grads[pl.ds(base + 2 * HEAD, HEAD), :] = grad_v[...].astype(low)
 
         return carry
 
@@ -214,8 +209,8 @@
             jax.ShapeDtypeStruct((all_cols, WIDE), full),
         ],
         scratch_shapes=[
-            pltpu.VMEM((heads, WIDE, slot_rows), low),
-            pltpu.VMEM((heads, WIDE, slot_rows), low),
+            pltpu.VMEM((WIDE, 512), low),
+            pltpu.VMEM((WIDE, 512), low),
             pltpu.VMEM((all_cols, slot_rows), low),
             pltpu.VMEM((HEAD, slot_rows), full),
             pltpu.VMEM((HEAD, slot_rows), full),
@@ -695,6 +690,506 @@
     )(lengths, layer_in, qkv_piece, up_weight, down_weight, out_weight)
 
 
+DW_FIRST = 3
+LINES = (3, 0, 2, 1)
+
+
+def add_low(left, right):
+    return (left.astype(full) + right.astype(full)).astype(low)
+
+
+class Reduce:
+    def __init__(self, place, given, mine, sums, from_y, from_x, from_z, sems):
+        self.place, self.given, self.mine, self.sums = place, given, mine, sums
+        self.from_y, self.from_x, self.from_z = from_y, from_x, from_z
+        (self.c_send, self.c_recv, self.y_send, self.y_recv, self.x_send, self.x_recv, self.z_send,
+         self.z_recv) = sems
+
+    def dest(self, column, line):
+        x = self.place.x
+        return 2 * line + (x if column == 0 else 1 - x)
+
+    def part_of(self, ref, array, column, line, core, far):
+        dest = self.dest(column, line)
+        if array == DOWN_W:
+            rows = ref.shape[0] // 8
+            part = rows // 4
+            y = self.place.y if not far else 1 - self.place.y
+            return ref.at[pl.ds(pl.multiple_of(dest * rows + (2 * y + core) * part, part), part)]
+        rows, columns = ref.shape[0] // 8, ref.shape[1] // 2
+        return ref.at[
+            pl.ds(pl.multiple_of(dest * rows, rows), rows), pl.ds(pl.multiple_of(core * columns, columns), columns)
+        ]
+
+    def slot(self, array, column, line, far=0):
+        if array >= DW_FIRST:
+            return self.sums[array].at[self.dest(column, line)]
+        if array == DOWN_W:
+            return self.sums[array].at[column, line, far]
+        return self.sums[array].at[column, line]
+
+    def load_mine(self, array, column, line, far, sem):
+        target = self.mine[array].at[column, line, far] if array == DOWN_W else self.mine[array].at[column, line]
+        return pltpu.make_async_copy(
+            self.part_of(self.given[array], array, column, line, self.place.c, far), target, sem
+        )
+
+    def to_core(self, array, column, line, far=0):
+        index = array + far
+        return remote(
+            self.part_of(self.given[array], array, column, line, 1 - self.place.c, far),
+            self.slot(array, column, line, far),
+            self.c_send.at[index, column, line], self.c_recv.at[index, column, line], self.place.core,
+        )
+
+    def add_core(self, array, column, line, far=0):
+        self.to_core(array, column, line, far).wait_recv()
+        slot = self.slot(array, column, line, far)
+        own = self.mine[array].at[column, line, far] if array == DOWN_W else self.mine[array].at[column, line]
+        slot[...] = add_low(slot[...], own[...])
+
+    def over_y(self, column, line):
+        return remote(
+            self.slot(DOWN_W, column, line, 1), self.from_y.at[column, line],
+            self.y_send.at[column, line], self.y_recv.at[column, line], self.place.across_y,
+        )
+
+    def add_y(self, column, line):
+        self.over_y(column, line).wait_recv()
+        slot = self.slot(DOWN_W, column, line, 0)
+        slot[...] = add_low(slot[...], self.from_y[column, line])
+
+    def over_x(self, array, line):
+        return remote(
+            self.slot(array, 1, line), self.from_x[array].at[line],
+            self.x_send.at[array, line], self.x_recv.at[array, line], self.place.across_x,
+        )
+
+    def add_x(self, array, line):
+        self.over_x(array, line).wait_recv()
+        slot = self.slot(array, 0, line)
+        slot[...] = add_low(slot[...], self.from_x[array][line])
+
+    def along_z(self, array, way, line):
+        return remote(
+            self.slot(array, 0, line), self.from_z[array].at[way, line],
+            self.z_send.at[array, way, line], self.z_recv.at[array, way, line],
+            self.place.above if way == 0 else self.place.below,
+        )
+
+    def add_z(self, array, way, line):
+        self.along_z(array, way, line).wait_recv()
+        slot = self.slot(array, 0, line)
+        slot[...] = add_low(slot[...], self.from_z[array][way, line])
+
+    def hop(self, array, level):
+        @pl.when(self.place.z == level)
+        def _():
+            for line in range(3, level, -1):
+                if level > 0:
+                    self.add_z(array, 0, line)
+                self.along_z(array, 0, line).start()
+
+        @pl.when(self.place.z == 3 - level)
+        def _():
+            for line in range(0, 3 - level):
+                if level > 0:
+                    self.add_z(array, 1, line)
+                self.along_z(array, 1, line).start()
+
+    def settle(self, array):
+        for line in range(4):
+
+            @pl.when(self.place.z == line)
+            def _(line=line):
+                if line > 0:
+                    self.add_z(array, 0, line)
+                if line < 3:
+                    self.add_z(array, 1, line)
+
+    def finish(self, array):
+        for line in range(4):
+            self.over_x(array, line).wait_send()
+            pl.when(self.place.z < line)(lambda line=line: self.along_z(array, 0, line).wait_send())
+            pl.when(self.place.z > line)(lambda line=line: self.along_z(array, 1, line).wait_send())
+            if array >= DW_FIRST:
+                continue
+            for column in range(2):
+                for far in range(2 if array == DOWN_W else 1):
+                    self.to_core(array, column, line, far).wait_send()
+                if array == DOWN_W:
+                    self.over_y(column, line).wait_send()
+
+
+def back_kernel(
+    length_ref, grad_own, q_x, k_t, k_wide, v_wide, mixed, row_stats, vectors_in,
+    rows_in, weight_in, resid_in, up_given, down_given, out_given,
+    input_out, read_out, write_out, qkv_out, vector_out, up_out, down_out, out_out,
+    grad_t, q_here, do_x, grads, grad_k, grad_v, rows_ref, weight_ref, resid_ref, up_mine, out_mine, down_mine,
+    up_sum, out_sum, down_sum, dw, down_y, up_x, out_x, down_x, dw_x, up_z, out_z, down_z, dw_z,
+    up_last, out_last, up_other, out_other, down_all, dw_all,
+    near_send, near_recv, near_own, far_sum, far_recv, memory_all,
+    mix_send, mix_recv, local_sem, mine_sem, share_send, share_recv, near_s, near_r, far_s, far_r, memory_s,
+    memory_r, *sems,
+):
+    place = Place()
+    heads, _, slot_rows = q_x.shape
+    width, local_rows = grad_own.shape
+    head_cols = heads * HEAD
+    last = DW_FIRST + heads - 1
+    given = {UP_W: up_given, OUT_W: out_given, DOWN_W: down_given}
+    mine = {UP_W: up_mine, OUT_W: out_mine, DOWN_W: down_mine}
+    sums = {UP_W: up_sum, OUT_W: out_sum, DOWN_W: down_sum}
+    from_x = {UP_W: up_x, OUT_W: out_x, DOWN_W: down_x}
+    from_z = {UP_W: up_z, OUT_W: out_z, DOWN_W: down_z}
+    for h in range(heads):
+        sums[DW_FIRST + h], from_x[DW_FIRST + h] = dw.at[h], dw_x.at[h]
+        from_z[DW_FIRST + h] = dw_z.at[h]
+    reduce = Reduce(place, given, mine, sums, down_y, from_x, from_z, sems)
+    greet(place, None)
+
+    peers = (place.across_y, place.diagonal, place.core)
+
+    def member_rows(turn):
+        member = place.member(turn)
+        return member, pl.ds(pl.multiple_of(member * local_rows, local_rows), local_rows)
+
+    def send_grad(turn, arriving=False):
+        member, lanes = member_rows(turn)
+        own_lanes = pl.ds(pl.multiple_of(place.s * local_rows, local_rows), local_rows)
+        src = grad_own.at[pl.ds(pl.multiple_of(member * head_cols, head_cols), head_cols)]
+        return remote(
+            src, grad_t.at[:, lanes if arriving else own_lanes], mix_send.at[turn], mix_recv.at[turn], peers[turn]
+        )
+
+    for turn in range(3):
+        send_grad(turn).start()
+    loads = []
+    for index, (src, dst) in enumerate(((rows_in, rows_ref), (weight_in, weight_ref), (resid_in, resid_ref))):
+        loads.append(pltpu.make_async_copy(src, dst, local_sem.at[index]))
+    order = (
+        (UP_W, 1, 0), (DOWN_W, 1, 1), (DOWN_W, 0, 1), (UP_W, 0, 0), (OUT_W, 1, 0), (OUT_W, 0, 0), (DOWN_W, 1, 0),
+        (DOWN_W, 0, 0),
+    )
+    for array, column, far in order:
+        for line in LINES:
+            reduce.to_core(array, column, line, far).start()
+            reduce.load_mine(array, column, line, far, mine_sem.at[array + far, column, line]).start()
+    for load in loads:
+        load.start()
+
+    def gather_core(array, column, far=0):
+        for line in LINES:
+            reduce.load_mine(array, column, line, far, mine_sem.at[array + far, column, line]).wait()
+            reduce.add_core(array, column, line, far)
+
+    own_lanes = pl.ds(pl.multiple_of(place.s * local_rows, local_rows), local_rows)
+    grad_t[:, own_lanes] = grad_own[pl.ds(pl.multiple_of(place.s * head_cols, head_cols), head_cols), :]
+
+    def send_x(array):
+        for line in LINES:
+            reduce.over_x(array, line).start()
+
+    def take_x(array):
+        for line in LINES:
+            reduce.add_x(array, line)
+
+    turns = slot_rows // local_rows
+
+    def weight_part(h):
+        if h == 0:
+            loads[0].wait()
+        base = 3 * h * HEAD
+        part = jnp.transpose(mul(grads[base : base + 3 * HEAD, :], rows_ref[...])).astype(low)
+        shard = width // 8
+        for dest in range(8):
+            dw[h, dest, :shard, :] = part[dest * shard : (dest + 1) * shard]
+            if h == heads - 1:
+                dw[h, dest, shard:, :] = vectors_in[dest].astype(low)
+            else:
+                dw[h, dest, shard:, :] = jnp.zeros((16, 3 * HEAD), low)
+        if h == heads - 1:
+            total = jnp.sum(grads[...].astype(full), axis=1, keepdims=True)
+            spread = jnp.transpose(jnp.broadcast_to(total, (total.shape[0], WIDE)))[0:1]
+            for kind, first_dest in ((0, 0), (2, 4)):
+                for head in range(heads):
+                    start = (3 * head + kind) * HEAD
+                    dw[h, first_dest + place.s, shard : shard + 1, head * HEAD : (head + 1) * HEAD] = spread[
+                        :, start : start + HEAD
+                    ].astype(low)
+        send_x(DW_FIRST + h)
+
+    def chores(index):
+        if index == 1:
+            send_grad(2, True).wait_recv()
+            gather_core(UP_W, 1)
+            send_x(UP_W)
+        elif index == 2:
+            send_grad(1, True).wait_recv()
+            for column in (1, 0):
+                gather_core(DOWN_W, column, 1)
+                for line in LINES:
+                    reduce.over_y(column, line).start()
+        elif index == 3:
+            send_grad(0, True).wait_recv()
+            gather_core(OUT_W, 1)
+            send_x(OUT_W)
+            gather_core(OUT_W, 0)
+        elif index == 4:
+            weight_part(0)
+            gather_core(UP_W, 0)
+        elif index == 5:
+            gather_core(DOWN_W, 1)
+            gather_core(DOWN_W, 0)
+        elif index == 6:
+            for line in LINES:
+                reduce.add_y(1, line)
+            send_x(DOWN_W)
+        elif index == 7:
+            take_x(UP_W)
+            reduce.hop(UP_W, 0)
+        elif index == 8:
+            weight_part(1)
+            take_x(OUT_W)
+            reduce.hop(OUT_W, 0)
+            take_x(DW_FIRST)
+            reduce.hop(DW_FIRST, 0)
+        elif index == 9:
+            for line in LINES:
+                reduce.add_y(0, line)
+        elif index == 10:
+            reduce.hop(UP_W, 1)
+            reduce.hop(DW_FIRST, 1)
+        elif index == 11:
+            take_x(DOWN_W)
+            reduce.hop(DOWN_W, 0)
+            reduce.hop(OUT_W, 1)
+            reduce.hop(DW_FIRST, 2)
+
+    def step(index, carry):
+        for when in range(1, 12):
+            pl.when(index == when)(lambda when=when: chores(when))
+        h, turn = index // turns, lax.rem(index, turns)
+        _, lanes = member_rows(turns - 1 - turn)
+        attend_back(
+            h, lanes, q_x, q_here, do_x, grad_t, mixed, row_stats, k_t, k_wide, v_wide, grads, grad_k, grad_v, turn == 0
+        )
+
+        @pl.when(turn == turns - 1)
+        def _():
+            base = pl.multiple_of(3 * h * HEAD, HEAD)
+            grads[pl.ds(base + HEAD, HEAD), :] = grad_k[...].astype(low)
+            grads[pl.ds(base + 2 * HEAD, HEAD), :] = grad_v[...].astype(low)
+
+        return carry
+
+    lax.fori_loop(0, heads * turns, step, 0)
+
+    weight_part(heads - 1)
+    loads[1].wait()
+
+    def part_for(turn):
+        _, lanes = member_rows(turn)
+        return mul(grads[:, lanes], weight_ref[...], TT)
+
+    def share_near(index):
+        return remote(
+            near_send.at[index], near_recv.at[index], near_s.at[index], near_r.at[index], place.core
+        )
+
+    def share_far():
+        return remote(far_sum, far_recv, far_s.at[0], far_r.at[0], place.across_y)
+
+    near_send[0] = part_for(1).astype(low)
+    share_near(0).start()
+    near_own[...] = part_for(0).astype(low)
+    share_near(0).wait_recv()
+    far_sum[...] = add_low(near_own[...], near_recv[0])
+    share_far().start()
+    take_x(last)
+    reduce.hop(last, 0)
+    near_send[1] = part_for(2).astype(low)
+    share_near(1).start()
+    take_x(last - 1)
+    reduce.hop(last - 1, 0)
+    loads[2].wait()
+    resid_ref[...] += part_for(3)
+    reduce.hop(last, 1)
+    reduce.hop(last - 1, 1)
+    reduce.hop(UP_W, 2)
+    reduce.hop(OUT_W, 2)
+    reduce.hop(DOWN_W, 1)
+    reduce.hop(last, 2)
+    reduce.hop(last - 1, 2)
+    reduce.hop(DOWN_W, 2)
+
+    share = {UP_W: (up_last, up_other), OUT_W: (out_last, out_other)}
+
+    def sum_y(array):
+        mine_now = sums[array].at[0, place.z]
+        return remote(mine_now, share[array][0], share_send.at[array, 0], share_recv.at[array, 0], place.across_y)
+
+    def half_to_core(array):
+        mine_now = sums[array].at[0, place.z]
+        return remote(mine_now, share[array][1], share_send.at[array, 1], share_recv.at[array, 1], place.core)
+
+    def quarter_to(turn, arriving=False):
+        member = place.member(turn) if arriving else place.s
+        return remote(
+            down_sum.at[0, place.z, 0], down_all.at[member], share_send.at[2, turn], share_recv.at[2, turn], peers[turn]
+        )
+
+    def dw_to(h, turn, arriving=False):
+        member = place.member(turn) if arriving else place.s
+        return remote(
+            dw.at[h, place.f], dw_all.at[h, member], share_send.at[DW_FIRST + h, turn],
+            share_recv.at[DW_FIRST + h, turn], peers[turn],
+        )
+
+    reduce.settle(UP_W)
+    sum_y(UP_W).start()
+    reduce.settle(OUT_W)
+    sum_y(OUT_W).start()
+    for h in range(heads):
+        reduce.settle(DW_FIRST + h)
+        for turn in range(3):
+            dw_to(h, turn).start()
+    reduce.settle(DOWN_W)
+    for turn in range(3):
+        quarter_to(turn).start()
+    for array in (UP_W, OUT_W):
+        sum_y(array).wait()
+        slot = sums[array].at[0, place.z]
+        slot[...] = add_low(slot[...], share[array][0][...])
+        half_to_core(array).start()
+
+    share_near(1).wait_recv()
+    share_far().wait_recv()
+    grad_layer = resid_ref[...] + near_recv[1].astype(full) + far_recv[...].astype(full)
+    length = length_ref[0]
+    rows_at = place.s * local_rows + lax.broadcasted_iota(jnp.int32, (local_rows, 1), 0)
+    in_read = rows_at < MEM
+    in_write = (rows_at >= length - MEM) & (rows_at < length)
+    input_out[...] = jnp.where(in_read | in_write, 0.0, grad_layer)
+    line_at = lax.broadcasted_iota(jnp.int32, (32, local_rows), 0)
+    row_at = place.s * local_rows + lax.broadcasted_iota(jnp.int32, (32, local_rows), 1)
+    wanted = jnp.where(line_at < 16, line_at, length - MEM + line_at - 16)
+    used = (line_at < MEM) | ((line_at >= 16) & (line_at < 16 + MEM))
+    pick = jnp.where(used & (wanted == row_at), 1.0, 0.0).astype(low)
+    memory_all[place.s] = mul(pick, grad_layer.astype(low)).astype(low)
+
+    def memory_to(turn, arriving=False):
+        member = place.member(turn) if arriving else place.s
+        return remote(
+            memory_all.at[place.s], memory_all.at[member], memory_s.at[turn], memory_r.at[turn], peers[turn]
+        )
+
+    for turn in range(3):
+        memory_to(turn).start()
+
+    for array, out in ((UP_W, up_out), (OUT_W, out_out)):
+        columns = out.shape[1] // 2
+        out[:, pl.ds(pl.multiple_of(place.c * columns, columns), columns)] = sums[array][0, place.z].astype(full)
+        half_to_core(array).wait()
+        out[:, pl.ds(pl.multiple_of((1 - place.c) * columns, columns), columns)] = share[array][1][...].astype(full)
+    down_all[place.s] = down_sum[0, place.z, 0]
+    for turn in range(3):
+        quarter_to(turn).wait_send()
+        quarter_to(turn, True).wait_recv()
+    quarter = down_out.shape[0] // 4
+    for member in range(4):
+        down_out[member * quarter : (member + 1) * quarter, :] = down_all[member].astype(full)
+    shard = qkv_out.shape[0]
+    for h in range(heads):
+        dw_all[h, place.s] = dw[h, place.f]
+        for turn in range(3):
+            dw_to(h, turn).wait_send()
+            dw_to(h, turn, True).wait_recv()
+        for member in range(4):
+            for kind in range(3):
+                start = kind * width + (member * heads + h) * HEAD
+                qkv_out[:, start : start + HEAD] = dw_all[
+                    h, member, :shard, kind * HEAD : (kind + 1) * HEAD
+                ].astype(full)
+    vector_sum = dw_all[heads - 1, 0, shard:, :].astype(full)
+    for member in range(1, 4):
+        vector_sum = vector_sum + dw_all[heads - 1, member, shard:, :].astype(full)
+    vector_out[...] = vector_sum
+    for turn in range(3):
+        memory_to(turn).wait_send()
+        memory_to(turn, True).wait_recv()
+    memory = memory_all[0].astype(full)
+    for member in range(1, 4):
+        memory = memory + memory_all[member].astype(full)
+    read_out[...] = memory[:MEM]
+    write_out[...] = memory[16 : 16 + MEM]
+    for array in range(DW_FIRST + heads):
+        reduce.finish(array)
+    for turn in range(3):
+        send_grad(turn).wait_send()
+    for index in range(2):
+        share_near(index).wait_send()
+    share_far().wait_send()
+
+
+def back(lengths, grad_own, saved, vectors, rows, weight, resid, up_given, down_given, out_given):
+    q_x, k_t, k_wide, v_wide, mixed, row_stats = saved
+    heads, _, slot_rows = q_x.shape
+    width, local_rows = grad_own.shape
+    hidden = up_given.shape[1]
+    shard, head_cols = width // 8, heads * HEAD
+    half, small, piece = hidden // 2, width // 2, hidden // 32
+    vmem = pl.BlockSpec(memory_space=pltpu.VMEM)
+    anywhere = pl.BlockSpec(memory_space=pl.ANY)
+    dma = pltpu.SemaphoreType.DMA
+    arrays = DW_FIRST + heads
+
+    def held(*shape, kind=low):
+        return pltpu.VMEM(shape, kind)
+
+    tall = (shard + 16, 3 * HEAD)
+    return pl.pallas_call(
+        back_kernel,
+        in_specs=[pl.BlockSpec(memory_space=pltpu.SMEM)] + [vmem] * 8 + [anywhere] * 6,
+        out_specs=[vmem] * 8,
+        out_shape=[
+            jax.ShapeDtypeStruct((local_rows, width), full),
+            jax.ShapeDtypeStruct((MEM, width), full),
+            jax.ShapeDtypeStruct((MEM, width), full),
+            jax.ShapeDtypeStruct((shard, 3 * width), full),
+            jax.ShapeDtypeStruct((16, 3 * HEAD), full),
+            jax.ShapeDtypeStruct((shard, hidden), full),
+            jax.ShapeDtypeStruct((hidden // 8, width), full),
+            jax.ShapeDtypeStruct((shard, width), full),
+        ],
+        scratch_shapes=[
+            held(head_cols, slot_rows), held(WIDE, local_rows), held(WIDE, local_rows), held(3 * head_cols, slot_rows),
+            held(HEAD, slot_rows, kind=full), held(HEAD, slot_rows, kind=full),
+            held(slot_rows, width), held(width, 3 * head_cols), held(local_rows, width, kind=full),
+            held(2, 4, shard, half), held(2, 4, shard, small), held(2, 4, 2, piece, width),
+            held(2, 4, shard, half), held(2, 4, shard, small), held(2, 4, 2, piece, width),
+            held(heads, 8, *tall), held(2, 4, piece, width),
+            held(4, shard, half), held(4, shard, small), held(4, piece, width), held(heads, 4, *tall),
+            held(2, 4, shard, half), held(2, 4, shard, small), held(2, 4, piece, width), held(heads, 2, 4, *tall),
+            held(shard, half), held(shard, small), held(shard, half), held(shard, small),
+            held(4, piece, width), held(heads, 4, *tall),
+            held(2, local_rows, width), held(2, local_rows, width), held(local_rows, width),
+            held(local_rows, width), held(local_rows, width), held(4, 32, width),
+            dma((3,)), dma((3,)), dma((3,)), dma((4, 2, 4)), dma((arrays, 3)), dma((arrays, 3)),
+            dma((2,)), dma((2,)), dma((1,)), dma((1,)), dma((3,)), dma((3,)),
+            dma((4, 2, 4)), dma((4, 2, 4)), dma((2, 4)), dma((2, 4)), dma((arrays, 4)), dma((arrays, 4)),
+            dma((arrays, 2, 4)), dma((arrays, 2, 4)),
+        ],
+        compiler_params=pltpu.CompilerParams(
+            vmem_limit_bytes=VMEM_BYTES, collective_id=1, has_side_effects=True
+        ),
+        name="back",
+    )(
+        lengths, grad_own, q_x, k_t, k_wide, v_wide, mixed, row_stats, vectors, rows, weight, resid,
+        up_given, down_given, out_given,
+    )
+
+
 def normalize(values, gain_vec, shift_vec):
     centre = values - jnp.mean(values, axis=-1, keepdims=True)
     factor = lax.rsqrt(jnp.mean(centre * centre, axis=-1, keepdims=True) + norm_epsilon)
@@ -726,9 +1221,11 @@
     memory = jnp.concatenate([read_memory[0], write_memory[0]], axis=0)
     layer_in = jnp.where(is_memory, mul(picks.astype(low), memory).astype(low), tokens)
 
+    heads = head_cols // HEAD
     own_shard = lax.dynamic_slice_in_dim(
-        qkv_weight.reshape(shard, 3, seq_count, head_cols), seq_place, 1, 2
-    ).reshape(shard, 3 * head_cols)
+        qkv_weight.reshape(shard, 3, seq_count, heads, HEAD), seq_place, 1, 2
+    )
+    own_shard = jnp.transpose(own_shard[:, :, 0], (0, 2, 1, 3)).reshape(shard, 3 * head_cols)
     vectors = (qv_bias, out_bias, norm1_gain, norm1_bias, up_bias, down_bias, norm2_gain, norm2_bias)
     packed = jnp.concatenate(vectors)
     on_block = (fsdp_count, seq_count) == (8, 4)
@@ -749,9 +1246,7 @@
     qv_vec, out_vec, gain_one, shift_one, up_vec, down_vec, gain_two, shift_two = whole
     if not on_block:
         own_qv = lax.dynamic_slice_in_dim(qv_vec.reshape(2, seq_count, head_cols), seq_place, 1, 1)
-        bias = jnp.concatenate(
-            [own_qv[0, 0], jnp.zeros((head_cols,), full), own_qv[1, 0], jnp.zeros((-3 * head_cols % WIDE,), full)]
-        )
+        bias = jnp.concatenate([own_qv[0, 0], own_qv[1, 0]])
         bias = jnp.broadcast_to(bias, (8, bias.shape[0]))
         out_full = lax.all_gather(out_weight, "fsdp", axis=0, tiled=True)
         up_full = lax.all_gather(up_weight, "fsdp", axis=0, tiled=True)
@@ -779,47 +1274,56 @@
     grad_branch = grad_resid_one.astype(low)
     grad_out_weight = mul(attended, grad_branch)
     grad_attended = mul(out_full, grad_branch, NT).astype(low)
-    grad_t = lax.all_to_all(grad_attended, "seq", split_axis=0, concat_axis=1, tiled=True)
-    partial_in, weight_part, sums = attention_backward(
-        q_x, k_t, k_wide, v_wide, mixed, row_stats, grad_t, rows, weight
-    )
-    from_heads = lax.psum_scatter(partial_in, "seq", scatter_dimension=0, tiled=True).astype(full)
-    grad_layer_in = grad_resid_one + from_heads
-    input_grad = jnp.where(is_memory, 0.0, grad_layer_in)
-    grad_memory = lax.dot_general(
-        picks, grad_layer_in, TN, precision=lax.Precision.HIGHEST, preferred_element_type=full
-    )
-    grad_memory = lax.psum(grad_memory.astype(low), "seq").astype(full)
-
-    sums = sums[:, 0]
-    own_sums = jnp.stack([sums[:head_cols], sums[2 * head_cols :]])[:, None]
-    zero_qv = jnp.zeros((2, seq_count, head_cols), full)
-    qv_grad = lax.dynamic_update_slice_in_dim(zero_qv, own_sums, seq_place, 1).reshape(-1)
     vector_grads = [
-        qv_grad, column_sums(grad_branch), grad_gain_one, grad_shift_one, column_sums(grad_up),
+        column_sums(grad_branch), grad_gain_one, grad_shift_one, column_sums(grad_up),
         column_sums(grad_down), grad_gain_two, grad_shift_two,
     ]
     packed_grad = jnp.concatenate([v.reshape(fsdp_count, -1) for v in vector_grads], axis=1)
-    packed_sum = lax.psum(packed_grad, ("fsdp", "seq"))
-    own_vectors = lax.dynamic_index_in_dim(packed_sum, lax.axis_index("fsdp"), 0, False)
+    saved = (q_x, k_t, k_wide, v_wide, mixed, row_stats)
+    if on_block:
+        packed_grad = jnp.pad(
+            packed_grad.reshape(fsdp_count, 5, head_cols), ((0, 0), (1, 10), (0, 0))
+        )
+        (input_grad, grad_read, grad_write, qkv_out, vector_sum, up_out, down_out, out_out) = back(
+            lengths, grad_attended, saved, packed_grad, rows, weight, grad_resid_one,
+            grad_up_weight.astype(low), grad_down_weight.astype(low), grad_out_weight.astype(low),
+        )
+        own_vectors = vector_sum[:6].reshape(-1)
+    else:
+        grad_t = lax.all_to_all(grad_attended, "seq", split_axis=0, concat_axis=1, tiled=True)
+        partial_in, weight_part, sums = attention_backward(*saved, grad_t, rows, weight)
+        from_heads = lax.psum_scatter(partial_in, "seq", scatter_dimension=0, tiled=True).astype(full)
+        grad_layer_in = grad_resid_one + from_heads
+        input_grad = jnp.where(is_memory, 0.0, grad_layer_in)
+        grad_memory = lax.dot_general(
+            picks, grad_layer_in, TN, precision=lax.Precision.HIGHEST, preferred_element_type=full
+        )
+        grad_memory = lax.psum(grad_memory.astype(low), "seq").astype(full)
+        grad_read, grad_write = grad_memory[:MEM], grad_memory[MEM:]
+        sums = sums[:, 0].reshape(heads, 3, HEAD)
+        own_sums = jnp.stack([sums[:, 0].reshape(-1), sums[:, 2].reshape(-1)])[:, None]
+        zero_qv = jnp.zeros((2, seq_count, head_cols), full)
+        qv_grad = lax.dynamic_update_slice_in_dim(zero_qv, own_sums, seq_place, 1)
+        packed_grad = jnp.concatenate([qv_grad.reshape(fsdp_count, -1), packed_grad], axis=1)
+        packed_sum = lax.psum(packed_grad, ("fsdp", "seq"))
+        own_vectors = lax.dynamic_index_in_dim(packed_sum, lax.axis_index("fsdp"), 0, False)
+
+        def both_axes(part):
+            piece = lax.psum_scatter(part.astype(low), "fsdp", scatter_dimension=0, tiled=True)
+            return lax.psum(piece, "seq").astype(full)
+
+        qkv_piece = lax.psum_scatter(weight_part, "fsdp", scatter_dimension=0, tiled=True)
+        qkv_parts = lax.all_gather(qkv_piece, "seq", axis=0).reshape(seq_count, shard, heads, 3, HEAD)
+        qkv_out = jnp.transpose(qkv_parts, (1, 3, 0, 2, 4)).reshape(shard, 3 * width).astype(full)
+        up_out, down_out, out_out = both_axes(grad_up_weight), both_axes(grad_down_weight), both_axes(grad_out_weight)
     vector_outs, start = [], 0
     for vector in vectors:
         vector_outs.append(own_vectors[start : start + vector.shape[0]])
         start += vector.shape[0]
     qv_out, out_b_out, gain_one_out, shift_one_out, up_b_out, down_b_out, gain_two_out, shift_two_out = vector_outs
-
-    def both_axes(part):
-        piece = lax.psum_scatter(part.astype(low), "fsdp", scatter_dimension=0, tiled=True)
-        return lax.psum(piece, "seq").astype(full)
-
-    qkv_piece = lax.psum_scatter(weight_part, "fsdp", scatter_dimension=0, tiled=True)
-    qkv_parts = lax.all_gather(qkv_piece, "seq", axis=0).reshape(seq_count, shard, 3, head_cols)
-    qkv_out = jnp.transpose(qkv_parts, (1, 2, 0, 3)).reshape(shard, 3 * width).astype(full)
     return (
-        output, input_grad, grad_memory[None, :MEM], grad_memory[None, MEM:], qkv_out, qv_out,
-        both_axes(grad_out_weight), out_b_out, gain_one_out, shift_one_out,
-        both_axes(grad_up_weight), up_b_out, both_axes(grad_down_weight), down_b_out,
-        gain_two_out, shift_two_out,
+        output, input_grad, grad_read[None], grad_write[None], qkv_out, qv_out, out_out, out_b_out, gain_one_out,
+        shift_one_out, up_out, up_b_out, down_out, down_b_out, gain_two_out, shift_two_out,
     )
 
 

time: 638 us -> 295 us (0.46)
  waiting for transfers between devices: 320 us -> 0 us
  Pallas kernels: 124 us -> 207 us
  blocking collectives: 79.2 us -> 0 us
  between operations: 15.3 us -> 1.79 us
  other arithmetic: 15.7 us -> 7.18 us
    reduce_scatter x5 -> x0, waiting for transfers between devices: 293 us -> none  [the longest x3 252 us: both_axes(): lax.psum_scatter(part.astype(low), 'fsdp', scatter_dimension=0, tiled=True)]
    pallas_call x1, Pallas kernels: 47.1 us -> 130 us  [back(): pl.pallas_call(back_kernel, in_specs=[pl.BlockSpec(memory_space=pltpu.SME...]
    psum x2 -> x0, blocking collectives: 55.7 us -> none  [the longest x1 44.5 us: per_device(): packed_sum = lax.psum(packed_grad, ('fsdp', 'seq'))]
    psum x1 -> x0, waiting for transfers between devices: 26.5 us -> none  [both_axes(): return lax.psum(piece, 'seq').astype(full)]
    all_to_all x1 -> x0, blocking collectives: 13.8 us -> none  [per_device(): lax.all_to_all(grad_attended, 'seq', split_axis=0, concat_axis=1, tiled=T...]
    unnamed x33 -> x46, local copies, waits for them, and re-layouts: 1.98 us -> 13.4 us
    all_gather x1 -> x0, blocking collectives: 9.65 us -> none  [per_device(): lax.all_gather(qkv_piece, 'seq', axis=0)]
  transfers between devices with their start and end apart: 6 -> 0, of which waited for: 6 -> 0; matrix products, arithmetic and copies ran while one was open for 5% -> 0% of each run, Pallas kernels for 0% -> 0%
where the time goes in v3:
time: 295 us; the launch traced here: 292 us
  Pallas kernels  207 us (70%)
  matrix products  51.3 us (17%)
  local copies, waits for them, and re-layouts  24.4 us (8%)
  other arithmetic  7.18 us (2%)
    pallas_call x1, Pallas kernels, back(): pl.pallas_call(back_kernel, in_specs=[pl.BlockSpec(memory_space=pltpu.SME...  130 us
    pallas_call x1, Pallas kernels, front(): pl.pallas_call(front_kernel, in_specs=[pl.BlockSpec(memory_space=pltpu.SM...  77.2 us
    dot_general x10, matrix products, mul(): return lax.dot_general(left, right, dims, preferred_element_type=full)  51.3 us
    unnamed x46, local copies, waits for them, and re-layouts  13.4 us

profile of v3, /device:TPU:9, one launch (start us, length us, event | category | flops | bytes accessed | tf_op | source)
XLA Modules:
  0.0 291.6 jit_solution(11234973026223963522)
XLA Ops:
  1.4 5.4 %concatenate.17 = bf16[1152]{0:T(1024)(128)(2,1)S(1)} concatenate(bf16[192]{0:T(256)(128)(2,1)} %param.22, bf16[96]{0:T(256)(128)(2,1)} %param.24, bf16[96]{0:T(256)(128)(2,1)} %param.25, bf16[96]{0:T(256)(128)(2,1)} %param.26, bf16[384]{0:T(512)(128)(2,1)} %param.28, bf16[96]{0:T(256)(128)(2,1)} %param.30, bf16[96]{0:T(256)(128)(2,1)} %param.31, bf16[96]{0:T(256)(128)(2,1)} %param.32), dimensions={0} | concatenate | bytes 4608 | tf_op jit(solution)/shard_map/concatenate | solution.py:1230
  7.0 1.3 copy.45
  8.6 0.8 maximum_maximum_fusion.qkv_in
  9.3 2.5 fusion.8.rows_in
  11.8 77.2 %front.1 = (bf16[2048,768]{1,0:T(8,128)(2,1)}, bf16[768,576]{1,0:T(8,128)(2,1)}, bf16[8,112,576]{2,1,0:T(8,128)(2,1)}, bf16[3,128,2048]{2,1,0:T(8,128)(2,1)}, bf...) custom-call(s32[1]{0:T(128)} %copy.55.length_ref, ...), custom_call_target="tpu_custom_call" | custom-call | tf_op jit(solution)/shard_map/front/pallas_call | solution.py:660
  88.9 0.9 slice_convert_fusion
  90.5 2.8 fusion.27
  93.7 18.5 %multiply_convert_fusion = (bf16[512,3072]{1,0:T(8,128)(2,1)S(1)}, f32[512,3072]{1,0:T(8,128)}, f32[512,3072]{1,0:T(8,128)}) fusion(f32[3072]{0:T(1024)S(1)} %add.122, bf16[768,3072]{1,0:T(8,128)(2,1)S(1)} %copy-done.9, f32[512,768]{1,0:T(8,128)S(1)} %get-tuple-element.157, f32[768]{0:T(1024)S(1)} %add.119, f32[768]{0:T(1024)S(1)} %mul.147, ...), kind=kOutput, calls=%fused_computation.4 | convolution fusion | flops 2521694208 | bytes 22042624 | tf_op jit(solution)/shard_map/dot_general | solution.py:27
  112.3 2.8 fusion.28
  115.4 0.8 multiply_reduce_fusion
  116.3 3.0 %fusion.23 = (f32[512]{0:T(512)S(1)}, f32[512,768]{1,0:T(8,128)S(1)}, bf16[512,768]{1,0:T(8,128)(2,1)}) fusion(f32[512]{0:T(512)S(1)} %multiply_multiply_fusion.6, f32[512,768]{1,0:T(8,128)S(1)} %get-tuple-element.160, f32[512]{0:T(512)S(1)} %broadcast_multiply_fusion, f32[512]{0:T(512)S(1)} %fusion.14, f32[768]{0:T(1024)S(1)} %mul.156, ...), kind=kLoop, calls=%fused_computation.74 | loop fusion | flops 5504512 | bytes 4733440 | tf_op jit(solution)/shard_map/transpose(jvp())/reduce_sum | solution.py:1194
  119.5 8.9 %convert_reduce_fusion = (f32[3072]{0:T(1024)S(1)}, bf16[512,3072]{1,0:T(8,128)(2,1)S(1)}) fusion(f32[512,3072]{1,0:T(8,128)} %get-tuple-element.139, f32[512,3072]{1,0:T(8,128)} %get-tuple-element.158, f32[3072]{0:T(1024)S(1)} %add.122, bf16[512,768]{1,0:T(8,128)(2,1)S(1)} %get-tuple-element.129, bf16[3072,768]{1,0:T(8,128)(2,1)} %get-tuple-element.41), kind=kOutput, calls=%fused_computation.2 | convolution fusion | flops 2442654720 | bytes 21258240 | tf_op jit(solution)/shard_map/dot_general | solution.py:27
  128.5 3.1 %multiply_reduce_fusion.1 = (f32[768]{0:T(1024)S(1)}, f32[512]{0:T(512)S(1)}, f32[768]{0:T(1024)S(1)}, f32[512,768]{1,0:T(8,128)S(1)}) fusion(f32[512,768]{1,0:T(8,128)S(1)} %get-tuple-element.157, f32[512]{0:T(512)S(1)} %fusion.13, f32[512]{0:T(512)S(1)} %broadcast_multiply_fusion.1, f32[768]{0:T(1024)S(1)} %mul.147, ...), kind=kOutput, calls=%fused_computation.24 | convolution fusion | flops 2419849216 | bytes 12600320 | tf_op jit(solution)/shard_map/dot_general | solution.py:27
  131.9 0.6 fusion.22
  132.5 1.3 copy-done.12
  133.8 4.8 %convolution_convert_fusion.1.up_given = bf16[768,3072]{1,0:T(8,128)(2,1)} fusion(bf16[512,3072]{1,0:T(8,128)(2,1)S(1)} %copy-done.12, f32[512,768]{1,0:T(8,128)S(1)} %get-tuple-element.157, f32[768]{0:T(1024)S(1)} %add.119, f32[768]{0:T(1024)S(1)} %mul.147, f32[512]{0:T(512)S(1)} %fusion.13, f32[512]{0:T(512)S(1)} %broadcast_multiply_fusion.1), kind=kOutput, calls=%fused_computation.19 | convolution fusion | flops 2420244480 | bytes 9447424 | tf_op jit(solution)/shard_map/dot_general | solution.py:27
  138.8 1.4 copy-done.10
  140.2 1.7 convolution_convert_fusion.3.grad_own
  142.2 0.7 pad.4.vectors_in
  142.8 1.8 convolution_convert_fusion.2.out_given
  144.7 4.4 %convolution_convert_fusion.down_given = bf16[3072,768]{1,0:T(8,128)(2,1)} fusion(bf16[512,3072]{1,0:T(8,128)(2,1)S(1)} %copy-done.14, bf16[512,768]{1,0:T(8,128)(2,1)S(1)} %copy-done.7), kind=kOutput, calls=%fused_computation.18 | convolution fusion | flops 2418278400 | bytes 8650752 | tf_op jit(solution)/shard_map/dot_general | solution.py:27
  149.0 129.7 %back.1 = (f32[512,768]{1,0:T(8,128)}, f32[10,768]{1,0:T(8,128)}, f32[10,768]{1,0:T(8,128)}, f32[96,2304]{1,0:T(8,128)}, f32[16,192]{1,0:T(8,128)}, /*index=5*/f...) custom-call(s32[1]{0:T(128)} %copy.55.length_ref, bf16[768,512]{1,0:T(8,128)(2,1)} %convolution_convert_fusion.3.grad_own, ...), custom_call_target="tpu_custom_call" | custom-call | tf_op jit(solution)/shard_map/back/pallas_call | solution.py:1151
  278.7 1.6 copy.48
  280.3 1.3 slice.63
  281.6 0.7 slice.65
  282.4 0.7 slice.83
  283.6 1.4 copy.49
  285.1 2.7 copy.56
  287.7 0.9 copy.57
  288.6 0.7 copy.58
  289.3 1.0 copy.59
  290.4 1.0 copy.60
  (81 shorter events, 3.6 us)
Async XLA Ops:
  90.5 3.2 %copy-start.9 = (bf16[768,3072]{1,0:T(8,128)(2,1)S(1)}, bf16[768,3072]{1,0:T(8,128)(2,1)}, u32[]{:S(2)}) copy-start(bf16[768,3072]{1,0:T(8,128)(2,1)} %get-tuple-element.40) | copy-start | bytes 14155780
  90.5 21.7 %slice-start.2 = ((s8[4718592]{0:T(1024)(128)(4,1)}), s8[4194304]{0:T(1024)(128)(4,1)S(1)}, s32[]{:S(2)}) async-start(s8[4718592]{0:T(1024)(128)(4,1)} %bitcast.37), calls=%async_computation.2 | async-start | bytes 8388608
  93.7 18.5 %slice-start.3 = ((s8[4718592]{0:T(1024)(128)(4,1)}), s8[524288]{0:T(1024)(128)(4,1)S(1)}, s32[]{:S(2)}) async-start(s8[4718592]{0:T(1024)(128)(4,1)} %bitcast.37), calls=%async_computation.3 | async-start | bytes 1048576
  112.2 2.8 copy-start.13
  112.3 3.1 %copy-start.1 = (bf16[512,768]{1,0:T(8,128)(2,1)S(1)}, bf16[512,768]{1,0:T(8,128)(2,1)}, u32[]{:S(2)}) copy-start(bf16[512,768]{1,0:T(8,128)(2,1)} %param.33) | copy-start | bytes 2359300
  116.3 12.2 %slice-start = ((s8[4718592]{0:T(1024)(128)(4,1)}), s8[4194304]{0:T(1024)(128)(4,1)S(1)}, s32[]{:S(2)}) async-start(s8[4718592]{0:T(1024)(128)(4,1)} %bitcast.35), calls=%async_computation | async-start | bytes 8388608
  119.5 9.0 %copy-start.6 = (bf16[512,768]{1,0:T(8,128)(2,1)}, bf16[512,768]{1,0:T(8,128)(2,1)S(1)}, u32[]{:S(2)}) copy-start(bf16[512,768]{1,0:T(8,128)(2,1)S(1)} %get-tuple-element.129) | copy-start | bytes 2359300
  119.5 9.0 %slice-start.1 = ((s8[4718592]{0:T(1024)(128)(4,1)}), s8[524288]{0:T(1024)(128)(4,1)S(1)}, s32[]{:S(2)}) async-start(s8[4718592]{0:T(1024)(128)(4,1)} %bitcast.35), calls=%async_computation.1 | async-start | bytes 1048576
  128.5 3.2 %copy-start.11 = (bf16[512,3072]{1,0:T(8,128)(2,1)}, bf16[512,3072]{1,0:T(8,128)(2,1)S(1)}, u32[]{:S(2)}) copy-start(bf16[512,3072]{1,0:T(8,128)(2,1)S(1)} %get-tuple-element.131) | copy-start | bytes 9437188
  131.9 1.9 copy-start.12
  138.6 1.6 copy-start.10
  138.6 4.3 %copy-start.5 = (bf16[768,512]{1,0:T(8,128)(2,1)S(1)}, bf16[768,512]{1,0:T(8,128)(2,1)}, u32[]{:S(2)}) copy-start(bf16[768,512]{1,0:T(8,128)(2,1)} %get-tuple-element.37) | copy-start | bytes 2359300
  138.8 5.8 %copy-start = (f32[512,768]{1,0:T(8,128)}, f32[512,768]{1,0:T(8,128)S(1)}, u32[]{:S(2)}) copy-start(f32[512,768]{1,0:T(8,128)S(1)} %get-tuple-element.133.resid_in) | copy-start | bytes 4718596
  140.2 4.5 %copy-start.7 = (bf16[512,768]{1,0:T(8,128)(2,1)S(1)}, bf16[512,768]{1,0:T(8,128)(2,1)}, u32[]{:S(2)}) copy-start(bf16[512,768]{1,0:T(8,128)(2,1)} %copy-done.6) | copy-start | bytes 2359300
  142.2 2.5 copy-start.14
  278.7 9.0 %copy-start.4 = (f32[96,2304]{1,0:T(8,128)S(1)}, f32[96,2304]{1,0:T(8,128)}, u32[]{:S(2)}) copy-start(f32[96,2304]{1,0:T(8,128)} %get-tuple-element.182) | copy-start | bytes 2654212
  278.7 9.9 %copy-start.8 = (f32[96,768]{1,0:T(8,128)S(1)}, f32[96,768]{1,0:T(8,128)}, u32[]{:S(2)}) copy-start(f32[96,768]{1,0:T(8,128)} %get-tuple-element.184) | copy-start | bytes 884740
  278.7 10.6 %copy-start.3 = (f32[96,3072]{1,0:T(8,128)S(1)}, f32[96,3072]{1,0:T(8,128)}, u32[]{:S(2)}) copy-start(f32[96,3072]{1,0:T(8,128)} %get-tuple-element.188) | copy-start | bytes 3538948
  287.7 2.6 copy-start.2

commit v4 on v3

--- a/solution.py
+++ b/solution.py
@@ -699,27 +699,14 @@
 
 
 class Reduce:
-    def __init__(self, place, given, mine, sums, from_y, from_x, from_z, sems):
-        self.place, self.given, self.mine, self.sums = place, given, mine, sums
+    def __init__(self, place, given, sums, from_y, from_x, from_z, sems):
+        self.place, self.given, self.sums = place, given, sums
         self.from_y, self.from_x, self.from_z = from_y, from_x, from_z
-        (self.c_send, self.c_recv, self.y_send, self.y_recv, self.x_send, self.x_recv, self.z_send,
-         self.z_recv) = sems
+        self.y_send, self.y_recv, self.x_send, self.x_recv, self.z_send, self.z_recv = sems
 
     def dest(self, column, line):
         x = self.place.x
         return 2 * line + (x if column == 0 else 1 - x)
-
-    def part_of(self, ref, array, column, line, core, far):
-        dest = self.dest(column, line)
-        if array == DOWN_W:
-            rows = ref.shape[0] // 8
-            part = rows // 4
-            y = self.place.y if not far else 1 - self.place.y
-            return ref.at[pl.ds(pl.multiple_of(dest * rows + (2 * y + core) * part, part), part)]
-        rows, columns = ref.shape[0] // 8, ref.shape[1] // 2
-        return ref.at[
-            pl.ds(pl.multiple_of(dest * rows, rows), rows), pl.ds(pl.multiple_of(core * columns, columns), columns)
-        ]
 
     def slot(self, array, column, line, far=0):
         if array >= DW_FIRST:
@@ -728,29 +715,15 @@
             return self.sums[array].at[column, line, far]
         return self.sums[array].at[column, line]
 
-    def load_mine(self, array, column, line, far, sem):
-        target = self.mine[array].at[column, line, far] if array == DOWN_W else self.mine[array].at[column, line]
-        return pltpu.make_async_copy(
-            self.part_of(self.given[array], array, column, line, self.place.c, far), target, sem
-        )
-
-    def to_core(self, array, column, line, far=0):
-        index = array + far
-        return remote(
-            self.part_of(self.given[array], array, column, line, 1 - self.place.c, far),
-            self.slot(array, column, line, far),
-            self.c_send.at[index, column, line], self.c_recv.at[index, column, line], self.place.core,
-        )
-
-    def add_core(self, array, column, line, far=0):
-        self.to_core(array, column, line, far).wait_recv()
-        slot = self.slot(array, column, line, far)
-        own = self.mine[array].at[column, line, far] if array == DOWN_W else self.mine[array].at[column, line]
-        slot[...] = add_low(slot[...], own[...])
+    def load(self, array, column, line, sem):
+        target, source = self.sums[array].at[column, line], self.given[array].at[column, line]
+        if array == DOWN_W:
+            target, source = target.at[0], source.at[0]
+        return pltpu.make_async_copy(source, target, sem)
 
     def over_y(self, column, line):
         return remote(
-            self.slot(DOWN_W, column, line, 1), self.from_y.at[column, line],
+            self.given[DOWN_W].at[column, line, 1], self.from_y.at[column, line],
             self.y_send.at[column, line], self.y_recv.at[column, line], self.place.across_y,
         )
 
@@ -760,8 +733,9 @@
         slot[...] = add_low(slot[...], self.from_y[column, line])
 
     def over_x(self, array, line):
+        start = self.given[array].at[1, line] if array in (UP_W, OUT_W) else self.slot(array, 1, line)
         return remote(
-            self.slot(array, 1, line), self.from_x[array].at[line],
+            start, self.from_x[array].at[line],
             self.x_send.at[array, line], self.x_recv.at[array, line], self.place.across_x,
         )
 
@@ -782,20 +756,22 @@
         slot = self.slot(array, 0, line)
         slot[...] = add_low(slot[...], self.from_z[array][way, line])
 
-    def hop(self, array, level):
+    def hop(self, array, level, lines=(0, 1, 2, 3)):
         @pl.when(self.place.z == level)
         def _():
             for line in range(3, level, -1):
-                if level > 0:
-                    self.add_z(array, 0, line)
-                self.along_z(array, 0, line).start()
+                if line in lines:
+                    if level > 0:
+                        self.add_z(array, 0, line)
+                    self.along_z(array, 0, line).start()
 
         @pl.when(self.place.z == 3 - level)
         def _():
             for line in range(0, 3 - level):
-                if level > 0:
-                    self.add_z(array, 1, line)
-                self.along_z(array, 1, line).start()
+                if line in lines:
+                    if level > 0:
+                        self.add_z(array, 1, line)
+                    self.along_z(array, 1, line).start()
 
     def settle(self, array):
         for line in range(4):
@@ -812,40 +788,68 @@
             self.over_x(array, line).wait_send()
             pl.when(self.place.z < line)(lambda line=line: self.along_z(array, 0, line).wait_send())
             pl.when(self.place.z > line)(lambda line=line: self.along_z(array, 1, line).wait_send())
-            if array >= DW_FIRST:
-                continue
-            for column in range(2):
-                for far in range(2 if array == DOWN_W else 1):
-                    self.to_core(array, column, line, far).wait_send()
-                if array == DOWN_W:
+            if array == DOWN_W:
+                for column in range(2):
                     self.over_y(column, line).wait_send()
 
 
+class Spread:
+    def __init__(self, place, blocks, source, send, recv):
+        self.place, self.blocks, self.source, self.send, self.recv = place, blocks, source, send, recv
+        self.near = 2 * place.y + 1 - place.c
+        self.far = 2 * (1 - place.y) + place.c
+        self.last = 2 * (1 - place.y) + 1 - place.c
+
+    def copy(self, kind, arriving=False):
+        place = self.place
+        if kind == 2:
+            here = self.blocks.at[self.last if arriving else self.far]
+            return remote(here, here, self.send.at[2], self.recv.at[2], place.core)
+        member = (self.near, self.far)[kind] if arriving else place.s
+        return remote(
+            self.source, self.blocks.at[member], self.send.at[kind], self.recv.at[kind],
+            (place.core, place.across_y)[kind],
+        )
+
+    def start(self):
+        self.copy(1).start()
+        self.copy(0).start()
+
+    def pass_on(self):
+        self.copy(1, True).wait_recv()
+        self.copy(2).start()
+
+    def finish(self):
+        self.blocks[self.place.s] = self.source[...]
+        self.copy(0, True).wait_recv()
+        self.copy(2, True).wait_recv()
+        for kind in range(3):
+            self.copy(kind).wait_send()
+
+
 def back_kernel(
-    length_ref, grad_own, q_x, k_t, k_wide, v_wide, mixed, row_stats, vectors_in,
-    rows_in, weight_in, resid_in, up_given, down_given, out_given,
+    length_ref, grad_own, vectors_in, q_in, k_in, k_wide_in, v_wide_in, mixed_in, stats_in, rows_in, weight_in, resid_in, up_given, down_given, out_given,
     input_out, read_out, write_out, qkv_out, vector_out, up_out, down_out, out_out,
-    grad_t, q_here, do_x, grads, grad_k, grad_v, rows_ref, weight_ref, resid_ref, up_mine, out_mine, down_mine,
+    q_x, k_t, k_wide, v_wide, mixed, row_stats, grad_t, q_here, do_x, grads, grad_k, grad_v, rows_ref, weight_ref, resid_ref,
     up_sum, out_sum, down_sum, dw, down_y, up_x, out_x, down_x, dw_x, up_z, out_z, down_z, dw_z,
     up_last, out_last, up_other, out_other, down_all, dw_all,
-    near_send, near_recv, near_own, far_sum, far_recv, memory_all,
-    mix_send, mix_recv, local_sem, mine_sem, share_send, share_recv, near_s, near_r, far_s, far_r, memory_s,
-    memory_r, *sems,
+    near_send, near_recv, far_sum, far_recv, memory_all, memory_own,
+    mix_send, mix_recv, local_sem, saved_sem, mine_sem, share_send, share_recv, near_s, near_r, far_s, far_r,
+    *sems,
 ):
     place = Place()
-    heads, _, slot_rows = q_x.shape
+    heads, _, slot_rows = q_in.shape
     width, local_rows = grad_own.shape
     head_cols = heads * HEAD
     last = DW_FIRST + heads - 1
     given = {UP_W: up_given, OUT_W: out_given, DOWN_W: down_given}
-    mine = {UP_W: up_mine, OUT_W: out_mine, DOWN_W: down_mine}
     sums = {UP_W: up_sum, OUT_W: out_sum, DOWN_W: down_sum}
     from_x = {UP_W: up_x, OUT_W: out_x, DOWN_W: down_x}
     from_z = {UP_W: up_z, OUT_W: out_z, DOWN_W: down_z}
     for h in range(heads):
         sums[DW_FIRST + h], from_x[DW_FIRST + h] = dw.at[h], dw_x.at[h]
         from_z[DW_FIRST + h] = dw_z.at[h]
-    reduce = Reduce(place, given, mine, sums, down_y, from_x, from_z, sems)
+    reduce = Reduce(place, given, sums, down_y, from_x, from_z, sems)
     greet(place, None)
 
     peers = (place.across_y, place.diagonal, place.core)
@@ -862,36 +866,52 @@
             src, grad_t.at[:, lanes if arriving else own_lanes], mix_send.at[turn], mix_recv.at[turn], peers[turn]
         )
 
+    def saved_loads(h):
+        own = pl.ds(h * HEAD, HEAD)
+        pairs = (
+            (k_wide_in.at[h], k_wide.at[h]), (q_in.at[h, pl.ds(0, HEAD)], q_x.at[h]), (v_wide_in.at[h], v_wide.at[h]),
+            (mixed_in.at[own], mixed.at[own]), (stats_in.at[h], row_stats.at[h]), (k_in.at[own], k_t.at[own]),
+        )
+        return [pltpu.make_async_copy(src, dst, saved_sem.at[h, i]) for i, (src, dst) in enumerate(pairs)]
+
     for turn in range(3):
         send_grad(turn).start()
+    for load in saved_loads(0):
+        load.start()
     loads = []
     for index, (src, dst) in enumerate(((rows_in, rows_ref), (weight_in, weight_ref), (resid_in, resid_ref))):
         loads.append(pltpu.make_async_copy(src, dst, local_sem.at[index]))
-    order = (
-        (UP_W, 1, 0), (DOWN_W, 1, 1), (DOWN_W, 0, 1), (UP_W, 0, 0), (OUT_W, 1, 0), (OUT_W, 0, 0), (DOWN_W, 1, 0),
-        (DOWN_W, 0, 0),
-    )
-    for array, column, far in order:
+
+    def sum_loads(array):
+        columns = (0, 1) if array == DOWN_W else (0,)
+        return [
+            reduce.load(array, column, line, mine_sem.at[array, column, line]) for column in columns for line in LINES
+        ]
+
+    def send_x(array, lines=LINES):
+        for line in lines:
+            reduce.over_x(array, line).start()
+
+    send_x(UP_W)
+    for column in (1, 0):
         for line in LINES:
-            reduce.to_core(array, column, line, far).start()
-            reduce.load_mine(array, column, line, far, mine_sem.at[array + far, column, line]).start()
+            reduce.over_y(column, line).start()
+    send_x(OUT_W)
+    for array in (UP_W, DOWN_W, OUT_W):
+        for load in sum_loads(array):
+            load.start()
     for load in loads:
         load.start()
 
-    def gather_core(array, column, far=0):
-        for line in LINES:
-            reduce.load_mine(array, column, line, far, mine_sem.at[array + far, column, line]).wait()
-            reduce.add_core(array, column, line, far)
+    for h in range(1, heads):
+        for load in saved_loads(h):
+            load.start()
 
     own_lanes = pl.ds(pl.multiple_of(place.s * local_rows, local_rows), local_rows)
     grad_t[:, own_lanes] = grad_own[pl.ds(pl.multiple_of(place.s * head_cols, head_cols), head_cols), :]
 
-    def send_x(array):
-        for line in LINES:
-            reduce.over_x(array, line).start()
-
-    def take_x(array):
-        for line in LINES:
+    def take_x(array, lines=LINES):
+        for line in lines:
             reduce.add_x(array, line)
 
     turns = slot_rows // local_rows
@@ -919,52 +939,85 @@
                     ].astype(low)
         send_x(DW_FIRST + h)
 
+    share = {UP_W: (up_last, up_other), OUT_W: (out_last, out_other)}
+
+    def sum_y(array):
+        mine_now = sums[array].at[0, place.z]
+        return remote(mine_now, share[array][0], share_send.at[array, 0], share_recv.at[array, 0], place.across_y)
+
+    def half_to_core(array):
+        mine_now = sums[array].at[0, place.z]
+        return remote(mine_now, share[array][1], share_send.at[array, 1], share_recv.at[array, 1], place.core)
+
+    def spread_of(array):
+        if array == DOWN_W:
+            return Spread(place, down_all, down_sum.at[0, place.z, 0], share_send.at[2], share_recv.at[2])
+        h = array - DW_FIRST
+        return Spread(place, dw_all.at[h], dw.at[h, place.f], share_send.at[array], share_recv.at[array])
+
+    def add_last(array):
+        sum_y(array).wait()
+        slot = sums[array].at[0, place.z]
+        slot[...] = add_low(slot[...], share[array][0][...])
+        half_to_core(array).start()
+
+    first, second = DW_FIRST, DW_FIRST + 1
+
+    def add_y(column):
+        for line in LINES:
+            reduce.add_y(column, line)
+
     def chores(index):
         if index == 1:
             send_grad(2, True).wait_recv()
-            gather_core(UP_W, 1)
-            send_x(UP_W)
         elif index == 2:
             send_grad(1, True).wait_recv()
-            for column in (1, 0):
-                gather_core(DOWN_W, column, 1)
-                for line in LINES:
-                    reduce.over_y(column, line).start()
+            for array in (UP_W, DOWN_W, OUT_W):
+                for load in sum_loads(array):
+                    load.wait()
         elif index == 3:
             send_grad(0, True).wait_recv()
-            gather_core(OUT_W, 1)
-            send_x(OUT_W)
-            gather_core(OUT_W, 0)
+            take_x(UP_W, (3,))
+            reduce.hop(UP_W, 0, (3,))
         elif index == 4:
+            for load in saved_loads(1):
+                load.wait()
             weight_part(0)
-            gather_core(UP_W, 0)
+            take_x(UP_W, (0,))
+            reduce.hop(UP_W, 0, (0,))
         elif index == 5:
-            gather_core(DOWN_W, 1)
-            gather_core(DOWN_W, 0)
+            add_y(1)
+            send_x(DOWN_W)
+            take_x(UP_W, (2,))
+            reduce.hop(UP_W, 0, (2,))
         elif index == 6:
-            for line in LINES:
-                reduce.add_y(1, line)
-            send_x(DOWN_W)
+            reduce.hop(UP_W, 1, (3, 0))
+            take_x(UP_W, (1,))
+            reduce.hop(UP_W, 0, (1,))
         elif index == 7:
-            take_x(UP_W)
-            reduce.hop(UP_W, 0)
-        elif index == 8:
-            weight_part(1)
             take_x(OUT_W)
             reduce.hop(OUT_W, 0)
-            take_x(DW_FIRST)
-            reduce.hop(DW_FIRST, 0)
+            reduce.hop(UP_W, 1, (2, 1))
+        elif index == 8:
+            for load in saved_loads(2):
+                load.wait()
+            weight_part(1)
+            reduce.hop(UP_W, 2)
+            add_y(0)
         elif index == 9:
-            for line in LINES:
-                reduce.add_y(0, line)
+            take_x(DOWN_W, (3, 0))
+            reduce.hop(DOWN_W, 0, (3, 0))
+            reduce.hop(OUT_W, 1)
         elif index == 10:
-            reduce.hop(UP_W, 1)
-            reduce.hop(DW_FIRST, 1)
+            reduce.settle(UP_W)
+            sum_y(UP_W).start()
+            take_x(DOWN_W, (2, 1))
+            reduce.hop(DOWN_W, 0, (2, 1))
         elif index == 11:
-            take_x(DOWN_W)
-            reduce.hop(DOWN_W, 0)
-            reduce.hop(OUT_W, 1)
-            reduce.hop(DW_FIRST, 2)
+            reduce.hop(OUT_W, 2)
+            reduce.hop(DOWN_W, 1)
+            take_x(first)
+            reduce.hop(first, 0)
 
     def step(index, carry):
         for when in range(1, 12):
@@ -983,160 +1036,133 @@
 
         return carry
 
+    for load in saved_loads(0):
+        load.wait()
     lax.fori_loop(0, heads * turns, step, 0)
 
     weight_part(heads - 1)
     loads[1].wait()
-
-    def part_for(turn):
-        _, lanes = member_rows(turn)
-        return mul(grads[:, lanes], weight_ref[...], TT)
-
-    def share_near(index):
+    loads[2].wait()
+
+    halves, part = 2, local_rows // 2
+    length = length_ref[0]
+
+    def memory_pick(rows, start):
+        line = lax.broadcasted_iota(jnp.int32, (32, rows), 0)
+        row = start + lax.broadcasted_iota(jnp.int32, (32, rows), 1)
+        wanted = jnp.where(line < 16, line, length - MEM + line - 16)
+        used = (line < MEM) | ((line >= 16) & (line < 16 + MEM))
+        return jnp.where(used & (wanted == row), 1.0, 0.0).astype(low)
+
+    def part_for(turn, half):
+        start = pl.multiple_of(place.member(turn) * local_rows + half * part, part)
+        return mul(grads[:, pl.ds(start, part)], weight_ref[...], TT)
+
+    def share_near(index, half):
+        rows = pl.ds(half * part, part)
         return remote(
-            near_send.at[index], near_recv.at[index], near_s.at[index], near_r.at[index], place.core
-        )
-
-    def share_far():
-        return remote(far_sum, far_recv, far_s.at[0], far_r.at[0], place.across_y)
-
-    near_send[0] = part_for(1).astype(low)
-    share_near(0).start()
-    near_own[...] = part_for(0).astype(low)
-    share_near(0).wait_recv()
-    far_sum[...] = add_low(near_own[...], near_recv[0])
-    share_far().start()
+            near_send.at[index, rows], near_recv.at[index, rows], near_s.at[index, half], near_r.at[index, half],
+            place.core,
+        )
+
+    def share_far(half):
+        rows = pl.ds(half * part, part)
+        return remote(far_sum.at[rows], far_recv.at[rows], far_s.at[half], far_r.at[half], place.across_y)
+
+    for half in range(halves):
+        rows = slice(half * part, (half + 1) * part)
+        near_send[0, rows, :] = part_for(1, half).astype(low)
+        share_near(0, half).start()
+        far_sum[rows, :] = part_for(0, half).astype(low)
+        if half == 0:
+            taken = mul(memory_pick(slot_rows, 0), grads[...], NT).astype(low)
+            own_part = mul(memory_pick(local_rows, place.s * local_rows), resid_ref[...].astype(low))
+            memory_own[...] = (mul(taken, weight_ref[...], NT) + own_part).astype(low)
+        share_near(0, half).wait_recv()
+        far_sum[rows, :] = add_low(far_sum[rows, :], near_recv[0, rows, :])
+        share_far(half).start()
+    memory = Spread(place, memory_all, memory_own, share_send.at[DW_FIRST + heads], share_recv.at[DW_FIRST + heads])
+    memory.start()
+    take_x(second)
+    reduce.hop(second, 0)
     take_x(last)
     reduce.hop(last, 0)
-    near_send[1] = part_for(2).astype(low)
-    share_near(1).start()
-    take_x(last - 1)
-    reduce.hop(last - 1, 0)
-    loads[2].wait()
-    resid_ref[...] += part_for(3)
+    reduce.hop(first, 1)
+    for half in range(halves):
+        rows = slice(half * part, (half + 1) * part)
+        near_send[1, rows, :] = part_for(2, half).astype(low)
+        share_near(1, half).start()
     reduce.hop(last, 1)
-    reduce.hop(last - 1, 1)
-    reduce.hop(UP_W, 2)
-    reduce.hop(OUT_W, 2)
-    reduce.hop(DOWN_W, 1)
+    reduce.hop(second, 1)
+    reduce.hop(DOWN_W, 2)
+    reduce.hop(first, 2)
+    for half in range(halves):
+        resid_ref[half * part : (half + 1) * part, :] += part_for(3, half)
     reduce.hop(last, 2)
-    reduce.hop(last - 1, 2)
-    reduce.hop(DOWN_W, 2)
-
-    share = {UP_W: (up_last, up_other), OUT_W: (out_last, out_other)}
-
-    def sum_y(array):
-        mine_now = sums[array].at[0, place.z]
-        return remote(mine_now, share[array][0], share_send.at[array, 0], share_recv.at[array, 0], place.across_y)
-
-    def half_to_core(array):
-        mine_now = sums[array].at[0, place.z]
-        return remote(mine_now, share[array][1], share_send.at[array, 1], share_recv.at[array, 1], place.core)
-
-    def quarter_to(turn, arriving=False):
-        member = place.member(turn) if arriving else place.s
-        return remote(
-            down_sum.at[0, place.z, 0], down_all.at[member], share_send.at[2, turn], share_recv.at[2, turn], peers[turn]
-        )
-
-    def dw_to(h, turn, arriving=False):
-        member = place.member(turn) if arriving else place.s
-        return remote(
-            dw.at[h, place.f], dw_all.at[h, member], share_send.at[DW_FIRST + h, turn],
-            share_recv.at[DW_FIRST + h, turn], peers[turn],
-        )
-
-    reduce.settle(UP_W)
-    sum_y(UP_W).start()
+    reduce.hop(second, 2)
     reduce.settle(OUT_W)
     sum_y(OUT_W).start()
-    for h in range(heads):
+    for h in (heads - 1, 0, 1):
         reduce.settle(DW_FIRST + h)
-        for turn in range(3):
-            dw_to(h, turn).start()
+        spread_of(DW_FIRST + h).start()
     reduce.settle(DOWN_W)
-    for turn in range(3):
-        quarter_to(turn).start()
-    for array in (UP_W, OUT_W):
-        sum_y(array).wait()
-        slot = sums[array].at[0, place.z]
-        slot[...] = add_low(slot[...], share[array][0][...])
-        half_to_core(array).start()
-
-    share_near(1).wait_recv()
-    share_far().wait_recv()
-    grad_layer = resid_ref[...] + near_recv[1].astype(full) + far_recv[...].astype(full)
-    length = length_ref[0]
-    rows_at = place.s * local_rows + lax.broadcasted_iota(jnp.int32, (local_rows, 1), 0)
-    in_read = rows_at < MEM
-    in_write = (rows_at >= length - MEM) & (rows_at < length)
-    input_out[...] = jnp.where(in_read | in_write, 0.0, grad_layer)
-    line_at = lax.broadcasted_iota(jnp.int32, (32, local_rows), 0)
-    row_at = place.s * local_rows + lax.broadcasted_iota(jnp.int32, (32, local_rows), 1)
-    wanted = jnp.where(line_at < 16, line_at, length - MEM + line_at - 16)
-    used = (line_at < MEM) | ((line_at >= 16) & (line_at < 16 + MEM))
-    pick = jnp.where(used & (wanted == row_at), 1.0, 0.0).astype(low)
-    memory_all[place.s] = mul(pick, grad_layer.astype(low)).astype(low)
-
-    def memory_to(turn, arriving=False):
-        member = place.member(turn) if arriving else place.s
-        return remote(
-            memory_all.at[place.s], memory_all.at[member], memory_s.at[turn], memory_r.at[turn], peers[turn]
-        )
-
-    for turn in range(3):
-        memory_to(turn).start()
-
+    spread_of(DOWN_W).start()
+    add_last(UP_W)
+    add_last(OUT_W)
+    memory.pass_on()
+    for h in (heads - 1, 0, 1):
+        spread_of(DW_FIRST + h).pass_on()
+    spread_of(DOWN_W).pass_on()
     for array, out in ((UP_W, up_out), (OUT_W, out_out)):
         columns = out.shape[1] // 2
-        out[:, pl.ds(pl.multiple_of(place.c * columns, columns), columns)] = sums[array][0, place.z].astype(full)
+        out[:, pl.ds(pl.multiple_of(place.c * columns, columns), columns)] = sums[array][0, place.z]
         half_to_core(array).wait()
-        out[:, pl.ds(pl.multiple_of((1 - place.c) * columns, columns), columns)] = share[array][1][...].astype(full)
-    down_all[place.s] = down_sum[0, place.z, 0]
-    for turn in range(3):
-        quarter_to(turn).wait_send()
-        quarter_to(turn, True).wait_recv()
+        out[:, pl.ds(pl.multiple_of((1 - place.c) * columns, columns), columns)] = share[array][1][...]
+    for h in range(heads):
+        spread_of(DW_FIRST + h).finish()
+    spread_of(DOWN_W).finish()
     quarter = down_out.shape[0] // 4
     for member in range(4):
-        down_out[member * quarter : (member + 1) * quarter, :] = down_all[member].astype(full)
+        down_out[member * quarter : (member + 1) * quarter, :] = down_all[member]
     shard = qkv_out.shape[0]
-    for h in range(heads):
-        dw_all[h, place.s] = dw[h, place.f]
-        for turn in range(3):
-            dw_to(h, turn).wait_send()
-            dw_to(h, turn, True).wait_recv()
+    for kind in range(3):
         for member in range(4):
-            for kind in range(3):
+            for h in range(heads):
                 start = kind * width + (member * heads + h) * HEAD
-                qkv_out[:, start : start + HEAD] = dw_all[
-                    h, member, :shard, kind * HEAD : (kind + 1) * HEAD
-                ].astype(full)
+                qkv_out[:, start : start + HEAD] = dw_all[h, member, :shard, kind * HEAD : (kind + 1) * HEAD]
     vector_sum = dw_all[heads - 1, 0, shard:, :].astype(full)
     for member in range(1, 4):
         vector_sum = vector_sum + dw_all[heads - 1, member, shard:, :].astype(full)
     vector_out[...] = vector_sum
-    for turn in range(3):
-        memory_to(turn).wait_send()
-        memory_to(turn, True).wait_recv()
-    memory = memory_all[0].astype(full)
+    memory.finish()
+    total = memory_all[0].astype(full)
     for member in range(1, 4):
-        memory = memory + memory_all[member].astype(full)
-    read_out[...] = memory[:MEM]
-    write_out[...] = memory[16 : 16 + MEM]
+        total = total + memory_all[member].astype(full)
+    read_out[...] = total[:MEM]
+    write_out[...] = total[16 : 16 + MEM]
+    for half in range(halves):
+        rows = slice(half * part, (half + 1) * part)
+        share_near(1, half).wait_recv()
+        share_far(half).wait_recv()
+        grad_layer = resid_ref[rows, :] + near_recv[1, rows, :].astype(full) + far_recv[rows, :].astype(full)
+        rows_at = place.s * local_rows + half * part + lax.broadcasted_iota(jnp.int32, (part, 1), 0)
+        in_write = (rows_at >= length - MEM) & (rows_at < length)
+        input_out[rows, :] = jnp.where((rows_at < MEM) | in_write, 0.0, grad_layer)
     for array in range(DW_FIRST + heads):
         reduce.finish(array)
     for turn in range(3):
         send_grad(turn).wait_send()
-    for index in range(2):
-        share_near(index).wait_send()
-    share_far().wait_send()
+    for half in range(halves):
+        for index in range(2):
+            share_near(index, half).wait_send()
+        share_far(half).wait_send()
 
 
 def back(lengths, grad_own, saved, vectors, rows, weight, resid, up_given, down_given, out_given):
     q_x, k_t, k_wide, v_wide, mixed, row_stats = saved
     heads, _, slot_rows = q_x.shape
     width, local_rows = grad_own.shape
-    hidden = up_given.shape[1]
+    hidden = 2 * up_given.shape[3]
     shard, head_cols = width // 8, heads * HEAD
     half, small, piece = hidden // 2, width // 2, hidden // 32
     vmem = pl.BlockSpec(memory_space=pltpu.VMEM)
@@ -1150,23 +1176,24 @@
     tall = (shard + 16, 3 * HEAD)
     return pl.pallas_call(
         back_kernel,
-        in_specs=[pl.BlockSpec(memory_space=pltpu.SMEM)] + [vmem] * 8 + [anywhere] * 6,
+        in_specs=[pl.BlockSpec(memory_space=pltpu.SMEM)] + [vmem] * 2 + [anywhere] * 12,
         out_specs=[vmem] * 8,
         out_shape=[
             jax.ShapeDtypeStruct((local_rows, width), full),
             jax.ShapeDtypeStruct((MEM, width), full),
             jax.ShapeDtypeStruct((MEM, width), full),
-            jax.ShapeDtypeStruct((shard, 3 * width), full),
+            jax.ShapeDtypeStruct((shard, 3 * width), low),
             jax.ShapeDtypeStruct((16, 3 * HEAD), full),
-            jax.ShapeDtypeStruct((shard, hidden), full),
-            jax.ShapeDtypeStruct((hidden // 8, width), full),
-            jax.ShapeDtypeStruct((shard, width), full),
+            jax.ShapeDtypeStruct((shard, hidden), low),
+            jax.ShapeDtypeStruct((hidden // 8, width), low),
+            jax.ShapeDtypeStruct((shard, width), low),
         ],
         scratch_shapes=[
+            held(heads, HEAD, slot_rows), held(head_cols, slot_rows), held(heads, slot_rows, WIDE),
+            held(heads, slot_rows, WIDE), held(head_cols, slot_rows, kind=full), held(heads, 8, slot_rows, kind=full),
             held(head_cols, slot_rows), held(WIDE, local_rows), held(WIDE, local_rows), held(3 * head_cols, slot_rows),
             held(HEAD, slot_rows, kind=full), held(HEAD, slot_rows, kind=full),
             held(slot_rows, width), held(width, 3 * head_cols), held(local_rows, width, kind=full),
-            held(2, 4, shard, half), held(2, 4, shard, small), held(2, 4, 2, piece, width),
             held(2, 4, shard, half), held(2, 4, shard, small), held(2, 4, 2, piece, width),
             held(heads, 8, *tall), held(2, 4, piece, width),
             held(4, shard, half), held(4, shard, small), held(4, piece, width), held(heads, 4, *tall),
@@ -1174,10 +1201,10 @@
             held(shard, half), held(shard, small), held(shard, half), held(shard, small),
             held(4, piece, width), held(heads, 4, *tall),
             held(2, local_rows, width), held(2, local_rows, width), held(local_rows, width),
-            held(local_rows, width), held(local_rows, width), held(4, 32, width),
-            dma((3,)), dma((3,)), dma((3,)), dma((4, 2, 4)), dma((arrays, 3)), dma((arrays, 3)),
-            dma((2,)), dma((2,)), dma((1,)), dma((1,)), dma((3,)), dma((3,)),
-            dma((4, 2, 4)), dma((4, 2, 4)), dma((2, 4)), dma((2, 4)), dma((arrays, 4)), dma((arrays, 4)),
+            held(local_rows, width), held(4, 32, width), held(32, width),
+            dma((3,)), dma((3,)), dma((3,)), dma((heads, 6)), dma((3, 2, 4)), dma((arrays + 1, 3)),
+            dma((arrays + 1, 3)), dma((2, 2)), dma((2, 2)), dma((2,)), dma((2,)),
+            dma((2, 4)), dma((2, 4)), dma((arrays, 4)), dma((arrays, 4)),
             dma((arrays, 2, 4)), dma((arrays, 2, 4)),
         ],
         compiler_params=pltpu.CompilerParams(
@@ -1185,9 +1212,270 @@
         ),
         name="back",
     )(
-        lengths, grad_own, q_x, k_t, k_wide, v_wide, mixed, row_stats, vectors, rows, weight, resid,
+        lengths, grad_own, vectors, q_x, k_t, k_wide, v_wide, mixed, row_stats, rows, weight, resid,
         up_given, down_given, out_given,
     )
+
+
+VECTOR_ROWS = ((1, 0), (1, 1), (2, 0), (4, 1), (5, 0), (5, 1))
+
+
+def phi_parts(value):
+    normal = 0.5 * (1.0 + lax.erf(value * (0.5**0.5)))
+    density = jnp.exp(-0.5 * value * value) * (0.5 * 2.0**0.5 * 3.141592653589793**-0.5)
+    return normal, normal + value * density
+
+
+def statistics(values):
+    centre = values - jnp.mean(values, axis=1, keepdims=True)
+    factor = lax.rsqrt(jnp.mean(centre * centre, axis=1, keepdims=True) + norm_epsilon)
+    return centre * factor, factor
+
+
+def norm_back(grad, gain, normed, factor):
+    scaled = grad * gain
+    first = jnp.mean(scaled, axis=1, keepdims=True)
+    second = jnp.mean(scaled * normed, axis=1, keepdims=True)
+    return factor * (scaled - first - normed * second)
+
+
+def column_total(values):
+    return jnp.sum(values, axis=0, keepdims=True)
+
+
+def middle_kernel(
+    length_ref, layer_in, cotangent, pieces, attended_in, up_in, down_in, out_in,
+    output, resid_out, grad_own, vector_out, up_out, down_out, out_out,
+    attended, up_w, down_w, out_w, vectors, small, up_bias, hidden, slope, normed_one, middle_low, grad_down,
+    grad_two, grad_mid, totals, up_total, up_grad, down_grad, out_grad, up_sum, down_sum, out_sum,
+    load_sem, save_sem, c_send, c_recv,
+):
+    place = Place()
+    rows, width = layer_in.shape
+    ff = up_w.shape[1]
+    chunk = ff // 4
+    shard = width // 8
+    barrier = pltpu.get_barrier_semaphore()
+    pl.semaphore_signal(barrier, inc=1, device_id=place.core, device_id_type=MESH)
+
+    def chunk_lanes(j):
+        return pl.ds(pl.multiple_of(j * chunk, chunk), chunk)
+
+    def up_load(j):
+        return pltpu.make_async_copy(up_in.at[:, chunk_lanes(j)], up_w.at[:, chunk_lanes(j)], load_sem.at[j])
+
+    def down_load(j):
+        return pltpu.make_async_copy(down_in.at[chunk_lanes(j)], down_w.at[chunk_lanes(j)], load_sem.at[4 + j])
+
+    first_loads = [
+        pltpu.make_async_copy(pieces.at[:, pl.ds(shard, 16)], vectors, load_sem.at[8]),
+        pltpu.make_async_copy(attended_in, attended, load_sem.at[9]),
+        pltpu.make_async_copy(out_in, out_w, load_sem.at[10]),
+    ]
+    for load in first_loads:
+        load.start()
+    for j in range(4):
+        up_load(j).start()
+        down_load(j).start()
+    first_loads[0].wait()
+    spots = ((0, 192), (0, 288), (0, 384), (1, 288), (1, 384), (1, 480))
+    for source in range(8):
+        for index, (line, start) in enumerate(spots):
+            small[index : index + 1, source * shard : (source + 1) * shard] = vectors[
+                source, line : line + 1, start : start + shard
+            ].astype(full)
+        base = source * 4 * shard
+        up_bias[0:1, base : base + shard] = vectors[source, 0:1, 480:576].astype(full)
+        up_bias[0:1, base + shard : base + 4 * shard] = vectors[source, 1:2, 0:288].astype(full)
+    out_bias, gain_one, shift_one = small[0:1, :], small[1:2, :], small[2:3, :]
+    down_bias, gain_two, shift_two = small[3:4, :], small[4:5, :], small[5:6, :]
+    first_loads[1].wait()
+    first_loads[2].wait()
+
+    branch = mul(attended[...], out_w[...], TN)
+    normed, factor_one = statistics(layer_in[...].astype(full) + branch + out_bias)
+    normed_one[...] = normed
+    middle_low[...] = (normed * gain_one + shift_one).astype(low)
+    grad_mid[...] = jnp.zeros_like(grad_mid)
+
+    def forward_chunk(j, carry):
+        up_load(j).wait()
+        lanes = chunk_lanes(j)
+        value = mul(middle_low[...], up_w[:, lanes]) + up_bias[0:1, lanes]
+        normal, slope_here = phi_parts(value)
+        hidden[:, lanes] = (value * normal).astype(low)
+        slope[:, lanes] = slope_here
+        down_load(j).wait()
+        grad_mid[...] += mul(hidden[:, lanes], down_w[lanes, :])
+        return carry
+
+    lax.fori_loop(0, 4, forward_chunk, 0)
+    middle = normed_one[...] * gain_one + shift_one
+    normed_two, factor_two = statistics(middle + grad_mid[...] + down_bias)
+    places = place.s * rows + lax.broadcasted_iota(jnp.int32, (rows, 1), 0)
+    in_slot = places < length_ref[0]
+    output[...] = jnp.where(in_slot, normed_two * gain_two + shift_two, 0.0).astype(low)
+    grad_final = jnp.where(in_slot, cotangent[...].astype(full), 0.0)
+    totals[4:5, :] = column_total(grad_final * normed_two)
+    totals[5:6, :] = column_total(grad_final)
+    grad_resid = norm_back(grad_final, gain_two, normed_two, factor_two)
+    grad_two[...] = grad_resid
+    grad_down[...] = grad_resid.astype(low)
+    totals[3:4, :] = column_total(grad_down[...].astype(full))
+    pl.semaphore_wait(barrier, 1)
+
+    def down_piece(ref, line, column, far, core):
+        dest = 2 * line + (place.x if column == 0 else 1 - place.x)
+        y = place.y if far == 0 else 1 - place.y
+        return ref.at[pl.ds(pl.multiple_of(dest * 4 * shard + (2 * y + core) * shard, shard), shard)]
+
+    def side_piece(ref, line, column, core):
+        dest = 2 * line + (place.x if column == 0 else 1 - place.x)
+        half = ref.shape[1] // 2
+        return ref.at[
+            pl.ds(pl.multiple_of(dest * shard, shard), shard), pl.ds(pl.multiple_of(core * half, half), half)
+        ]
+
+    def down_share(line, column, far):
+        return remote(
+            down_piece(down_grad, line, column, far, 1 - place.c), down_sum.at[column, line, far],
+            c_send.at[2 + far, column, line], c_recv.at[2 + far, column, line], place.core,
+        )
+
+    def side_share(array, line, column):
+        grad, total = ((up_grad, up_sum), (out_grad, out_sum))[array]
+        return remote(
+            side_piece(grad, line, column, 1 - place.c), total.at[column, line],
+            c_send.at[array, column, line], c_recv.at[array, column, line], place.core,
+        )
+
+    def down_save(column, line):
+        return pltpu.make_async_copy(down_sum.at[column, line], down_out.at[column, line], save_sem.at[2, column, line])
+
+    def side_save(array, column, line):
+        total, out = ((up_sum, up_out), (out_sum, out_out))[array]
+        return pltpu.make_async_copy(total.at[column, line], out.at[column, line], save_sem.at[array, column, line])
+
+    def down_chunk(line, carry):
+        lanes = chunk_lanes(line)
+        down_grad[lanes, :] = mul(hidden[:, lanes], grad_down[...], TN).astype(low)
+        for column in range(2):
+            for far in range(2):
+                down_share(line, column, far).start()
+        return carry
+
+    lax.fori_loop(0, 4, down_chunk, 0)
+    grad_mid[...] = grad_two[...]
+
+    def back_chunk(turn, carry):
+        j = lax.rem(2 * (1 - place.c) + turn, 4)
+        lanes = chunk_lanes(j)
+        grad_up = (mul(grad_down[...], down_w[lanes, :], NT) * slope[:, lanes]).astype(low)
+        up_total[0:1, lanes] = column_total(grad_up.astype(full))
+        up_grad[:, lanes] = mul(middle_low[...], grad_up, TN).astype(low)
+        grad_mid[...] += mul(grad_up, up_w[:, lanes], NT)
+
+        @pl.when(turn == 1)
+        def _():
+            for column in (1, 0):
+                for line in LINES:
+                    side_share(0, line, column).start()
+
+        return carry
+
+    lax.fori_loop(0, 4, back_chunk, 0)
+    grad_middle = grad_mid[...]
+    normed = normed_one[...]
+    totals[1:2, :] = column_total(grad_middle * normed)
+    totals[2:3, :] = column_total(grad_middle)
+    grad_one = norm_back(grad_middle, gain_one, normed, factor_one)
+    resid_out[...] = grad_one
+    grad_branch = grad_one.astype(low)
+    totals[0:1, :] = column_total(grad_branch.astype(full))
+    out_grad[...] = mul(attended[...], grad_branch).astype(low)
+    for column in (1, 0):
+        for line in LINES:
+            side_share(1, line, column).start()
+    grad_own[...] = mul(out_w[...], grad_branch, NT).astype(low)
+
+    def add_down(column, line):
+        for far in range(2):
+            down_share(line, column, far).wait_recv()
+            down_sum[column, line, far] = add_low(
+                down_sum[column, line, far], down_piece(down_grad, line, column, far, place.c)[...]
+            )
+        down_save(column, line).start()
+
+    def add_side(array, column, line):
+        grad, total = ((up_grad, up_sum), (out_grad, out_sum))[array]
+        side_share(array, line, column).wait_recv()
+        total[column, line] = add_low(total[column, line], side_piece(grad, line, column, place.c)[...])
+        side_save(array, column, line).start()
+
+    for column in range(2):
+        for line in range(4):
+            add_side(0, column, line)
+            add_down(column, line)
+    vector_out[...] = jnp.zeros_like(vector_out)
+    half = 3 * HEAD // 2
+    for dest in range(8):
+        for index, (line, side) in enumerate(VECTOR_ROWS):
+            vector_out[dest, line : line + 1, side * half : (side + 1) * half] = totals[
+                index : index + 1, dest * shard : (dest + 1) * shard
+            ]
+        base = dest * 4 * shard
+        vector_out[dest, 2:3, half:] = up_total[0:1, base : base + shard]
+        vector_out[dest, 3:4, :] = up_total[0:1, base + shard : base + 3 * shard]
+        vector_out[dest, 4:5, :half] = up_total[0:1, base + 3 * shard : base + 4 * shard]
+    for column in range(2):
+        for line in range(4):
+            add_side(1, column, line)
+    for column in range(2):
+        for line in range(4):
+            for array in range(2):
+                side_share(array, line, column).wait_send()
+                side_save(array, column, line).wait()
+            for far in range(2):
+                down_share(line, column, far).wait_send()
+            down_save(column, line).wait()
+
+
+def middle_part(lengths, layer_in, cotangent, pieces, attended, up_full, down_full, out_full):
+    rows, width = layer_in.shape
+    ff = up_full.shape[1]
+    shard = width // 8
+    vmem = pl.BlockSpec(memory_space=pltpu.VMEM)
+    anywhere = pl.BlockSpec(memory_space=pl.ANY)
+    dma = pltpu.SemaphoreType.DMA
+
+    def held(*shape, kind=low):
+        return pltpu.VMEM(shape, kind)
+
+    def shaped(*shape, kind=low):
+        return jax.ShapeDtypeStruct(shape, kind)
+
+    up_parts, down_parts, out_parts = (2, 4, shard, ff // 2), (2, 4, 2, ff // 32, width), (2, 4, shard, width // 2)
+    return pl.pallas_call(
+        middle_kernel,
+        in_specs=[pl.BlockSpec(memory_space=pltpu.SMEM)] + [vmem] * 2 + [anywhere] * 5,
+        out_specs=[vmem] * 4 + [anywhere] * 3,
+        out_shape=[
+            shaped(rows, width), shaped(rows, width, kind=full), shaped(width, rows),
+            shaped(8, 16, 3 * HEAD, kind=full), shaped(*up_parts), shaped(*down_parts), shaped(*out_parts),
+        ],
+        scratch_shapes=[
+            held(width, rows), held(width, ff), held(ff, width), held(width, width), held(8, 16, 9 * HEAD),
+            held(8, width, kind=full), held(8, ff, kind=full), held(rows, ff), held(rows, ff, kind=full),
+            held(rows, width, kind=full), held(rows, width), held(rows, width), held(rows, width, kind=full),
+            held(rows, width, kind=full), held(8, width, kind=full), held(8, ff, kind=full),
+            held(width, ff), held(ff, width), held(width, width), held(*up_parts), held(*down_parts),
+            held(*out_parts), dma((11,)), dma((3, 2, 4)), dma((4, 2, 4)), dma((4, 2, 4)),
+        ],
+        compiler_params=pltpu.CompilerParams(
+            vmem_limit_bytes=VMEM_BYTES, collective_id=2, has_side_effects=True
+        ),
+        name="middle",
+    )(lengths, layer_in, cotangent, pieces, attended, up_full, down_full, out_full)
 
 
 def normalize(values, gain_vec, shift_vec):
@@ -1234,17 +1522,16 @@
         piece = jnp.concatenate([own_shard, packed.reshape(2, -1), spare], axis=0)
         (rows, weight, pieces, q_x, k_t, k_wide, v_wide, mixed, row_stats, up_full, down_full, out_full,
          attended) = front(lengths, layer_in, piece, up_weight, down_weight, out_weight)
-        packed = pieces[:, shard : shard + 2].reshape(fsdp_count, -1).astype(full)
     else:
         rows = lax.all_gather(layer_in, "seq", axis=0, tiled=True)
         weight = lax.all_gather(own_shard, "fsdp", axis=0, tiled=True)
         packed = lax.all_gather(packed.reshape(1, -1), "fsdp", axis=0, tiled=True).astype(full)
-    whole, start = [], 0
-    for vector in vectors:
-        whole.append(packed[:, start : start + vector.shape[0]].reshape(-1))
-        start += vector.shape[0]
-    qv_vec, out_vec, gain_one, shift_one, up_vec, down_vec, gain_two, shift_two = whole
     if not on_block:
+        whole, start = [], 0
+        for vector in vectors:
+            whole.append(packed[:, start : start + vector.shape[0]].reshape(-1))
+            start += vector.shape[0]
+        qv_vec, out_vec, gain_one, shift_one, up_vec, down_vec, gain_two, shift_two = whole
         own_qv = lax.dynamic_slice_in_dim(qv_vec.reshape(2, seq_count, head_cols), seq_place, 1, 1)
         bias = jnp.concatenate([own_qv[0, 0], own_qv[1, 0]])
         bias = jnp.broadcast_to(bias, (8, bias.shape[0]))
@@ -1253,42 +1540,45 @@
         down_full = lax.all_gather(down_weight, "fsdp", axis=0, tiled=True)
         q_x, k_t, k_wide, v_wide, mixed, mixed_low, row_stats = attention_forward(lengths, rows, weight, bias)
         attended = lax.all_to_all(mixed_low, "seq", split_axis=1, concat_axis=0, tiled=True)
-    resid_one = layer_in.astype(full) + mul(attended, out_full, TN) + out_vec
-    middle, norm_one_back = jax.vjp(normalize, resid_one, gain_one, shift_one)
-    middle_low = middle.astype(low)
-    up_pre = mul(middle_low, up_full) + up_vec
-    gelu_out, gelu_back = jax.vjp(partial(jax.nn.gelu, approximate=False), up_pre)
-    hidden = gelu_out.astype(low)
-    down_pre = mul(hidden, down_full) + down_vec
-    final, norm_two_back = jax.vjp(normalize, middle + down_pre, gain_two, shift_two)
-    output = jnp.where(in_slot, final, 0.0).astype(low)
-    grad_final = jnp.where(in_slot, cotangent.astype(full), 0.0)
-    grad_resid_two, grad_gain_two, grad_shift_two = norm_two_back(grad_final)
-    grad_down = grad_resid_two.astype(low)
-    grad_down_weight = mul(hidden, grad_down, TN)
-    (grad_up_pre,) = gelu_back(mul(grad_down, down_full, NT))
-    grad_up = grad_up_pre.astype(low)
-    grad_up_weight = mul(middle_low, grad_up, TN)
-    grad_middle = grad_resid_two + mul(grad_up, up_full, NT)
-    grad_resid_one, grad_gain_one, grad_shift_one = norm_one_back(grad_middle)
-    grad_branch = grad_resid_one.astype(low)
-    grad_out_weight = mul(attended, grad_branch)
-    grad_attended = mul(out_full, grad_branch, NT).astype(low)
-    vector_grads = [
-        column_sums(grad_branch), grad_gain_one, grad_shift_one, column_sums(grad_up),
-        column_sums(grad_down), grad_gain_two, grad_shift_two,
-    ]
-    packed_grad = jnp.concatenate([v.reshape(fsdp_count, -1) for v in vector_grads], axis=1)
+    if on_block:
+        (output, grad_resid_one, grad_attended, packed_grad, grad_up_weight, grad_down_weight, grad_out_weight) = (
+            middle_part(lengths, layer_in, cotangent, pieces, attended, up_full, down_full, out_full)
+        )
+    else:
+        resid_one = layer_in.astype(full) + mul(attended, out_full, TN) + out_vec
+        middle, norm_one_back = jax.vjp(normalize, resid_one, gain_one, shift_one)
+        middle_low = middle.astype(low)
+        up_pre = mul(middle_low, up_full) + up_vec
+        gelu_out, gelu_back = jax.vjp(partial(jax.nn.gelu, approximate=False), up_pre)
+        hidden = gelu_out.astype(low)
+        down_pre = mul(hidden, down_full) + down_vec
+        final, norm_two_back = jax.vjp(normalize, middle + down_pre, gain_two, shift_two)
+        output = jnp.where(in_slot, final, 0.0).astype(low)
+        grad_final = jnp.where(in_slot, cotangent.astype(full), 0.0)
+        grad_resid_two, grad_gain_two, grad_shift_two = norm_two_back(grad_final)
+        grad_down = grad_resid_two.astype(low)
+        grad_down_weight = mul(hidden, grad_down, TN)
+        (grad_up_pre,) = gelu_back(mul(grad_down, down_full, NT))
+        grad_up = grad_up_pre.astype(low)
+        grad_up_weight = mul(middle_low, grad_up, TN)
+        grad_middle = grad_resid_two + mul(grad_up, up_full, NT)
+        grad_resid_one, grad_gain_one, grad_shift_one = norm_one_back(grad_middle)
+        grad_branch = grad_resid_one.astype(low)
+        grad_out_weight = mul(attended, grad_branch)
+        grad_attended = mul(out_full, grad_branch, NT).astype(low)
+        vector_grads = [
+            column_sums(grad_branch), grad_gain_one, grad_shift_one, column_sums(grad_up),
+            column_sums(grad_down), grad_gain_two, grad_shift_two,
+        ]
+        packed_grad = jnp.concatenate([v.reshape(fsdp_count, -1) for v in vector_grads], axis=1)
     saved = (q_x, k_t, k_wide, v_wide, mixed, row_stats)
     if on_block:
-        packed_grad = jnp.pad(
-            packed_grad.reshape(fsdp_count, 5, head_cols), ((0, 0), (1, 10), (0, 0))
-        )
         (input_grad, grad_read, grad_write, qkv_out, vector_sum, up_out, down_out, out_out) = back(
             lengths, grad_attended, saved, packed_grad, rows, weight, grad_resid_one,
-            grad_up_weight.astype(low), grad_down_weight.astype(low), grad_out_weight.astype(low),
+            grad_up_weight, grad_down_weight, grad_out_weight,
         )
         own_vectors = vector_sum[:6].reshape(-1)
+        qkv_out, up_out, down_out, out_out = (g.astype(full) for g in (qkv_out, up_out, down_out, out_out))
     else:
         grad_t = lax.all_to_all(grad_attended, "seq", split_axis=0, concat_axis=1, tiled=True)
         partial_in, weight_part, sums = attention_backward(*saved, grad_t, rows, weight)

time: 295 us -> 243 us (0.82)
  matrix products: 51.3 us -> 1.29 us
  Pallas kernels: 207 us -> 217 us
  local copies, waits for them, and re-layouts: 24.4 us -> 15.4 us
    dot_general x10 -> x1, matrix products: 51.3 us -> 1.29 us  [mul(): return lax.dot_general(left, right, dims, preferred_element_type=full)]
    pallas_call x0 -> x1, Pallas kernels: none -> 34.3 us  [middle_part(): pl.pallas_call(middle_kernel, in_specs=[pl.BlockSpec(memory_space=pltpu.S...]
    pallas_call x1, Pallas kernels: 130 us -> 106 us  [back(): pl.pallas_call(back_kernel, in_specs=[pl.BlockSpec(memory_space=pltpu.SME...]
    unnamed x46 -> x19, local copies, waits for them, and re-layouts: 13.4 us -> 6.31 us
    reduce_sum x7 -> x0, other arithmetic: 5.36 us -> none  [the longest x2 3.6 us: normalize(): centre = values - jnp.mean(values, axis=-1, keepdims=True)]
    convert_element_type x1 -> x4, other arithmetic: 0.9 us -> 5.89 us  [per_device(): g.astype(full)]
where the time goes in v4:
time: 243 us; the launch traced here: 242 us
  Pallas kernels  217 us (89%)
  local copies, waits for them, and re-layouts  15.4 us (6%)
  other arithmetic  6.74 us (3%)
    pallas_call x1, Pallas kernels, back(): pl.pallas_call(back_kernel, in_specs=[pl.BlockSpec(memory_space=pltpu.SME...  106 us
    pallas_call x1, Pallas kernels, front(): pl.pallas_call(front_kernel, in_specs=[pl.BlockSpec(memory_space=pltpu.SM...  77.1 us
    pallas_call x1, Pallas kernels, middle_part(): pl.pallas_call(middle_kernel, in_specs=[pl.BlockSpec(memory_space=pltpu.S...  34.3 us
    unnamed x19, local copies, waits for them, and re-layouts  6.31 us
    convert_element_type x4, other arithmetic, per_device(): g.astype(full)  5.89 us
    concatenate x1, local copies, waits for them, and re-layouts, per_device(): packed = jnp.concatenate(vectors)  5.44 us

profile of v4, /device:TPU:9, one launch (start us, length us, event | category | flops | bytes accessed | tf_op | source)
XLA Modules:
  0.0 242.3 jit_solution(4898950499466181942)
XLA Ops:
  0.6 0.0 copy-start.5
  0.7 0.0 copy-start.6
  0.7 0.0 copy-start.1
  1.4 0.1 pad.2.clone
  1.5 5.4 %concatenate.14 = bf16[1152]{0:T(1024)(128)(2,1)S(1)} concatenate(bf16[192]{0:T(256)(128)(2,1)} %param.22, bf16[96]{0:T(256)(128)(2,1)} %param.24, bf16[96]{0:T(256)(128)(2,1)} %param.25, bf16[96]{0:T(256)(128)(2,1)} %param.26, bf16[384]{0:T(512)(128)(2,1)} %param.28, bf16[96]{0:T(256)(128)(2,1)} %param.30, bf16[96]{0:T(256)(128)(2,1)} %param.31, bf16[96]{0:T(256)(128)(2,1)} %param.32), dimensions={0} | concatenate | bytes 4608 | tf_op jit(solution)/shard_map/concatenate | solution.py:1518
  6.9 0.1 reshape.59
  7.0 0.1 broadcast_compare_fusion
  7.1 1.3 copy.45
  8.5 0.1 copy.47
  8.6 0.8 maximum_maximum_fusion.qkv_in
  9.4 0.0 copy-done.5
  9.4 0.0 copy-done.6
  9.4 0.0 copy-done.1
  9.4 1.3 fusion.rows_in.layer_in
  10.7 77.1 %front.1 = (bf16[2048,768]{1,0:T(8,128)(2,1)}, bf16[768,576]{1,0:T(8,128)(2,1)}, bf16[8,112,576]{2,1,0:T(8,128)(2,1)}, bf16[3,128,2048]{2,1,0:T(8,128)(2,1)}, bf...) custom-call(s32[1]{0:T(128)S(6)} %copy.52.length_ref, ...), custom_call_target="tpu_custom_call" | custom-call | tf_op jit(solution)/shard_map/front/pallas_call | solution.py:660
  87.8 34.3 %middle.1 = (bf16[512,768]{1,0:T(8,128)(2,1)}, f32[512,768]{1,0:T(8,128)}, bf16[768,512]{1,0:T(8,128)(2,1)}, f32[8,16,192]{2,1,0:T(8,128)}, bf16[2,4,96,1536]{3,...) custom-call(s32[1]{0:T(128)S(6)} %copy.52.length_ref, ...), custom_call_target="tpu_custom_call" | custom-call | tf_op jit(solution)/shard_map/middle/pallas_call | solution.py:1458
  122.2 106.0 %back.1 = (f32[512,768]{1,0:T(8,128)}, f32[10,768]{1,0:T(8,128)}, f32[10,768]{1,0:T(8,128)}, bf16[96,2304]{1,0:T(8,128)(2,1)}, f32[16,192]{1,0:T(8,128)}, /*inde...) custom-call(s32[1]{0:T(128)S(6)} %copy.52.length_ref, ...), custom_call_target="tpu_custom_call" | custom-call | tf_op jit(solution)/shard_map/back/pallas_call | solution.py:1177
  228.1 0.0 copy-start.4
  228.2 1.5 copy.48
  229.7 1.3 slice.31
  230.9 0.7 slice.33
  231.6 0.1 reshape.60
  231.7 0.7 slice.44
  232.3 0.6 fusion.6
  232.9 1.4 copy.49
  234.4 1.6 convert_element_type.25
  236.0 2.0 convert_element_type.24
  238.1 1.1 convert_element_type.26
  239.2 0.0 copy-done.3
  239.2 1.1 convert_element_type.27
  240.3 0.9 copy.53
  241.2 1.1 copy.54
  (11 shorter events, 0.1 us)
Async XLA Ops:
  0.6 8.8 %copy-start.5 = (bf16[1,10,768]{2,1,0:T(8,128)(2,1)S(1)}, bf16[1,10,768]{2,1,0:T(8,128)(2,1)}, u32[]{:S(2)}) copy-start(bf16[1,10,768]{2,1,0:T(8,128)(2,1)} %param.19) | copy-start | bytes 46084
  0.7 8.8 %copy-start.6 = (bf16[1,10,768]{2,1,0:T(8,128)(2,1)S(1)}, bf16[1,10,768]{2,1,0:T(8,128)(2,1)}, u32[]{:S(2)}) copy-start(bf16[1,10,768]{2,1,0:T(8,128)(2,1)} %param.18) | copy-start | bytes 46084
  0.7 8.7 %copy-start.1 = (bf16[512,768]{1,0:T(8,128)(2,1)S(1)}, bf16[512,768]{1,0:T(8,128)(2,1)}, u32[]{:S(2)}) copy-start(bf16[512,768]{1,0:T(8,128)(2,1)} %param.17) | copy-start | bytes 2359300
  228.1 9.9 %copy-start.4 = (bf16[96,3072]{1,0:T(8,128)(2,1)S(1)}, bf16[96,3072]{1,0:T(8,128)(2,1)}, u32[]{:S(2)}) copy-start(bf16[96,3072]{1,0:T(8,128)(2,1)} %get-tuple-element.70) | copy-start | bytes 1769476
  236.0 3.2 %copy-start.3 = (bf16[384,768]{1,0:T(8,128)(2,1)S(1)}, bf16[384,768]{1,0:T(8,128)(2,1)}, u32[]{:S(2)}) copy-start(bf16[384,768]{1,0:T(8,128)(2,1)} %get-tuple-element.71) | copy-start | bytes 1769476
  238.1 2.2 copy-start.2
  239.2 2.0 copy-start

commit v5 on v4

--- a/solution.py
+++ b/solution.py
@@ -702,59 +702,76 @@
     def __init__(self, place, given, sums, from_y, from_x, from_z, sems):
         self.place, self.given, self.sums = place, given, sums
         self.from_y, self.from_x, self.from_z = from_y, from_x, from_z
+        self.last = max(sums)
         self.y_send, self.y_recv, self.x_send, self.x_recv, self.z_send, self.z_recv = sems
 
     def dest(self, column, line):
         x = self.place.x
         return 2 * line + (x if column == 0 else 1 - x)
 
-    def slot(self, array, column, line, far=0):
+    def slot(self, array, line, column=0):
         if array >= DW_FIRST:
-            return self.sums[array].at[self.dest(column, line)]
-        if array == DOWN_W:
-            return self.sums[array].at[column, line, far]
-        return self.sums[array].at[column, line]
+            rows = 4 * HEAD if array == self.last else 3 * HEAD
+            return self.sums[array].at[self.dest(column, line), pl.ds(0, rows // 4)]
+        return self.sums[array].at[line]
+
+    def cut(self, array, ref):
+        if DW_FIRST <= array < self.last:
+            return ref.at[pl.ds(0, 3 * HEAD // 4)]
+        return ref
 
     def load(self, array, column, line, sem):
-        target, source = self.sums[array].at[column, line], self.given[array].at[column, line]
-        if array == DOWN_W:
-            target, source = target.at[0], source.at[0]
-        return pltpu.make_async_copy(source, target, sem)
-
-    def over_y(self, column, line):
+        source = self.given[array]
+        if array == OUT_W:
+            return pltpu.make_async_copy(source.at[line], self.sums[array].at[line], sem)
+        source = source.at[column, line, 0] if array == DOWN_W else source.at[column, line]
+        return pltpu.make_async_copy(source, self.sums[array].at[line], sem)
+
+    def over_y(self, line):
         return remote(
-            self.given[DOWN_W].at[column, line, 1], self.from_y.at[column, line],
-            self.y_send.at[column, line], self.y_recv.at[column, line], self.place.across_y,
-        )
-
-    def add_y(self, column, line):
-        self.over_y(column, line).wait_recv()
-        slot = self.slot(DOWN_W, column, line, 0)
-        slot[...] = add_low(slot[...], self.from_y[column, line])
+            self.given[DOWN_W].at[0, line, 1], self.from_y.at[line], self.y_send.at[line], self.y_recv.at[line],
+            self.place.across_y,
+        )
+
+    def add_y(self, line):
+        self.over_y(line).wait_recv()
+        slot = self.slot(DOWN_W, line)
+        slot[...] = add_low(slot[...], self.from_y[line])
 
     def over_x(self, array, line):
-        start = self.given[array].at[1, line] if array in (UP_W, OUT_W) else self.slot(array, 1, line)
+        if array == OUT_W:
+            here = self.sums[array].at[self.place.z]
+            return remote(
+                here.at[1], self.from_x[array], self.x_send.at[array, 0], self.x_recv.at[array, 0], self.place.across_x
+            )
+        if array == UP_W:
+            start = self.given[array].at[1, line]
+        elif array == DOWN_W:
+            start = self.given[array].at[1, line, 0]
+        else:
+            start = self.slot(array, line, 1)
         return remote(
-            start, self.from_x[array].at[line],
-            self.x_send.at[array, line], self.x_recv.at[array, line], self.place.across_x,
+            start, self.cut(array, self.from_x[array].at[line]), self.x_send.at[array, line],
+            self.x_recv.at[array, line], self.place.across_x,
         )
 
     def add_x(self, array, line):
         self.over_x(array, line).wait_recv()
-        slot = self.slot(array, 0, line)
-        slot[...] = add_low(slot[...], self.from_x[array][line])
+        slot = self.sums[array].at[self.place.z, 0] if array == OUT_W else self.slot(array, line)
+        came = self.from_x[array] if array == OUT_W else self.cut(array, self.from_x[array].at[line])
+        slot[...] = add_low(slot[...], came[...])
 
     def along_z(self, array, way, line):
         return remote(
-            self.slot(array, 0, line), self.from_z[array].at[way, line],
+            self.slot(array, line), self.cut(array, self.from_z[array].at[way, line]),
             self.z_send.at[array, way, line], self.z_recv.at[array, way, line],
             self.place.above if way == 0 else self.place.below,
         )
 
     def add_z(self, array, way, line):
         self.along_z(array, way, line).wait_recv()
-        slot = self.slot(array, 0, line)
-        slot[...] = add_low(slot[...], self.from_z[array][way, line])
+        slot = self.slot(array, line)
+        slot[...] = add_low(slot[...], self.cut(array, self.from_z[array].at[way, line])[...])
 
     def hop(self, array, level, lines=(0, 1, 2, 3)):
         @pl.when(self.place.z == level)
@@ -785,12 +802,12 @@
 
     def finish(self, array):
         for line in range(4):
-            self.over_x(array, line).wait_send()
+            if array != OUT_W or line == 0:
+                self.over_x(array, line).wait_send()
             pl.when(self.place.z < line)(lambda line=line: self.along_z(array, 0, line).wait_send())
             pl.when(self.place.z > line)(lambda line=line: self.along_z(array, 1, line).wait_send())
             if array == DOWN_W:
-                for column in range(2):
-                    self.over_y(column, line).wait_send()
+                self.over_y(line).wait_send()
 
 
 class Spread:
@@ -883,21 +900,17 @@
         loads.append(pltpu.make_async_copy(src, dst, local_sem.at[index]))
 
     def sum_loads(array):
-        columns = (0, 1) if array == DOWN_W else (0,)
-        return [
-            reduce.load(array, column, line, mine_sem.at[array, column, line]) for column in columns for line in LINES
-        ]
+        return [reduce.load(array, 0, line, mine_sem.at[array, line]) for line in LINES]
 
     def send_x(array, lines=LINES):
         for line in lines:
             reduce.over_x(array, line).start()
 
     send_x(UP_W)
-    for column in (1, 0):
-        for line in LINES:
-            reduce.over_y(column, line).start()
-    send_x(OUT_W)
-    for array in (UP_W, DOWN_W, OUT_W):
+    for line in LINES:
+        reduce.over_y(line).start()
+    send_x(DOWN_W)
+    for array in (OUT_W, UP_W, DOWN_W):
         for load in sum_loads(array):
             load.start()
     for load in loads:
@@ -921,64 +934,71 @@
             loads[0].wait()
         base = 3 * h * HEAD
         part = jnp.transpose(mul(grads[base : base + 3 * HEAD, :], rows_ref[...])).astype(low)
-        shard = width // 8
+        half = width // 16
         for dest in range(8):
-            dw[h, dest, :shard, :] = part[dest * shard : (dest + 1) * shard]
+            start = 2 * half * dest
+            dw[h, dest, :half, :] = jnp.concatenate(
+                [part[start : start + half], part[start + half : start + 2 * half]], axis=1
+            )
             if h == heads - 1:
-                dw[h, dest, shard:, :] = vectors_in[dest].astype(low)
-            else:
-                dw[h, dest, shard:, :] = jnp.zeros((16, 3 * HEAD), low)
+                dw[h, dest, half:, :] = vectors_in[dest].astype(low)
         if h == heads - 1:
             total = jnp.sum(grads[...].astype(full), axis=1, keepdims=True)
             spread = jnp.transpose(jnp.broadcast_to(total, (total.shape[0], WIDE)))[0:1]
             for kind, first_dest in ((0, 0), (2, 4)):
                 for head in range(heads):
                     start = (3 * head + kind) * HEAD
-                    dw[h, first_dest + place.s, shard : shard + 1, head * HEAD : (head + 1) * HEAD] = spread[
+                    dw[h, first_dest + place.s, half : half + 1, head * HEAD : (head + 1) * HEAD] = spread[
                         :, start : start + HEAD
                     ].astype(low)
         send_x(DW_FIRST + h)
 
     share = {UP_W: (up_last, up_other), OUT_W: (out_last, out_other)}
 
+    def settled(array):
+        return sums[array].at[place.z, 0] if array == OUT_W else sums[array].at[place.z]
+
     def sum_y(array):
-        mine_now = sums[array].at[0, place.z]
+        mine_now = settled(array)
         return remote(mine_now, share[array][0], share_send.at[array, 0], share_recv.at[array, 0], place.across_y)
 
     def half_to_core(array):
-        mine_now = sums[array].at[0, place.z]
+        mine_now = settled(array)
         return remote(mine_now, share[array][1], share_send.at[array, 1], share_recv.at[array, 1], place.core)
 
     def spread_of(array):
         if array == DOWN_W:
-            return Spread(place, down_all, down_sum.at[0, place.z, 0], share_send.at[2], share_recv.at[2])
+            return Spread(place, down_all, down_sum.at[place.z], share_send.at[2], share_recv.at[2])
         h = array - DW_FIRST
-        return Spread(place, dw_all.at[h], dw.at[h, place.f], share_send.at[array], share_recv.at[array])
+        return Spread(
+            place, dw_all.at[h, :, pl.ds(0, reduce.slot(array, 0).shape[0])], reduce.slot(array, place.z),
+            share_send.at[array], share_recv.at[array],
+        )
 
     def add_last(array):
         sum_y(array).wait()
-        slot = sums[array].at[0, place.z]
+        slot = settled(array)
         slot[...] = add_low(slot[...], share[array][0][...])
         half_to_core(array).start()
 
     first, second = DW_FIRST, DW_FIRST + 1
-
-    def add_y(column):
-        for line in LINES:
-            reduce.add_y(column, line)
 
     def chores(index):
         if index == 1:
             send_grad(2, True).wait_recv()
+            for load in sum_loads(OUT_W):
+                load.wait()
+            reduce.hop(OUT_W, 0)
         elif index == 2:
             send_grad(1, True).wait_recv()
-            for array in (UP_W, DOWN_W, OUT_W):
+            for array in (UP_W, DOWN_W):
                 for load in sum_loads(array):
                     load.wait()
+            take_x(UP_W, (3,))
+            reduce.hop(UP_W, 0, (3,))
         elif index == 3:
             send_grad(0, True).wait_recv()
-            take_x(UP_W, (3,))
-            reduce.hop(UP_W, 0, (3,))
+            reduce.hop(OUT_W, 1)
         elif index == 4:
             for load in saved_loads(1):
                 load.wait()
@@ -986,38 +1006,37 @@
             take_x(UP_W, (0,))
             reduce.hop(UP_W, 0, (0,))
         elif index == 5:
-            add_y(1)
-            send_x(DOWN_W)
+            reduce.hop(OUT_W, 2)
+        elif index == 6:
+            for line in LINES:
+                reduce.add_y(line)
             take_x(UP_W, (2,))
             reduce.hop(UP_W, 0, (2,))
-        elif index == 6:
+            reduce.settle(OUT_W)
+            reduce.over_x(OUT_W, 0).start()
+        elif index == 7:
             reduce.hop(UP_W, 1, (3, 0))
-            take_x(UP_W, (1,))
-            reduce.hop(UP_W, 0, (1,))
-        elif index == 7:
-            take_x(OUT_W)
-            reduce.hop(OUT_W, 0)
-            reduce.hop(UP_W, 1, (2, 1))
         elif index == 8:
             for load in saved_loads(2):
                 load.wait()
             weight_part(1)
+            take_x(UP_W, (1,))
+            reduce.hop(UP_W, 0, (1,))
+        elif index == 9:
             reduce.hop(UP_W, 2)
-            add_y(0)
-        elif index == 9:
+            reduce.hop(UP_W, 1, (2,))
             take_x(DOWN_W, (3, 0))
             reduce.hop(DOWN_W, 0, (3, 0))
-            reduce.hop(OUT_W, 1)
         elif index == 10:
+            reduce.hop(UP_W, 1, (1,))
+            take_x(DOWN_W, (2,))
+            reduce.hop(DOWN_W, 0, (2,))
+        elif index == 11:
             reduce.settle(UP_W)
             sum_y(UP_W).start()
-            take_x(DOWN_W, (2, 1))
-            reduce.hop(DOWN_W, 0, (2, 1))
-        elif index == 11:
-            reduce.hop(OUT_W, 2)
-            reduce.hop(DOWN_W, 1)
-            take_x(first)
-            reduce.hop(first, 0)
+            take_x(DOWN_W, (1,))
+            reduce.hop(DOWN_W, 0, (1,))
+            reduce.hop(DOWN_W, 1, (3, 0))
 
     def step(index, carry):
         for when in range(1, 12):
@@ -1083,31 +1102,37 @@
         share_far(half).start()
     memory = Spread(place, memory_all, memory_own, share_send.at[DW_FIRST + heads], share_recv.at[DW_FIRST + heads])
     memory.start()
+    take_x(first)
+    reduce.hop(first, 0)
+    reduce.add_x(OUT_W, 0)
+    sum_y(OUT_W).start()
+    for half in range(halves):
+        rows = slice(half * part, (half + 1) * part)
+        near_send[1, rows, :] = part_for(2, half).astype(low)
+        share_near(1, half).start()
+    reduce.hop(DOWN_W, 1, (2, 1))
+    reduce.hop(DOWN_W, 2)
     take_x(second)
     reduce.hop(second, 0)
     take_x(last)
     reduce.hop(last, 0)
     reduce.hop(first, 1)
-    for half in range(halves):
-        rows = slice(half * part, (half + 1) * part)
-        near_send[1, rows, :] = part_for(2, half).astype(low)
-        share_near(1, half).start()
-    reduce.hop(last, 1)
-    reduce.hop(second, 1)
-    reduce.hop(DOWN_W, 2)
-    reduce.hop(first, 2)
+    add_last(UP_W)
     for half in range(halves):
         resid_ref[half * part : (half + 1) * part, :] += part_for(3, half)
-    reduce.hop(last, 2)
-    reduce.hop(second, 2)
-    reduce.settle(OUT_W)
-    sum_y(OUT_W).start()
-    for h in (heads - 1, 0, 1):
-        reduce.settle(DW_FIRST + h)
-        spread_of(DW_FIRST + h).start()
+    reduce.hop(second, 1)
+    reduce.hop(first, 2)
+    reduce.hop(last, 1)
     reduce.settle(DOWN_W)
     spread_of(DOWN_W).start()
-    add_last(UP_W)
+    reduce.hop(second, 2)
+    reduce.settle(first)
+    spread_of(first).start()
+    reduce.hop(last, 2)
+    reduce.settle(second)
+    spread_of(second).start()
+    reduce.settle(last)
+    spread_of(last).start()
     add_last(OUT_W)
     memory.pass_on()
     for h in (heads - 1, 0, 1):
@@ -1115,7 +1140,7 @@
     spread_of(DOWN_W).pass_on()
     for array, out in ((UP_W, up_out), (OUT_W, out_out)):
         columns = out.shape[1] // 2
-        out[:, pl.ds(pl.multiple_of(place.c * columns, columns), columns)] = sums[array][0, place.z]
+        out[:, pl.ds(pl.multiple_of(place.c * columns, columns), columns)] = settled(array)[...]
         half_to_core(array).wait()
         out[:, pl.ds(pl.multiple_of((1 - place.c) * columns, columns), columns)] = share[array][1][...]
     for h in range(heads):
@@ -1124,15 +1149,19 @@
     quarter = down_out.shape[0] // 4
     for member in range(4):
         down_out[member * quarter : (member + 1) * quarter, :] = down_all[member]
-    shard = qkv_out.shape[0]
+    half = qkv_out.shape[0] // 2
     for kind in range(3):
         for member in range(4):
             for h in range(heads):
                 start = kind * width + (member * heads + h) * HEAD
-                qkv_out[:, start : start + HEAD] = dw_all[h, member, :shard, kind * HEAD : (kind + 1) * HEAD]
-    vector_sum = dw_all[heads - 1, 0, shard:, :].astype(full)
+                for side in range(2):
+                    lanes = (3 * side + kind) * HEAD
+                    qkv_out[side * half : (side + 1) * half, start : start + HEAD] = dw_all[
+                        h, member, :half, lanes : lanes + HEAD
+                    ]
+    vector_sum = dw_all[heads - 1, 0, half:, :].astype(full)
     for member in range(1, 4):
-        vector_sum = vector_sum + dw_all[heads - 1, member, shard:, :].astype(full)
+        vector_sum = vector_sum + dw_all[heads - 1, member, half:, :].astype(full)
     vector_out[...] = vector_sum
     memory.finish()
     total = memory_all[0].astype(full)
@@ -1173,7 +1202,7 @@
     def held(*shape, kind=low):
         return pltpu.VMEM(shape, kind)
 
-    tall = (shard + 16, 3 * HEAD)
+    tall = (shard // 2 + 16, 6 * HEAD)
     return pl.pallas_call(
         back_kernel,
         in_specs=[pl.BlockSpec(memory_space=pltpu.SMEM)] + [vmem] * 2 + [anywhere] * 12,
@@ -1183,7 +1212,7 @@
             jax.ShapeDtypeStruct((MEM, width), full),
             jax.ShapeDtypeStruct((MEM, width), full),
             jax.ShapeDtypeStruct((shard, 3 * width), low),
-            jax.ShapeDtypeStruct((16, 3 * HEAD), full),
+            jax.ShapeDtypeStruct((16, 6 * HEAD), full),
             jax.ShapeDtypeStruct((shard, hidden), low),
             jax.ShapeDtypeStruct((hidden // 8, width), low),
             jax.ShapeDtypeStruct((shard, width), low),
@@ -1194,17 +1223,17 @@
             held(head_cols, slot_rows), held(WIDE, local_rows), held(WIDE, local_rows), held(3 * head_cols, slot_rows),
             held(HEAD, slot_rows, kind=full), held(HEAD, slot_rows, kind=full),
             held(slot_rows, width), held(width, 3 * head_cols), held(local_rows, width, kind=full),
-            held(2, 4, shard, half), held(2, 4, shard, small), held(2, 4, 2, piece, width),
-            held(heads, 8, *tall), held(2, 4, piece, width),
-            held(4, shard, half), held(4, shard, small), held(4, piece, width), held(heads, 4, *tall),
-            held(2, 4, shard, half), held(2, 4, shard, small), held(2, 4, piece, width), held(heads, 2, 4, *tall),
+            held(4, shard, half), held(4, 2, shard, small), held(4, piece, width),
+            held(heads, 8, *tall), held(4, piece, width),
+            held(4, shard, half), held(shard, small), held(4, piece, width), held(heads, 4, *tall),
+            held(2, 4, shard, half), held(2, 4, 2, shard, small), held(2, 4, piece, width), held(heads, 2, 4, *tall),
             held(shard, half), held(shard, small), held(shard, half), held(shard, small),
             held(4, piece, width), held(heads, 4, *tall),
             held(2, local_rows, width), held(2, local_rows, width), held(local_rows, width),
             held(local_rows, width), held(4, 32, width), held(32, width),
-            dma((3,)), dma((3,)), dma((3,)), dma((heads, 6)), dma((3, 2, 4)), dma((arrays + 1, 3)),
+            dma((3,)), dma((3,)), dma((3,)), dma((heads, 6)), dma((3, 4)), dma((arrays + 1, 3)),
             dma((arrays + 1, 3)), dma((2, 2)), dma((2, 2)), dma((2,)), dma((2,)),
-            dma((2, 4)), dma((2, 4)), dma((arrays, 4)), dma((arrays, 4)),
+            dma((4,)), dma((4,)), dma((arrays, 4)), dma((arrays, 4)),
             dma((arrays, 2, 4)), dma((arrays, 2, 4)),
         ],
         compiler_params=pltpu.CompilerParams(
@@ -1217,9 +1246,6 @@
     )
 
 
-VECTOR_ROWS = ((1, 0), (1, 1), (2, 0), (4, 1), (5, 0), (5, 1))
-
-
 def phi_parts(value):
     normal = 0.5 * (1.0 + lax.erf(value * (0.5**0.5)))
     density = jnp.exp(-0.5 * value * value) * (0.5 * 2.0**0.5 * 3.141592653589793**-0.5)
@@ -1248,7 +1274,7 @@
     output, resid_out, grad_own, vector_out, up_out, down_out, out_out,
     attended, up_w, down_w, out_w, vectors, small, up_bias, hidden, slope, normed_one, middle_low, grad_down,
     grad_two, grad_mid, totals, up_total, up_grad, down_grad, out_grad, up_sum, down_sum, out_sum,
-    load_sem, save_sem, c_send, c_recv,
+    from_y, load_sem, save_sem, c_send, c_recv, y_send, y_recv,
 ):
     place = Place()
     rows, width = layer_in.shape
@@ -1256,7 +1282,8 @@
     chunk = ff // 4
     shard = width // 8
     barrier = pltpu.get_barrier_semaphore()
-    pl.semaphore_signal(barrier, inc=1, device_id=place.core, device_id_type=MESH)
+    for where in (place.core, place.across_y):
+        pl.semaphore_signal(barrier, inc=1, device_id=where, device_id_type=MESH)
 
     def chunk_lanes(j):
         return pl.ds(pl.multiple_of(j * chunk, chunk), chunk)
@@ -1322,7 +1349,7 @@
     grad_two[...] = grad_resid
     grad_down[...] = grad_resid.astype(low)
     totals[3:4, :] = column_total(grad_down[...].astype(full))
-    pl.semaphore_wait(barrier, 1)
+    pl.semaphore_wait(barrier, 2)
 
     def down_piece(ref, line, column, far, core):
         dest = 2 * line + (place.x if column == 0 else 1 - place.x)
@@ -1342,10 +1369,16 @@
             c_send.at[2 + far, column, line], c_recv.at[2 + far, column, line], place.core,
         )
 
+    def side_slot(array, line, column):
+        return out_sum.at[line, column] if array == 1 else up_sum.at[column, line]
+
+    def over_y(line):
+        return remote(down_sum.at[1, line, 1], from_y.at[line], y_send.at[line], y_recv.at[line], place.across_y)
+
     def side_share(array, line, column):
-        grad, total = ((up_grad, up_sum), (out_grad, out_sum))[array]
+        grad = (up_grad, out_grad)[array]
         return remote(
-            side_piece(grad, line, column, 1 - place.c), total.at[column, line],
+            side_piece(grad, line, column, 1 - place.c), side_slot(array, line, column),
             c_send.at[array, column, line], c_recv.at[array, column, line], place.core,
         )
 
@@ -1353,8 +1386,14 @@
         return pltpu.make_async_copy(down_sum.at[column, line], down_out.at[column, line], save_sem.at[2, column, line])
 
     def side_save(array, column, line):
-        total, out = ((up_sum, up_out), (out_sum, out_out))[array]
-        return pltpu.make_async_copy(total.at[column, line], out.at[column, line], save_sem.at[array, column, line])
+        out = out_out.at[line, column] if array == 1 else up_out.at[column, line]
+        return pltpu.make_async_copy(side_slot(array, line, column), out, save_sem.at[array, column, line])
+
+    def add_far(column, line):
+        down_share(line, column, 1).wait_recv()
+        down_sum[column, line, 1] = add_low(
+            down_sum[column, line, 1], down_piece(down_grad, line, column, 1, place.c)[...]
+        )
 
     def down_chunk(line, carry):
         lanes = chunk_lanes(line)
@@ -1374,6 +1413,12 @@
         up_total[0:1, lanes] = column_total(grad_up.astype(full))
         up_grad[:, lanes] = mul(middle_low[...], grad_up, TN).astype(low)
         grad_mid[...] += mul(grad_up, up_w[:, lanes], NT)
+
+        @pl.when(turn == 0)
+        def _():
+            for line in LINES:
+                add_far(1, line)
+                over_y(line).start()
 
         @pl.when(turn == 1)
         def _():
@@ -1399,37 +1444,42 @@
     grad_own[...] = mul(out_w[...], grad_branch, NT).astype(low)
 
     def add_down(column, line):
-        for far in range(2):
-            down_share(line, column, far).wait_recv()
-            down_sum[column, line, far] = add_low(
-                down_sum[column, line, far], down_piece(down_grad, line, column, far, place.c)[...]
-            )
+        down_share(line, column, 0).wait_recv()
+        down_sum[column, line, 0] = add_low(
+            down_sum[column, line, 0], down_piece(down_grad, line, column, 0, place.c)[...]
+        )
+        if column == 0:
+            add_far(column, line)
+        else:
+            over_y(line).wait()
+            down_sum[column, line, 0] = add_low(down_sum[column, line, 0], from_y[line])
         down_save(column, line).start()
 
     def add_side(array, column, line):
-        grad, total = ((up_grad, up_sum), (out_grad, out_sum))[array]
+        slot = side_slot(array, line, column)
         side_share(array, line, column).wait_recv()
-        total[column, line] = add_low(total[column, line], side_piece(grad, line, column, place.c)[...])
+        slot[...] = add_low(slot[...], side_piece((up_grad, out_grad)[array], line, column, place.c)[...])
         side_save(array, column, line).start()
 
-    for column in range(2):
-        for line in range(4):
+    for line in LINES:
+        add_down(0, line)
+    for column in (1, 0):
+        for line in LINES:
             add_side(0, column, line)
-            add_down(column, line)
     vector_out[...] = jnp.zeros_like(vector_out)
-    half = 3 * HEAD // 2
     for dest in range(8):
-        for index, (line, side) in enumerate(VECTOR_ROWS):
-            vector_out[dest, line : line + 1, side * half : (side + 1) * half] = totals[
+        for index, (line, start) in enumerate(((0, 2), (0, 3), (1, 0), (2, 1), (2, 2), (2, 3))):
+            vector_out[dest, line : line + 1, start * shard : (start + 1) * shard] = totals[
                 index : index + 1, dest * shard : (dest + 1) * shard
             ]
         base = dest * 4 * shard
-        vector_out[dest, 2:3, half:] = up_total[0:1, base : base + shard]
-        vector_out[dest, 3:4, :] = up_total[0:1, base + shard : base + 3 * shard]
-        vector_out[dest, 4:5, :half] = up_total[0:1, base + 3 * shard : base + 4 * shard]
+        vector_out[dest, 1:2, shard:] = up_total[0:1, base : base + 3 * shard]
+        vector_out[dest, 2:3, :shard] = up_total[0:1, base + 3 * shard : base + 4 * shard]
     for column in range(2):
         for line in range(4):
             add_side(1, column, line)
+    for line in LINES:
+        add_down(1, line)
     for column in range(2):
         for line in range(4):
             for array in range(2):
@@ -1454,14 +1504,14 @@
     def shaped(*shape, kind=low):
         return jax.ShapeDtypeStruct(shape, kind)
 
-    up_parts, down_parts, out_parts = (2, 4, shard, ff // 2), (2, 4, 2, ff // 32, width), (2, 4, shard, width // 2)
+    up_parts, down_parts, out_parts = (2, 4, shard, ff // 2), (2, 4, 2, ff // 32, width), (4, 2, shard, width // 2)
     return pl.pallas_call(
         middle_kernel,
         in_specs=[pl.BlockSpec(memory_space=pltpu.SMEM)] + [vmem] * 2 + [anywhere] * 5,
         out_specs=[vmem] * 4 + [anywhere] * 3,
         out_shape=[
             shaped(rows, width), shaped(rows, width, kind=full), shaped(width, rows),
-            shaped(8, 16, 3 * HEAD, kind=full), shaped(*up_parts), shaped(*down_parts), shaped(*out_parts),
+            shaped(8, 16, 4 * shard, kind=full), shaped(*up_parts), shaped(*down_parts), shaped(*out_parts),
         ],
         scratch_shapes=[
             held(width, rows), held(width, ff), held(ff, width), held(width, width), held(8, 16, 9 * HEAD),
@@ -1469,7 +1519,8 @@
             held(rows, width, kind=full), held(rows, width), held(rows, width), held(rows, width, kind=full),
             held(rows, width, kind=full), held(8, width, kind=full), held(8, ff, kind=full),
             held(width, ff), held(ff, width), held(width, width), held(*up_parts), held(*down_parts),
-            held(*out_parts), dma((11,)), dma((3, 2, 4)), dma((4, 2, 4)), dma((4, 2, 4)),
+            held(*out_parts), held(4, ff // 32, width), dma((11,)), dma((3, 2, 4)), dma((4, 2, 4)),
+            dma((4, 2, 4)), dma((4,)), dma((4,)),
         ],
         compiler_params=pltpu.CompilerParams(
             vmem_limit_bytes=VMEM_BYTES, collective_id=2, has_side_effects=True
@@ -1577,7 +1628,7 @@
             lengths, grad_attended, saved, packed_grad, rows, weight, grad_resid_one,
             grad_up_weight, grad_down_weight, grad_out_weight,
         )
-        own_vectors = vector_sum[:6].reshape(-1)
+        own_vectors = vector_sum[:3].reshape(-1)
         qkv_out, up_out, down_out, out_out = (g.astype(full) for g in (qkv_out, up_out, down_out, out_out))
     else:
         grad_t = lax.all_to_all(grad_attended, "seq", split_axis=0, concat_axis=1, tiled=True)

time: 243 us -> 240 us (0.988)
    pallas_call x1, Pallas kernels: 106 us -> 99.3 us  [back(): pl.pallas_call(back_kernel, in_specs=[pl.BlockSpec(memory_space=pltpu.SME...]
    pallas_call x1, Pallas kernels: 34.3 us -> 39.1 us  [middle_part(): pl.pallas_call(middle_kernel, in_specs=[pl.BlockSpec(memory_space=pltpu.S...]
where the time goes in v5:
time: 240 us
  Pallas kernels  215 us (90%)
  local copies, waits for them, and re-layouts  14.6 us (6%)
  other arithmetic  6.74 us (3%)
    pallas_call x1, Pallas kernels, back(): pl.pallas_call(back_kernel, in_specs=[pl.BlockSpec(memory_space=pltpu.SME...  99.3 us
    pallas_call x1, Pallas kernels, front(): pl.pallas_call(front_kernel, in_specs=[pl.BlockSpec(memory_space=pltpu.SM...  77.1 us
    pallas_call x1, Pallas kernels, middle_part(): pl.pallas_call(middle_kernel, in_specs=[pl.BlockSpec(memory_space=pltpu.S...  39.1 us
    unnamed x19, local copies, waits for them, and re-layouts  6.31 us
    convert_element_type x4, other arithmetic, per_device(): g.astype(full)  5.89 us
    concatenate x1, local copies, waits for them, and re-layouts, per_device(): packed = jnp.concatenate(vectors)  5.44 us

profile of v5, /device:TPU:9, one launch (start us, length us, event | category | flops | bytes accessed | tf_op | source)
XLA Modules:
  0.0 239.6 jit_solution(16758453579199321539)
XLA Ops:
  0.6 0.0 copy-start.5
  0.7 0.0 copy-start.6
  0.7 0.0 copy-start.1
  1.4 0.1 pad.2.clone
  1.5 5.4 %concatenate.14 = bf16[1152]{0:T(1024)(128)(2,1)S(1)} concatenate(bf16[192]{0:T(256)(128)(2,1)} %param.22, bf16[96]{0:T(256)(128)(2,1)} %param.24, bf16[96]{0:T(256)(128)(2,1)} %param.25, bf16[96]{0:T(256)(128)(2,1)} %param.26, bf16[384]{0:T(512)(128)(2,1)} %param.28, bf16[96]{0:T(256)(128)(2,1)} %param.30, bf16[96]{0:T(256)(128)(2,1)} %param.31, bf16[96]{0:T(256)(128)(2,1)} %param.32), dimensions={0} | concatenate | bytes 4608 | tf_op jit(solution)/shard_map/concatenate | solution.py:1569
  6.9 0.1 reshape.58
  7.0 0.1 broadcast_compare_fusion
  7.1 1.3 copy.45
  8.5 0.1 copy.47
  8.6 0.8 maximum_maximum_fusion.qkv_in
  9.4 0.0 copy-done.5
  9.4 0.0 copy-done.6
  9.4 0.0 copy-done.1
  9.4 1.3 fusion.rows_in.layer_in
  10.7 77.1 %front.1 = (bf16[2048,768]{1,0:T(8,128)(2,1)}, bf16[768,576]{1,0:T(8,128)(2,1)}, bf16[8,112,576]{2,1,0:T(8,128)(2,1)}, bf16[3,128,2048]{2,1,0:T(8,128)(2,1)}, bf...) custom-call(s32[1]{0:T(128)S(6)} %copy.52.length_ref, ...), custom_call_target="tpu_custom_call" | custom-call | tf_op jit(solution)/shard_map/front/pallas_call | solution.py:660
  87.8 39.1 %middle.1 = (bf16[512,768]{1,0:T(8,128)(2,1)}, f32[512,768]{1,0:T(8,128)}, bf16[768,512]{1,0:T(8,128)(2,1)}, f32[8,16,384]{2,1,0:T(8,128)}, bf16[2,4,96,1536]{3,...) custom-call(s32[1]{0:T(128)S(6)} %copy.52.length_ref, ...), custom_call_target="tpu_custom_call" | custom-call | tf_op jit(solution)/shard_map/middle/pallas_call | solution.py:1508
  126.9 99.3 %back.1 = (f32[512,768]{1,0:T(8,128)}, f32[10,768]{1,0:T(8,128)}, f32[10,768]{1,0:T(8,128)}, bf16[96,2304]{1,0:T(8,128)(2,1)}, f32[16,384]{1,0:T(8,128)}, /*inde...) custom-call(s32[1]{0:T(128)S(6)} %copy.52.length_ref, ...), custom_call_target="tpu_custom_call" | custom-call | tf_op jit(solution)/shard_map/back/pallas_call | solution.py:1206
  226.2 0.0 copy-start.4
  226.2 1.5 copy.48
  227.7 0.7 slice.27
  228.4 0.6 slice.36
  229.0 0.6 slice.40
  229.6 0.6 fusion.6
  230.2 1.4 copy.49
  231.7 1.6 convert_element_type.25
  233.3 2.0 convert_element_type.24
  235.4 1.1 convert_element_type.26
  236.5 0.0 copy-done.3
  236.5 1.1 convert_element_type.27
  237.6 0.9 copy.53
  238.4 0.0 copy-done
  238.4 1.1 copy.54
  (11 shorter events, 0.1 us)
Async XLA Ops:
  0.6 8.8 %copy-start.5 = (bf16[1,10,768]{2,1,0:T(8,128)(2,1)S(1)}, bf16[1,10,768]{2,1,0:T(8,128)(2,1)}, u32[]{:S(2)}) copy-start(bf16[1,10,768]{2,1,0:T(8,128)(2,1)} %param.19) | copy-start | bytes 46084
  0.7 8.8 %copy-start.6 = (bf16[1,10,768]{2,1,0:T(8,128)(2,1)S(1)}, bf16[1,10,768]{2,1,0:T(8,128)(2,1)}, u32[]{:S(2)}) copy-start(bf16[1,10,768]{2,1,0:T(8,128)(2,1)} %param.18) | copy-start | bytes 46084
  0.7 8.7 %copy-start.1 = (bf16[512,768]{1,0:T(8,128)(2,1)S(1)}, bf16[512,768]{1,0:T(8,128)(2,1)}, u32[]{:S(2)}) copy-start(bf16[512,768]{1,0:T(8,128)(2,1)} %param.17) | copy-start | bytes 2359300
  226.2 9.2 %copy-start.4 = (bf16[96,3072]{1,0:T(8,128)(2,1)S(1)}, bf16[96,3072]{1,0:T(8,128)(2,1)}, u32[]{:S(2)}) copy-start(bf16[96,3072]{1,0:T(8,128)(2,1)} %get-tuple-element.70) | copy-start | bytes 1769476
  233.3 3.2 %copy-start.3 = (bf16[384,768]{1,0:T(8,128)(2,1)S(1)}, bf16[384,768]{1,0:T(8,128)(2,1)}, u32[]{:S(2)}) copy-start(bf16[384,768]{1,0:T(8,128)(2,1)} %get-tuple-element.71) | copy-start | bytes 1769476
  235.3 2.2 copy-start.2
  236.5 2.0 copy-start

commit v6 on v5

--- a/solution.py
+++ b/solution.py
@@ -262,21 +262,22 @@
     )
 
 
-def greet(place, everyone):
+def greet(place, all_lines):
     barrier = pltpu.get_barrier_semaphore()
     near = [place.core, place.across_y, place.diagonal, place.across_x]
     for where in near:
         pl.semaphore_signal(barrier, inc=1, device_id=where, device_id_type=MESH)
-
-    @pl.when(place.z > 0)
-    def _():
-        pl.semaphore_signal(barrier, inc=1, device_id=place.below, device_id_type=MESH)
-
-    @pl.when(place.z < 3)
-    def _():
-        pl.semaphore_signal(barrier, inc=1, device_id=place.above, device_id_type=MESH)
-
-    ends = jnp.where((place.z == 0) | (place.z == 3), 1, 2)
+    for line in range(4):
+        gap = place.z - line
+        meets = gap != 0 if all_lines else (gap == 1) | (gap == -1)
+
+        @pl.when(meets)
+        def _(line=line):
+            pl.semaphore_signal(
+                barrier, inc=1, device_id=(2 * line + place.x, place.s), device_id_type=MESH
+            )
+
+    ends = 3 if all_lines else jnp.where((place.z == 0) | (place.z == 3), 1, 2)
     pl.semaphore_wait(barrier, len(near) + ends)
 
 
@@ -286,7 +287,7 @@
         (self.z_send, self.z_recv, self.x_send, self.x_recv, self.c_send, self.c_recv,
          self.y_send, self.y_recv, self.d_send, self.d_recv) = sems
 
-    def piece(self, array, source, quarter=None):
+    def piece(self, array, source, quarter=None, pair=False):
         c = self.place.c
         ref = self.whole[array]
         if array == QKV_W:
@@ -297,24 +298,31 @@
             quarter = self.place.s if quarter is None else quarter
             return ref.at[pl.ds(pl.multiple_of(source * rows + quarter * part, part), part)]
         rows, columns = ref.shape[0] // 8, ref.shape[1] // 2
+        count = 2 if pair else 1
         return ref.at[
-            pl.ds(pl.multiple_of(source * rows, rows), rows),
+            pl.ds(pl.multiple_of(source * rows, rows), count * rows),
             pl.ds(pl.multiple_of(c * columns, columns), columns),
         ]
 
     def own_piece(self, array):
+        if array == QKV_W:
+            return self.piece(array, self.place.f)
         ref = self.own[array]
-        if array == QKV_W:
-            return ref
         if array == DOWN_W:
             part = ref.shape[0] // 4
             return ref.at[pl.ds(pl.multiple_of(self.place.s * part, part), part)]
         columns = ref.shape[1] // 2
         return ref.at[:, pl.ds(pl.multiple_of(self.place.c * columns, columns), columns)]
 
+    def z_piece(self, array, relation):
+        source = self.place.source(relation, 0)
+        if array == OUT_W:
+            return self.piece(array, source - self.place.x, pair=True)
+        return self.piece(array, source)
+
     def along_z(self, array, relation, way):
-        here = self.piece(array, self.place.source(relation, 0))
-        src = self.own_piece(array) if relation == OWN else here
+        here = self.z_piece(array, relation)
+        src = self.own_piece(array) if relation == OWN and array != OUT_W else here
         step = abs(offset_of(relation))
         where = self.place.above if way == 0 else self.place.below
         return remote(src, here, self.z_send.at[array, way, step], self.z_recv.at[array, way, step], where)
@@ -331,7 +339,7 @@
     def wait_z(self, array, relation):
         way = 0 if offset_of(relation) < 0 else 1
         step = abs(offset_of(relation)) - 1
-        here = self.piece(array, self.place.source(relation, 0))
+        here = self.z_piece(array, relation)
         where = self.place.below if way == 0 else self.place.above
         remote(
             here, here, self.z_send.at[array, way, step], self.z_recv.at[array, way, step], where
@@ -351,7 +359,10 @@
         )
 
     def to_core(self, array, relation, column):
-        here = self.piece(array, self.place.source(relation, column))
+        if array == OUT_W and relation != OWN:
+            here = self.z_piece(array, relation)
+        else:
+            here = self.piece(array, self.place.source(relation, column))
         return remote(
             here, here, self.c_send.at[array, relation, column], self.c_recv.at[array, relation, column],
             self.place.core,
@@ -392,13 +403,24 @@
                 self.wait_z(array, relation)
             for way, holds in self.z_ways(relation):
                 pl.when(holds)(lambda way=way: self.along_z(array, relation, way).start())
-            self.over_x(array, relation).start()
+            if array != OUT_W:
+                self.over_x(array, relation).start()
             if array != QKV_W and relation != OWN:
                 self.to_core(array, relation, 0).start()
                 if array == DOWN_W:
                     self.over_y(relation, 0).start()
 
         self.when(relation, action)
+
+    def cross_out(self):
+        self.over_x(OUT_W, OWN).start()
+
+    def pair_out(self, own_copy):
+        own_copy.wait()
+        self.from_x(OUT_W, OWN).wait_recv()
+        self.to_core(OUT_W, OWN, 1).start()
+        for way, holds in self.z_ways(OWN):
+            pl.when(holds)(lambda way=way: self.along_z(OUT_W, OWN, way).start())
 
     def arrive_x(self, array, relation):
         def action():
@@ -421,13 +443,14 @@
     def finish(self, array):
         for relation in range(RELATIONS):
             def action():
-                self.over_x(array, relation).wait_send()
+                if array != OUT_W or relation == OWN:
+                    self.over_x(array, relation).wait_send()
                 for way, holds in self.z_ways(relation):
                     pl.when(holds)(lambda way=way: self.along_z(array, relation, way).wait_send())
                 if array == QKV_W:
                     return
                 for column in range(2):
-                    if (relation, column) == (OWN, 0):
+                    if (relation, column) == (OWN, 0) or (array == OUT_W and relation != OWN and column == 1):
                         continue
                     self.to_core(array, relation, column).wait()
                     if array == DOWN_W:
@@ -438,20 +461,50 @@
 
 
 def front_kernel(
-    length_ref, rows_in, qkv_in, up_in, down_in, out_in,
-    rows_ref, weight_ref, pieces, q_x, k_t, k_wide, v_wide, mixed, row_stats, up_full, down_full, out_full,
-    attended,
-    v_x, mixed_low, row_send, row_recv, far_send, far_recv, mix_send, mix_recv, local_sem, *gather_sems,
+    length_ref, tokens, read_rows, write_rows, qkv_in, vectors_in, up_in, down_in, out_in,
+    small, up_bias, rows_out, weight_out, q_out, k_out, k_wide_out, v_wide_out, mixed_out, stats_out, up_full,
+    down_full, out_full, attended,
+    rows_ref, weight_ref, pieces, memory, q_x, k_t, k_wide, v_wide, v_x, mixed, mixed_low, row_stats,
+    row_send, row_recv, far_send, far_recv, mix_send, mix_recv, local_sem, save_sem, head_sem, *gather_sems,
 ):
     place = Place()
     slot_rows, width = rows_ref.shape
-    local_rows = rows_in.shape[0]
+    local_rows = tokens.shape[0]
     head_cols = k_t.shape[0]
     heads = head_cols // HEAD
-    own_shards = {UP_W: up_in, DOWN_W: down_in, OUT_W: out_in, QKV_W: qkv_in}
+    shard = width // 8
+    length = length_ref[0]
+    own_shards = {UP_W: up_in, DOWN_W: down_in, OUT_W: out_in}
     whole = {UP_W: up_full, DOWN_W: down_full, OUT_W: out_full, QKV_W: pieces}
     gather = Gather(place, own_shards, whole, gather_sems)
-    greet(place, None)
+
+    memory[...] = jnp.zeros_like(memory)
+    memory[:MEM, :] = read_rows[...]
+    memory[16 : 16 + MEM, :] = write_rows[...]
+    line = lax.broadcasted_iota(jnp.int32, (local_rows, 32), 1)
+    at = place.s * local_rows + lax.broadcasted_iota(jnp.int32, (local_rows, 32), 0)
+    wanted = jnp.where(line < 16, line, length - MEM + line - 16)
+    used = (line < MEM) | ((line >= 16) & (line < 16 + MEM))
+    pick = jnp.where(used & (wanted == at), 1.0, 0.0)
+    taken = mul(pick.astype(low), memory[...]).astype(low)
+    is_memory = jnp.sum(pick, axis=1, keepdims=True) > 0.5
+    own_start = pl.multiple_of(place.s * local_rows, local_rows)
+    rows_ref[pl.ds(own_start, local_rows), :] = jnp.where(is_memory, taken, tokens[...])
+    for member in range(4):
+
+        @pl.when(place.s == member)
+        def _(member=member):
+            for h in range(heads):
+                for kind in range(3):
+                    start = kind * width + (member * heads + h) * HEAD
+                    to = (3 * h + kind) * HEAD
+                    pieces[place.f, :, to : to + HEAD] = qkv_in[:, start : start + HEAD]
+
+    columns = 3 * head_cols
+    pieces[place.f, :, columns:] = jnp.zeros((shard, HEAD), low)
+    for line in range(18):
+        pieces[place.f, line : line + 1, columns:] = vectors_in[:, line * HEAD : (line + 1) * HEAD].astype(low)
+    greet(place, False)
 
     halves = 2
     part = local_rows // halves
@@ -461,10 +514,8 @@
 
     def send_rows(half, index):
         where = (place.core, place.across_y)[index]
-        return remote(
-            rows_in.at[pl.ds(half * part, part)], rows_ref.at[rows_of(place.s, half)],
-            row_send.at[index, half], row_recv.at[index, half], where,
-        )
+        here = rows_ref.at[rows_of(place.s, half)]
+        return remote(here, here, row_send.at[index, half], row_recv.at[index, half], where)
 
     def rows_from(half, index):
         member = (2 * place.y + 1 - place.c, 2 * (1 - place.y) + place.c)[index]
@@ -476,11 +527,6 @@
         flip = place.c if not arriving else 1 - place.c
         here = rows_ref.at[rows_of(2 * (1 - place.y) + flip, half)]
         return remote(here, here, far_send.at[half], far_recv.at[half], place.core)
-
-    for half in range(halves):
-        send_rows(half, 1).start()
-        send_rows(half, 0).start()
-    gather.arrive_z(QKV_W, OWN)
 
     def own_copies():
         copies = []
@@ -490,40 +536,38 @@
                 own_shards[array], whole[array].at[pl.ds(pl.multiple_of(place.f * rows, rows), rows)],
                 local_sem.at[index],
             ))
-        copies.append(pltpu.make_async_copy(qkv_in, pieces.at[place.f], local_sem.at[3]))
-        copies.append(pltpu.make_async_copy(
-            rows_in, rows_ref.at[pl.ds(pl.multiple_of(place.s * local_rows, local_rows), local_rows)],
-            local_sem.at[4],
-        ))
         return copies
 
+    gather.arrive_z(QKV_W, OWN)
+    for half in range(halves):
+        send_rows(half, 1).start()
+        send_rows(half, 0).start()
+    gather.cross_out()
+    gather.arrive_z(UP_W, OWN)
     for copy in own_copies():
         copy.start()
-
     for relation in (1, 4):
         gather.arrive_z(QKV_W, relation)
-    gather.arrive_z(UP_W, OWN)
+    gather.pair_out(own_copies()[2])
+    rows_from(0, 1).wait_recv()
+    pass_rows(0, False).start()
     for relation in (2, 5):
         gather.arrive_z(QKV_W, relation)
-    gather.arrive_z(OUT_W, OWN)
     gather.arrive_z(DOWN_W, OWN)
-    rows_from(0, 1).wait_recv()
-    pass_rows(0, False).start()
+    for relation in (1, 4):
+        gather.arrive_z(UP_W, relation)
     for relation in (3, 6):
         gather.arrive_z(QKV_W, relation)
-    for relation in (1, 4):
-        gather.arrive_z(UP_W, relation)
     for relation in range(RELATIONS):
         gather.arrive_x(QKV_W, relation)
-    for copy in own_copies()[3:]:
-        copy.wait()
-
-    shard = weight_ref.shape[0] // 8
+
     for source in range(8):
-        weight_ref[source * shard : (source + 1) * shard, :] = pieces[source, :shard, :]
-    bias_q = jnp.transpose(pieces[place.s, shard : shard + 16, :].astype(full))[:head_cols, 0:1]
-    bias_v = jnp.transpose(pieces[4 + place.s, shard : shard + 16, :].astype(full))[:head_cols, 0:1]
-    length = length_ref[0]
+        weight_ref[source * shard : (source + 1) * shard, :] = pieces[source, :, :columns]
+    tile = slice(columns - HEAD, columns + HEAD)
+    bias_q = jnp.transpose(pieces[place.s, 0:16, tile].astype(full))[HEAD:]
+    bias_v = jnp.transpose(pieces[4 + place.s, 0:16, tile].astype(full))[HEAD:]
+    bias_q = jnp.concatenate([bias_q[:, h : h + 1] for h in range(heads)], axis=0)
+    bias_v = jnp.concatenate([bias_v[:, h : h + 1] for h in range(heads)], axis=0)
 
     def project(member):
         start = pl.multiple_of(member * local_rows, local_rows)
@@ -541,43 +585,82 @@
     for relation in (1, 4):
         gather.arrive_z(OUT_W, relation)
         gather.arrive_z(DOWN_W, relation)
+
+    def scatter_vector(target, index, size, first):
+        for source in range(8):
+            done = 0
+            while done < size:
+                line, lane = divmod(first + done, HEAD)
+                count = min(HEAD - lane, size - done)
+                target[index : index + 1, source * size + done : source * size + done + count] = pieces[
+                    source, line : line + 1, columns + lane : columns + lane + count
+                ].astype(full)
+                done += count
+
+    for index, first in enumerate((2, 3, 4, 9, 10, 11)):
+        scatter_vector(small, index, shard, first * shard)
+    scatter_vector(up_bias, 0, 4 * shard, 5 * shard)
     for half in range(halves):
         pass_rows(half, True).wait_recv()
     project(2 * (1 - place.y) + 1 - place.c)
 
+    def saves():
+        pairs = [(rows_ref, rows_out), (weight_ref, weight_out), (k_t, k_out), (k_wide, k_wide_out), (v_wide, v_wide_out)]
+        pairs += [(q_x.at[h, pl.ds(0, HEAD)], q_out.at[h]) for h in range(heads)]
+        return [pltpu.make_async_copy(src, dst, save_sem.at[index]) for index, (src, dst) in enumerate(pairs)]
+
+    for save in saves():
+        save.start()
+
+    def head_saves(h):
+        own = pl.ds(h * HEAD, HEAD)
+        return [
+            pltpu.make_async_copy(mixed.at[own], mixed_out.at[own], head_sem.at[h, 0]),
+            pltpu.make_async_copy(row_stats.at[h], stats_out.at[h], head_sem.at[h, 1]),
+        ]
+
     def chores(step):
         if step == 0:
-            gather.arrive_x(UP_W, OWN)
             for relation in (2, 5):
                 gather.arrive_z(UP_W, relation)
-        elif step == 2:
+        elif step == 1:
+            gather.arrive_x(UP_W, OWN)
+            gather.arrive_x(DOWN_W, OWN)
+        elif step == 3:
             for relation in (2, 5):
                 gather.arrive_z(OUT_W, relation)
                 gather.arrive_z(DOWN_W, relation)
-            gather.arrive_x(OUT_W, OWN)
-            gather.arrive_x(DOWN_W, OWN)
         elif step == 4:
             for relation in (1, 4):
                 gather.arrive_x(UP_W, relation)
                 gather.arrive_y(relation, 0)
+            for save in head_saves(0):
+                save.start()
+        elif step == 5:
             gather.arrive_y(OWN, 1)
         elif step == 6:
             for relation in (3, 6):
                 gather.arrive_z(UP_W, relation)
+        elif step == 7:
             for relation in (1, 4):
-                gather.arrive_x(OUT_W, relation)
                 gather.arrive_x(DOWN_W, relation)
         elif step == 8:
+            for relation in (2, 5):
+                gather.arrive_x(UP_W, relation)
+            for save in head_saves(1):
+                save.start()
+        elif step == 9:
             for relation in (3, 6):
                 gather.arrive_z(OUT_W, relation)
                 gather.arrive_z(DOWN_W, relation)
             for relation in (2, 5):
-                gather.arrive_x(UP_W, relation)
                 gather.arrive_y(relation, 0)
         elif step == 10:
             for relation in (2, 5):
-                gather.arrive_x(OUT_W, relation)
                 gather.arrive_x(DOWN_W, relation)
+        elif step == 11:
+            for relation in (3, 6):
+                gather.arrive_x(UP_W, relation)
             for relation in (1, 4):
                 gather.arrive_y(relation, 1)
 
@@ -611,7 +694,7 @@
             keep_mixed(h).start()
 
     def step(index, carry):
-        for when in range(0, 12, 2):
+        for when in range(12):
             pl.when(index == when)(lambda when=when: chores(when))
         h, turn = index // turns, lax.rem(index, turns)
         start = pl.multiple_of(place.member(turn) * local_rows, local_rows)
@@ -625,17 +708,18 @@
 
     lax.fori_loop(0, heads * turns, step, 0)
     pass_on(heads * turns - 1)
+    for save in head_saves(2):
+        save.start()
     for relation in (3, 6):
-        gather.arrive_x(UP_W, relation)
-        gather.arrive_x(OUT_W, relation)
         gather.arrive_x(DOWN_W, relation)
-    for relation in (3, 6):
-        gather.arrive_y(relation, 0)
-    for relation in (2, 5, 3, 6):
+    for relation in (2, 5):
         gather.arrive_y(relation, 1)
+    for column in range(2):
+        for relation in (3, 6):
+            gather.arrive_y(relation, column)
     for array in (UP_W, OUT_W, DOWN_W, QKV_W):
         gather.finish(array)
-    for copy in own_copies()[:3]:
+    for copy in own_copies()[:2]:
         copy.wait()
     for half in range(halves):
         for index in range(2):
@@ -646,40 +730,47 @@
             send_mixed(h, turn).wait_send()
             send_mixed(h, turn, True).wait_recv()
         keep_mixed(h).wait()
-
-
-def front(lengths, layer_in, qkv_piece, up_weight, down_weight, out_weight):
-    local_rows, width = layer_in.shape
+        for save in head_saves(h):
+            save.wait()
+    for save in saves():
+        save.wait()
+
+
+def front(lengths, tokens, read_rows, write_rows, qkv_shard, vectors, up_weight, down_weight, out_weight):
+    local_rows, width = tokens.shape
     slot_rows = local_rows * 4
     head_cols = width // 4
     heads = head_cols // HEAD
+    shard = width // 8
     vmem = pl.BlockSpec(memory_space=pltpu.VMEM)
     anywhere = pl.BlockSpec(memory_space=pl.ANY)
     dma = pltpu.SemaphoreType.DMA
     hidden = up_weight.shape[1]
+
+    def held(*shape, kind=low):
+        return pltpu.VMEM(shape, kind)
+
+    def shaped(*shape, kind=low):
+        return jax.ShapeDtypeStruct(shape, kind)
+
     return pl.pallas_call(
         front_kernel,
-        in_specs=[pl.BlockSpec(memory_space=pltpu.SMEM)] + [vmem] * 5,
-        out_specs=[vmem] * 9 + [anywhere] * 4,
+        in_specs=[pl.BlockSpec(memory_space=pltpu.SMEM)] + [vmem] * 8,
+        out_specs=[vmem] * 2 + [anywhere] * 12,
         out_shape=[
-            jax.ShapeDtypeStruct((slot_rows, width), low),
-            jax.ShapeDtypeStruct((width, 3 * head_cols), low),
-            jax.ShapeDtypeStruct((8,) + qkv_piece.shape, low),
-            jax.ShapeDtypeStruct((heads, WIDE, slot_rows), low),
-            jax.ShapeDtypeStruct((head_cols, slot_rows), low),
-            jax.ShapeDtypeStruct((heads, slot_rows, WIDE), low),
-            jax.ShapeDtypeStruct((heads, slot_rows, WIDE), low),
-            jax.ShapeDtypeStruct((head_cols, slot_rows), full),
-            jax.ShapeDtypeStruct((heads, 8, slot_rows), full),
-            jax.ShapeDtypeStruct((width, hidden), low),
-            jax.ShapeDtypeStruct((hidden, width), low),
-            jax.ShapeDtypeStruct((width, width), low),
-            jax.ShapeDtypeStruct((width, local_rows), low),
+            shaped(8, width, kind=full), shaped(8, hidden, kind=full),
+            shaped(slot_rows, width), shaped(width, 3 * head_cols), shaped(heads, HEAD, slot_rows),
+            shaped(head_cols, slot_rows), shaped(heads, slot_rows, WIDE), shaped(heads, slot_rows, WIDE),
+            shaped(head_cols, slot_rows, kind=full), shaped(heads, 8, slot_rows, kind=full),
+            shaped(width, hidden), shaped(hidden, width), shaped(width, width), shaped(width, local_rows),
         ],
         scratch_shapes=[
-            pltpu.VMEM((heads, WIDE, slot_rows), low),
-            pltpu.VMEM((head_cols, slot_rows), low),
-            dma((2, 2)), dma((2, 2)), dma((2,)), dma((2,)), dma((heads, 4)), dma((heads, 4)), dma((5,)),
+            held(slot_rows, width), held(width, 3 * head_cols), held(8, shard, 3 * head_cols + HEAD),
+            held(32, width), held(heads, WIDE, slot_rows), held(head_cols, slot_rows),
+            held(heads, slot_rows, WIDE), held(heads, slot_rows, WIDE), held(heads, WIDE, slot_rows),
+            held(head_cols, slot_rows, kind=full), held(head_cols, slot_rows), held(heads, 8, slot_rows, kind=full),
+            dma((2, 2)), dma((2, 2)), dma((2,)), dma((2,)), dma((heads, 4)), dma((heads, 4)), dma((3,)),
+            dma((5 + heads,)), dma((heads, 2)),
             dma((4, 2, 3)), dma((4, 2, 3)), dma((4, 7)), dma((4, 7)), dma((3, 7, 2)), dma((3, 7, 2)),
             dma((7, 2)), dma((7, 2)), dma((7, 2)), dma((7, 2)),
         ],
@@ -687,7 +778,7 @@
             vmem_limit_bytes=VMEM_BYTES, collective_id=0, has_side_effects=True
         ),
         name="front",
-    )(lengths, layer_in, qkv_piece, up_weight, down_weight, out_weight)
+    )(lengths, tokens, read_rows, write_rows, qkv_shard, vectors, up_weight, down_weight, out_weight)
 
 
 DW_FIRST = 3
@@ -790,7 +881,31 @@
                         self.add_z(array, 1, line)
                     self.along_z(array, 1, line).start()
 
+    def to_line(self, array, line):
+        where = (2 * line + self.place.x, self.place.s)
+        return remote(
+            self.slot(array, line), self.cut(array, self.from_z[array].at[self.place.z]),
+            self.z_send.at[array, 0, line], self.z_recv.at[array, 0, self.place.z], where,
+        )
+
+    def fling(self, array, lines=LINES):
+        for line in lines:
+            pl.when(self.place.z != line)(lambda line=line: self.to_line(array, line).start())
+
     def settle(self, array):
+        if array >= DOWN_W:
+            slot = self.slot(array, self.place.z)
+            for line in range(4):
+
+                @pl.when(self.place.z != line)
+                def _(line=line):
+                    came = self.cut(array, self.from_z[array].at[line])
+                    remote(
+                        came, came, self.z_send.at[array, 0, line], self.z_recv.at[array, 0, line], self.place.core
+                    ).wait_recv()
+                    slot[...] = add_low(slot[...], came[...])
+
+            return
         for line in range(4):
 
             @pl.when(self.place.z == line)
@@ -804,8 +919,11 @@
         for line in range(4):
             if array != OUT_W or line == 0:
                 self.over_x(array, line).wait_send()
-            pl.when(self.place.z < line)(lambda line=line: self.along_z(array, 0, line).wait_send())
-            pl.when(self.place.z > line)(lambda line=line: self.along_z(array, 1, line).wait_send())
+            if array >= DOWN_W:
+                pl.when(self.place.z != line)(lambda line=line: self.to_line(array, line).wait_send())
+            else:
+                pl.when(self.place.z < line)(lambda line=line: self.along_z(array, 0, line).wait_send())
+                pl.when(self.place.z > line)(lambda line=line: self.along_z(array, 1, line).wait_send())
             if array == DOWN_W:
                 self.over_y(line).wait_send()
 
@@ -867,7 +985,7 @@
         sums[DW_FIRST + h], from_x[DW_FIRST + h] = dw.at[h], dw_x.at[h]
         from_z[DW_FIRST + h] = dw_z.at[h]
     reduce = Reduce(place, given, sums, down_y, from_x, from_z, sems)
-    greet(place, None)
+    greet(place, True)
 
     peers = (place.across_y, place.diagonal, place.core)
 
@@ -886,22 +1004,24 @@
     def saved_loads(h):
         own = pl.ds(h * HEAD, HEAD)
         pairs = (
-            (k_wide_in.at[h], k_wide.at[h]), (q_in.at[h, pl.ds(0, HEAD)], q_x.at[h]), (v_wide_in.at[h], v_wide.at[h]),
+            (k_wide_in.at[h], k_wide.at[h]), (q_in.at[h], q_x.at[h]), (v_wide_in.at[h], v_wide.at[h]),
             (mixed_in.at[own], mixed.at[own]), (stats_in.at[h], row_stats.at[h]), (k_in.at[own], k_t.at[own]),
         )
         return [pltpu.make_async_copy(src, dst, saved_sem.at[h, i]) for i, (src, dst) in enumerate(pairs)]
+
+    def sum_loads(array):
+        return [reduce.load(array, 0, line, mine_sem.at[array, line]) for line in LINES]
 
     for turn in range(3):
         send_grad(turn).start()
+    for load in sum_loads(OUT_W):
+        load.start()
     for load in saved_loads(0):
         load.start()
     loads = []
     for index, (src, dst) in enumerate(((rows_in, rows_ref), (weight_in, weight_ref), (resid_in, resid_ref))):
         loads.append(pltpu.make_async_copy(src, dst, local_sem.at[index]))
 
-    def sum_loads(array):
-        return [reduce.load(array, 0, line, mine_sem.at[array, line]) for line in LINES]
-
     def send_x(array, lines=LINES):
         for line in lines:
             reduce.over_x(array, line).start()
@@ -910,7 +1030,7 @@
     for line in LINES:
         reduce.over_y(line).start()
     send_x(DOWN_W)
-    for array in (OUT_W, UP_W, DOWN_W):
+    for array in (UP_W, DOWN_W):
         for load in sum_loads(array):
             load.start()
     for load in loads:
@@ -986,9 +1106,6 @@
     def chores(index):
         if index == 1:
             send_grad(2, True).wait_recv()
-            for load in sum_loads(OUT_W):
-                load.wait()
-            reduce.hop(OUT_W, 0)
         elif index == 2:
             send_grad(1, True).wait_recv()
             for array in (UP_W, DOWN_W):
@@ -996,17 +1113,19 @@
                     load.wait()
             take_x(UP_W, (3,))
             reduce.hop(UP_W, 0, (3,))
+            reduce.hop(OUT_W, 1, (3, 0))
         elif index == 3:
             send_grad(0, True).wait_recv()
-            reduce.hop(OUT_W, 1)
+            reduce.hop(OUT_W, 1, (2, 1))
         elif index == 4:
             for load in saved_loads(1):
                 load.wait()
             weight_part(0)
             take_x(UP_W, (0,))
             reduce.hop(UP_W, 0, (0,))
+            reduce.hop(OUT_W, 2)
         elif index == 5:
-            reduce.hop(OUT_W, 2)
+            reduce.hop(UP_W, 1, (3,))
         elif index == 6:
             for line in LINES:
                 reduce.add_y(line)
@@ -1015,28 +1134,27 @@
             reduce.settle(OUT_W)
             reduce.over_x(OUT_W, 0).start()
         elif index == 7:
-            reduce.hop(UP_W, 1, (3, 0))
+            reduce.hop(UP_W, 1, (0,))
+            take_x(UP_W, (1,))
+            reduce.hop(UP_W, 0, (1,))
         elif index == 8:
             for load in saved_loads(2):
                 load.wait()
             weight_part(1)
-            take_x(UP_W, (1,))
-            reduce.hop(UP_W, 0, (1,))
+            reduce.hop(UP_W, 2, (3,))
         elif index == 9:
-            reduce.hop(UP_W, 2)
-            reduce.hop(UP_W, 1, (2,))
+            reduce.hop(UP_W, 2, (0,))
+            reduce.hop(UP_W, 1, (2, 1))
             take_x(DOWN_W, (3, 0))
-            reduce.hop(DOWN_W, 0, (3, 0))
+            reduce.fling(DOWN_W, (3, 0))
         elif index == 10:
-            reduce.hop(UP_W, 1, (1,))
             take_x(DOWN_W, (2,))
-            reduce.hop(DOWN_W, 0, (2,))
+            reduce.fling(DOWN_W, (2,))
         elif index == 11:
+            take_x(DOWN_W, (1,))
+            reduce.fling(DOWN_W, (1,))
             reduce.settle(UP_W)
             sum_y(UP_W).start()
-            take_x(DOWN_W, (1,))
-            reduce.hop(DOWN_W, 0, (1,))
-            reduce.hop(DOWN_W, 1, (3, 0))
 
     def step(index, carry):
         for when in range(1, 12):
@@ -1055,6 +1173,9 @@
 
         return carry
 
+    for load in sum_loads(OUT_W):
+        load.wait()
+    reduce.hop(OUT_W, 0)
     for load in saved_loads(0):
         load.wait()
     lax.fori_loop(0, heads * turns, step, 0)
@@ -1103,36 +1224,25 @@
     memory = Spread(place, memory_all, memory_own, share_send.at[DW_FIRST + heads], share_recv.at[DW_FIRST + heads])
     memory.start()
     take_x(first)
-    reduce.hop(first, 0)
+    reduce.fling(first)
     reduce.add_x(OUT_W, 0)
     sum_y(OUT_W).start()
     for half in range(halves):
         rows = slice(half * part, (half + 1) * part)
         near_send[1, rows, :] = part_for(2, half).astype(low)
         share_near(1, half).start()
-    reduce.hop(DOWN_W, 1, (2, 1))
-    reduce.hop(DOWN_W, 2)
     take_x(second)
-    reduce.hop(second, 0)
+    reduce.fling(second)
+    reduce.settle(DOWN_W)
+    spread_of(DOWN_W).start()
     take_x(last)
-    reduce.hop(last, 0)
-    reduce.hop(first, 1)
+    reduce.fling(last)
     add_last(UP_W)
     for half in range(halves):
         resid_ref[half * part : (half + 1) * part, :] += part_for(3, half)
-    reduce.hop(second, 1)
-    reduce.hop(first, 2)
-    reduce.hop(last, 1)
-    reduce.settle(DOWN_W)
-    spread_of(DOWN_W).start()
-    reduce.hop(second, 2)
-    reduce.settle(first)
-    spread_of(first).start()
-    reduce.hop(last, 2)
-    reduce.settle(second)
-    spread_of(second).start()
-    reduce.settle(last)
-    spread_of(last).start()
+    for array in (first, second, last):
+        reduce.settle(array)
+        spread_of(array).start()
     add_last(OUT_W)
     memory.pass_on()
     for h in (heads - 1, 0, 1):
@@ -1226,7 +1336,7 @@
             held(4, shard, half), held(4, 2, shard, small), held(4, piece, width),
             held(heads, 8, *tall), held(4, piece, width),
             held(4, shard, half), held(shard, small), held(4, piece, width), held(heads, 4, *tall),
-            held(2, 4, shard, half), held(2, 4, 2, shard, small), held(2, 4, piece, width), held(heads, 2, 4, *tall),
+            held(2, 4, shard, half), held(2, 4, 2, shard, small), held(4, piece, width), held(heads, 4, *tall),
             held(shard, half), held(shard, small), held(shard, half), held(shard, small),
             held(4, piece, width), held(heads, 4, *tall),
             held(2, local_rows, width), held(2, local_rows, width), held(local_rows, width),
@@ -1270,14 +1380,14 @@
 
 
 def middle_kernel(
-    length_ref, layer_in, cotangent, pieces, attended_in, up_in, down_in, out_in,
+    length_ref, cotangent, small, up_bias, rows_in, attended_in, up_in, down_in, out_in,
     output, resid_out, grad_own, vector_out, up_out, down_out, out_out,
-    attended, up_w, down_w, out_w, vectors, small, up_bias, hidden, slope, normed_one, middle_low, grad_down,
+    layer_in, attended, up_w, down_w, out_w, hidden, slope, normed_one, middle_low, grad_down,
     grad_two, grad_mid, totals, up_total, up_grad, down_grad, out_grad, up_sum, down_sum, out_sum,
     from_y, load_sem, save_sem, c_send, c_recv, y_send, y_recv,
 ):
     place = Place()
-    rows, width = layer_in.shape
+    rows, width = cotangent.shape
     ff = up_w.shape[1]
     chunk = ff // 4
     shard = width // 8
@@ -1295,7 +1405,9 @@
         return pltpu.make_async_copy(down_in.at[chunk_lanes(j)], down_w.at[chunk_lanes(j)], load_sem.at[4 + j])
 
     first_loads = [
-        pltpu.make_async_copy(pieces.at[:, pl.ds(shard, 16)], vectors, load_sem.at[8]),
+        pltpu.make_async_copy(
+            rows_in.at[pl.ds(pl.multiple_of(place.s * rows, rows), rows)], layer_in, load_sem.at[8]
+        ),
         pltpu.make_async_copy(attended_in, attended, load_sem.at[9]),
         pltpu.make_async_copy(out_in, out_w, load_sem.at[10]),
     ]
@@ -1304,20 +1416,10 @@
     for j in range(4):
         up_load(j).start()
         down_load(j).start()
-    first_loads[0].wait()
-    spots = ((0, 192), (0, 288), (0, 384), (1, 288), (1, 384), (1, 480))
-    for source in range(8):
-        for index, (line, start) in enumerate(spots):
-            small[index : index + 1, source * shard : (source + 1) * shard] = vectors[
-                source, line : line + 1, start : start + shard
-            ].astype(full)
-        base = source * 4 * shard
-        up_bias[0:1, base : base + shard] = vectors[source, 0:1, 480:576].astype(full)
-        up_bias[0:1, base + shard : base + 4 * shard] = vectors[source, 1:2, 0:288].astype(full)
     out_bias, gain_one, shift_one = small[0:1, :], small[1:2, :], small[2:3, :]
     down_bias, gain_two, shift_two = small[3:4, :], small[4:5, :], small[5:6, :]
-    first_loads[1].wait()
-    first_loads[2].wait()
+    for load in first_loads:
+        load.wait()
 
     branch = mul(attended[...], out_w[...], TN)
     normed, factor_one = statistics(layer_in[...].astype(full) + branch + out_bias)
@@ -1490,8 +1592,8 @@
             down_save(column, line).wait()
 
 
-def middle_part(lengths, layer_in, cotangent, pieces, attended, up_full, down_full, out_full):
-    rows, width = layer_in.shape
+def middle_part(lengths, cotangent, small, up_bias, rows_full, attended, up_full, down_full, out_full):
+    rows, width = cotangent.shape
     ff = up_full.shape[1]
     shard = width // 8
     vmem = pl.BlockSpec(memory_space=pltpu.VMEM)
@@ -1507,15 +1609,14 @@
     up_parts, down_parts, out_parts = (2, 4, shard, ff // 2), (2, 4, 2, ff // 32, width), (4, 2, shard, width // 2)
     return pl.pallas_call(
         middle_kernel,
-        in_specs=[pl.BlockSpec(memory_space=pltpu.SMEM)] + [vmem] * 2 + [anywhere] * 5,
+        in_specs=[pl.BlockSpec(memory_space=pltpu.SMEM)] + [vmem] * 3 + [anywhere] * 5,
         out_specs=[vmem] * 4 + [anywhere] * 3,
         out_shape=[
             shaped(rows, width), shaped(rows, width, kind=full), shaped(width, rows),
             shaped(8, 16, 4 * shard, kind=full), shaped(*up_parts), shaped(*down_parts), shaped(*out_parts),
         ],
         scratch_shapes=[
-            held(width, rows), held(width, ff), held(ff, width), held(width, width), held(8, 16, 9 * HEAD),
-            held(8, width, kind=full), held(8, ff, kind=full), held(rows, ff), held(rows, ff, kind=full),
+            held(rows, width), held(width, rows), held(width, ff), held(ff, width), held(width, width), held(rows, ff), held(rows, ff, kind=full),
             held(rows, width, kind=full), held(rows, width), held(rows, width), held(rows, width, kind=full),
             held(rows, width, kind=full), held(8, width, kind=full), held(8, ff, kind=full),
             held(width, ff), held(ff, width), held(width, width), held(*up_parts), held(*down_parts),
@@ -1526,7 +1627,49 @@
             vmem_limit_bytes=VMEM_BYTES, collective_id=2, has_side_effects=True
         ),
         name="middle",
-    )(lengths, layer_in, cotangent, pieces, attended, up_full, down_full, out_full)
+    )(lengths, cotangent, small, up_bias, rows_full, attended, up_full, down_full, out_full)
+
+
+def finish_kernel(
+    output_in, input_in, qkv_in, vector_in, up_in, down_in, out_in, read_in, write_in,
+    output, input_out, read_out, write_out, qkv_out, qv_out, out_out, out_b, gain_one, shift_one, up_out, up_b,
+    down_out, down_b, gain_two, shift_two,
+):
+    shard = qkv_out.shape[0]
+    output[...] = output_in[...]
+    input_out[...] = input_in[...]
+    read_out[...] = read_in[...]
+    write_out[...] = write_in[...]
+    for given, out in ((qkv_in, qkv_out), (up_in, up_out), (down_in, down_out), (out_in, out_out)):
+        out[...] = given[...].astype(full)
+    qv_out[...] = vector_in[0:1, : 2 * shard]
+    out_b[...] = vector_in[0:1, 2 * shard : 3 * shard]
+    gain_one[...] = vector_in[0:1, 3 * shard :]
+    shift_one[...] = vector_in[1:2, :shard]
+    up_b[:, : 3 * shard] = vector_in[1:2, shard:]
+    up_b[:, 3 * shard :] = vector_in[2:3, :shard]
+    down_b[...] = vector_in[2:3, shard : 2 * shard]
+    gain_two[...] = vector_in[2:3, 2 * shard : 3 * shard]
+    shift_two[...] = vector_in[2:3, 3 * shard :]
+
+
+def finish(output, input_grad, qkv_grad, vectors, up_grad, down_grad, out_grad, grad_read, grad_write):
+    shard = qkv_grad.shape[0]
+
+    def shaped(*shape, kind=full):
+        return jax.ShapeDtypeStruct(shape, kind)
+
+    line = shaped(1, shard)
+    return pl.pallas_call(
+        finish_kernel,
+        out_shape=[
+            shaped(*output.shape, kind=low), shaped(*input_grad.shape), shaped(*grad_read.shape),
+            shaped(*grad_write.shape), shaped(*qkv_grad.shape), shaped(1, 2 * shard), shaped(*out_grad.shape),
+            line, line, line, shaped(*up_grad.shape), shaped(1, 4 * shard), shaped(*down_grad.shape), line, line, line,
+        ],
+        compiler_params=pltpu.CompilerParams(vmem_limit_bytes=VMEM_BYTES),
+        name="finish",
+    )(output, input_grad, qkv_grad, vectors, up_grad, down_grad, out_grad, grad_read, grad_write)
 
 
 def normalize(values, gain_vec, shift_vec):
@@ -1537,6 +1680,33 @@
 
 def column_sums(values):
     return jnp.sum(values, axis=0, dtype=full)
+
+
+def on_block(
+    tokens, read_rows, write_rows, lengths, qkv_weight, vectors, out_weight, up_weight, down_weight, cotangent
+):
+    total = sum(vector.shape[0] for vector in vectors)
+    packed, start = jnp.zeros((1, total), full), 0
+    for vector in vectors:
+        size = vector.shape[0]
+        packed = packed + jnp.pad(vector.astype(full).reshape(1, -1), ((0, 0), (start, total - start - size)))
+        start += size
+    (small, up_bias, rows, weight, q_t, k_t, k_wide, v_wide, mixed, row_stats, up_full, down_full, out_full,
+     attended) = front(
+        lengths, tokens, read_rows, write_rows, qkv_weight, packed, up_weight, down_weight, out_weight
+    )
+    output, resid, grad_own, vector_parts, up_parts, down_parts, out_parts = middle_part(
+        lengths, cotangent, small, up_bias, rows, attended, up_full, down_full, out_full
+    )
+    saved = (q_t, k_t, k_wide, v_wide, mixed, row_stats)
+    input_grad, grad_read, grad_write, qkv_grad, vector_sum, up_grad, down_grad, out_grad = back(
+        lengths, grad_own, saved, vector_parts, rows, weight, resid, up_parts, down_parts, out_parts
+    )
+    results = finish(
+        output, input_grad, qkv_grad, vector_sum, up_grad, down_grad, out_grad, grad_read, grad_write
+    )
+    shaped = [result[None] if index in (2, 3) else result for index, result in enumerate(results)]
+    return tuple(result.reshape(-1) if result.shape[0] == 1 and result.ndim == 2 else result for result in shaped)
 
 
 def per_device(
@@ -1550,6 +1720,13 @@
     head_cols = width // seq_count
     shard = width // fsdp_count
     length = lengths[0]
+    heads = head_cols // HEAD
+    vectors = (qv_bias, out_bias, norm1_gain, norm1_bias, up_bias, down_bias, norm2_gain, norm2_bias)
+    if (fsdp_count, seq_count) == (8, 4):
+        return on_block(
+            tokens, read_memory[0], write_memory[0], lengths, qkv_weight, vectors, out_weight, up_weight, down_weight,
+            cotangent,
+        )
     places = seq_place * local_rows + jnp.arange(local_rows, dtype=jnp.int32)
     in_slot = (places < length)[:, None]
     memory_slots = jnp.arange(MEM, dtype=jnp.int32)
@@ -1560,103 +1737,80 @@
     memory = jnp.concatenate([read_memory[0], write_memory[0]], axis=0)
     layer_in = jnp.where(is_memory, mul(picks.astype(low), memory).astype(low), tokens)
 
-    heads = head_cols // HEAD
     own_shard = lax.dynamic_slice_in_dim(
         qkv_weight.reshape(shard, 3, seq_count, heads, HEAD), seq_place, 1, 2
     )
     own_shard = jnp.transpose(own_shard[:, :, 0], (0, 2, 1, 3)).reshape(shard, 3 * head_cols)
-    vectors = (qv_bias, out_bias, norm1_gain, norm1_bias, up_bias, down_bias, norm2_gain, norm2_bias)
     packed = jnp.concatenate(vectors)
-    on_block = (fsdp_count, seq_count) == (8, 4)
-    if on_block:
-        spare = jnp.zeros((14, 3 * head_cols), low)
-        piece = jnp.concatenate([own_shard, packed.reshape(2, -1), spare], axis=0)
-        (rows, weight, pieces, q_x, k_t, k_wide, v_wide, mixed, row_stats, up_full, down_full, out_full,
-         attended) = front(lengths, layer_in, piece, up_weight, down_weight, out_weight)
-    else:
-        rows = lax.all_gather(layer_in, "seq", axis=0, tiled=True)
-        weight = lax.all_gather(own_shard, "fsdp", axis=0, tiled=True)
-        packed = lax.all_gather(packed.reshape(1, -1), "fsdp", axis=0, tiled=True).astype(full)
-    if not on_block:
-        whole, start = [], 0
-        for vector in vectors:
-            whole.append(packed[:, start : start + vector.shape[0]].reshape(-1))
-            start += vector.shape[0]
-        qv_vec, out_vec, gain_one, shift_one, up_vec, down_vec, gain_two, shift_two = whole
-        own_qv = lax.dynamic_slice_in_dim(qv_vec.reshape(2, seq_count, head_cols), seq_place, 1, 1)
-        bias = jnp.concatenate([own_qv[0, 0], own_qv[1, 0]])
-        bias = jnp.broadcast_to(bias, (8, bias.shape[0]))
-        out_full = lax.all_gather(out_weight, "fsdp", axis=0, tiled=True)
-        up_full = lax.all_gather(up_weight, "fsdp", axis=0, tiled=True)
-        down_full = lax.all_gather(down_weight, "fsdp", axis=0, tiled=True)
-        q_x, k_t, k_wide, v_wide, mixed, mixed_low, row_stats = attention_forward(lengths, rows, weight, bias)
-        attended = lax.all_to_all(mixed_low, "seq", split_axis=1, concat_axis=0, tiled=True)
-    if on_block:
-        (output, grad_resid_one, grad_attended, packed_grad, grad_up_weight, grad_down_weight, grad_out_weight) = (
-            middle_part(lengths, layer_in, cotangent, pieces, attended, up_full, down_full, out_full)
-        )
-    else:
-        resid_one = layer_in.astype(full) + mul(attended, out_full, TN) + out_vec
-        middle, norm_one_back = jax.vjp(normalize, resid_one, gain_one, shift_one)
-        middle_low = middle.astype(low)
-        up_pre = mul(middle_low, up_full) + up_vec
-        gelu_out, gelu_back = jax.vjp(partial(jax.nn.gelu, approximate=False), up_pre)
-        hidden = gelu_out.astype(low)
-        down_pre = mul(hidden, down_full) + down_vec
-        final, norm_two_back = jax.vjp(normalize, middle + down_pre, gain_two, shift_two)
-        output = jnp.where(in_slot, final, 0.0).astype(low)
-        grad_final = jnp.where(in_slot, cotangent.astype(full), 0.0)
-        grad_resid_two, grad_gain_two, grad_shift_two = norm_two_back(grad_final)
-        grad_down = grad_resid_two.astype(low)
-        grad_down_weight = mul(hidden, grad_down, TN)
-        (grad_up_pre,) = gelu_back(mul(grad_down, down_full, NT))
-        grad_up = grad_up_pre.astype(low)
-        grad_up_weight = mul(middle_low, grad_up, TN)
-        grad_middle = grad_resid_two + mul(grad_up, up_full, NT)
-        grad_resid_one, grad_gain_one, grad_shift_one = norm_one_back(grad_middle)
-        grad_branch = grad_resid_one.astype(low)
-        grad_out_weight = mul(attended, grad_branch)
-        grad_attended = mul(out_full, grad_branch, NT).astype(low)
-        vector_grads = [
-            column_sums(grad_branch), grad_gain_one, grad_shift_one, column_sums(grad_up),
-            column_sums(grad_down), grad_gain_two, grad_shift_two,
-        ]
-        packed_grad = jnp.concatenate([v.reshape(fsdp_count, -1) for v in vector_grads], axis=1)
+    rows = lax.all_gather(layer_in, "seq", axis=0, tiled=True)
+    weight = lax.all_gather(own_shard, "fsdp", axis=0, tiled=True)
+    packed = lax.all_gather(packed.reshape(1, -1), "fsdp", axis=0, tiled=True).astype(full)
+    whole, start = [], 0
+    for vector in vectors:
+        whole.append(packed[:, start : start + vector.shape[0]].reshape(-1))
+        start += vector.shape[0]
+    qv_vec, out_vec, gain_one, shift_one, up_vec, down_vec, gain_two, shift_two = whole
+    own_qv = lax.dynamic_slice_in_dim(qv_vec.reshape(2, seq_count, head_cols), seq_place, 1, 1)
+    bias = jnp.concatenate([own_qv[0, 0], own_qv[1, 0]])
+    bias = jnp.broadcast_to(bias, (8, bias.shape[0]))
+    out_full = lax.all_gather(out_weight, "fsdp", axis=0, tiled=True)
+    up_full = lax.all_gather(up_weight, "fsdp", axis=0, tiled=True)
+    down_full = lax.all_gather(down_weight, "fsdp", axis=0, tiled=True)
+    q_x, k_t, k_wide, v_wide, mixed, mixed_low, row_stats = attention_forward(lengths, rows, weight, bias)
+    attended = lax.all_to_all(mixed_low, "seq", split_axis=1, concat_axis=0, tiled=True)
+    resid_one = layer_in.astype(full) + mul(attended, out_full, TN) + out_vec
+    middle, norm_one_back = jax.vjp(normalize, resid_one, gain_one, shift_one)
+    middle_low = middle.astype(low)
+    up_pre = mul(middle_low, up_full) + up_vec
+    gelu_out, gelu_back = jax.vjp(partial(jax.nn.gelu, approximate=False), up_pre)
+    hidden = gelu_out.astype(low)
+    down_pre = mul(hidden, down_full) + down_vec
+    final, norm_two_back = jax.vjp(normalize, middle + down_pre, gain_two, shift_two)
+    output = jnp.where(in_slot, final, 0.0).astype(low)
+    grad_final = jnp.where(in_slot, cotangent.astype(full), 0.0)
+    grad_resid_two, grad_gain_two, grad_shift_two = norm_two_back(grad_final)
+    grad_down = grad_resid_two.astype(low)
+    grad_down_weight = mul(hidden, grad_down, TN)
+    (grad_up_pre,) = gelu_back(mul(grad_down, down_full, NT))
+    grad_up = grad_up_pre.astype(low)
+    grad_up_weight = mul(middle_low, grad_up, TN)
+    grad_middle = grad_resid_two + mul(grad_up, up_full, NT)
+    grad_resid_one, grad_gain_one, grad_shift_one = norm_one_back(grad_middle)
+    grad_branch = grad_resid_one.astype(low)
+    grad_out_weight = mul(attended, grad_branch)
+    grad_attended = mul(out_full, grad_branch, NT).astype(low)
+    vector_grads = [
+        column_sums(grad_branch), grad_gain_one, grad_shift_one, column_sums(grad_up),
+        column_sums(grad_down), grad_gain_two, grad_shift_two,
+    ]
+    packed_grad = jnp.concatenate([v.reshape(fsdp_count, -1) for v in vector_grads], axis=1)
     saved = (q_x, k_t, k_wide, v_wide, mixed, row_stats)
-    if on_block:
-        (input_grad, grad_read, grad_write, qkv_out, vector_sum, up_out, down_out, out_out) = back(
-            lengths, grad_attended, saved, packed_grad, rows, weight, grad_resid_one,
-            grad_up_weight, grad_down_weight, grad_out_weight,
-        )
-        own_vectors = vector_sum[:3].reshape(-1)
-        qkv_out, up_out, down_out, out_out = (g.astype(full) for g in (qkv_out, up_out, down_out, out_out))
-    else:
-        grad_t = lax.all_to_all(grad_attended, "seq", split_axis=0, concat_axis=1, tiled=True)
-        partial_in, weight_part, sums = attention_backward(*saved, grad_t, rows, weight)
-        from_heads = lax.psum_scatter(partial_in, "seq", scatter_dimension=0, tiled=True).astype(full)
-        grad_layer_in = grad_resid_one + from_heads
-        input_grad = jnp.where(is_memory, 0.0, grad_layer_in)
-        grad_memory = lax.dot_general(
-            picks, grad_layer_in, TN, precision=lax.Precision.HIGHEST, preferred_element_type=full
-        )
-        grad_memory = lax.psum(grad_memory.astype(low), "seq").astype(full)
-        grad_read, grad_write = grad_memory[:MEM], grad_memory[MEM:]
-        sums = sums[:, 0].reshape(heads, 3, HEAD)
-        own_sums = jnp.stack([sums[:, 0].reshape(-1), sums[:, 2].reshape(-1)])[:, None]
-        zero_qv = jnp.zeros((2, seq_count, head_cols), full)
-        qv_grad = lax.dynamic_update_slice_in_dim(zero_qv, own_sums, seq_place, 1)
-        packed_grad = jnp.concatenate([qv_grad.reshape(fsdp_count, -1), packed_grad], axis=1)
-        packed_sum = lax.psum(packed_grad, ("fsdp", "seq"))
-        own_vectors = lax.dynamic_index_in_dim(packed_sum, lax.axis_index("fsdp"), 0, False)
-
-        def both_axes(part):
-            piece = lax.psum_scatter(part.astype(low), "fsdp", scatter_dimension=0, tiled=True)
-            return lax.psum(piece, "seq").astype(full)
-
-        qkv_piece = lax.psum_scatter(weight_part, "fsdp", scatter_dimension=0, tiled=True)
-        qkv_parts = lax.all_gather(qkv_piece, "seq", axis=0).reshape(seq_count, shard, heads, 3, HEAD)
-        qkv_out = jnp.transpose(qkv_parts, (1, 3, 0, 2, 4)).reshape(shard, 3 * width).astype(full)
-        up_out, down_out, out_out = both_axes(grad_up_weight), both_axes(grad_down_weight), both_axes(grad_out_weight)
+    grad_t = lax.all_to_all(grad_attended, "seq", split_axis=0, concat_axis=1, tiled=True)
+    partial_in, weight_part, sums = attention_backward(*saved, grad_t, rows, weight)
+    from_heads = lax.psum_scatter(partial_in, "seq", scatter_dimension=0, tiled=True).astype(full)
+    grad_layer_in = grad_resid_one + from_heads
+    input_grad = jnp.where(is_memory, 0.0, grad_layer_in)
+    grad_memory = lax.dot_general(
+        picks, grad_layer_in, TN, precision=lax.Precision.HIGHEST, preferred_element_type=full
+    )
+    grad_memory = lax.psum(grad_memory.astype(low), "seq").astype(full)
+    grad_read, grad_write = grad_memory[:MEM], grad_memory[MEM:]
+    sums = sums[:, 0].reshape(heads, 3, HEAD)
+    own_sums = jnp.stack([sums[:, 0].reshape(-1), sums[:, 2].reshape(-1)])[:, None]
+    zero_qv = jnp.zeros((2, seq_count, head_cols), full)
+    qv_grad = lax.dynamic_update_slice_in_dim(zero_qv, own_sums, seq_place, 1)
+    packed_grad = jnp.concatenate([qv_grad.reshape(fsdp_count, -1), packed_grad], axis=1)
+    packed_sum = lax.psum(packed_grad, ("fsdp", "seq"))
+    own_vectors = lax.dynamic_index_in_dim(packed_sum, lax.axis_index("fsdp"), 0, False)
+
+    def both_axes(part):
+        piece = lax.psum_scatter(part.astype(low), "fsdp", scatter_dimension=0, tiled=True)
+        return lax.psum(piece, "seq").astype(full)
+
+    qkv_piece = lax.psum_scatter(weight_part, "fsdp", scatter_dimension=0, tiled=True)
+    qkv_parts = lax.all_gather(qkv_piece, "seq", axis=0).reshape(seq_count, shard, heads, 3, HEAD)
+    qkv_out = jnp.transpose(qkv_parts, (1, 3, 0, 2, 4)).reshape(shard, 3 * width).astype(full)
+    up_out, down_out, out_out = both_axes(grad_up_weight), both_axes(grad_down_weight), both_axes(grad_out_weight)
     vector_outs, start = [], 0
     for vector in vectors:
         vector_outs.append(own_vectors[start : start + vector.shape[0]])

time: 240 us -> 224 us (0.933)
  local copies, waits for them, and re-layouts: 14.6 us -> 4.22 us
  other arithmetic: 6.74 us -> 2.69 us
    pallas_call x1, Pallas kernels: 77.1 us -> 68.6 us  [front(): pl.pallas_call(front_kernel, in_specs=[pl.BlockSpec(memory_space=pltpu.SM...]
    convert_element_type x4 -> x0, other arithmetic: 5.89 us -> none  [per_device(): g.astype(full)]
    concatenate x2 -> x0, local copies, waits for them, and re-layouts: 5.52 us -> none  [the longest x1 5.44 us: per_device(): packed = jnp.concatenate(vectors)]
    pallas_call x0 -> x1, Pallas kernels: none -> 4.85 us  [finish(): pl.pallas_call(finish_kernel, out_shape=[shaped(*output.shape, kind=low),...]
    pallas_call x1, Pallas kernels: 99.3 us -> 103 us  [back(): pl.pallas_call(back_kernel, in_specs=[pl.BlockSpec(memory_space=pltpu.SME...]
    unnamed x19 -> x2, local copies, waits for them, and re-layouts: 6.31 us -> 2.88 us
    slice x4 -> x0, local copies, waits for them, and re-layouts: 2.52 us -> none  [the longest x3 1.81 us: per_device(): vector_outs.append(own_vectors[start:start + vector.shape[0]])]
where the time goes in v6:
time: 224 us
  Pallas kernels  215 us (96%)
  local copies, waits for them, and re-layouts  4.22 us (2%)
  other arithmetic  2.69 us (1%)
    pallas_call x1, Pallas kernels, back(): pl.pallas_call(back_kernel, in_specs=[pl.BlockSpec(memory_space=pltpu.SME...  103 us
    pallas_call x1, Pallas kernels, front(): pl.pallas_call(front_kernel, in_specs=[pl.BlockSpec(memory_space=pltpu.SM...  68.6 us
    pallas_call x1, Pallas kernels, middle_part(): pl.pallas_call(middle_kernel, in_specs=[pl.BlockSpec(memory_space=pltpu.S...  38.7 us
    pallas_call x1, Pallas kernels, finish(): pl.pallas_call(finish_kernel, out_shape=[shaped(*output.shape, kind=low),...  4.85 us

profile of v6, /device:TPU:9, one launch (start us, length us, event | category | flops | bytes accessed | tf_op | source)
XLA Modules:
  0.0 223.6 jit_solution(16924638743212424470)
XLA Ops:
  1.3 0.7 reshape.88
  2.0 0.7 reshape.92
  2.6 1.4 convert_add_fusion.vectors_in
  4.0 68.6 %front.1 = (f32[8,768]{1,0:T(8,128)}, f32[8,3072]{1,0:T(8,128)}, bf16[2048,768]{1,0:T(8,128)(2,1)}, bf16[768,576]{1,0:T(8,128)(2,1)}, bf16[3,64,2048]{2,1,0:T(8,...) custom-call(s32[1]{0:T(128)S(6)} %copy.35.length_ref, ...), custom_call_target="tpu_custom_call" | custom-call | tf_op jit(solution)/shard_map/front/pallas_call | solution.py:756
  72.7 38.7 %middle.1 = (bf16[512,768]{1,0:T(8,128)(2,1)}, f32[512,768]{1,0:T(8,128)}, bf16[768,512]{1,0:T(8,128)(2,1)}, f32[8,16,384]{2,1,0:T(8,128)}, bf16[2,4,96,1536]{3,...) custom-call(s32[1]{0:T(128)S(6)} %copy.35.length_ref, ...), custom_call_target="tpu_custom_call" | custom-call | tf_op jit(solution)/shard_map/middle/pallas_call | solution.py:1610
  111.4 103.1 %back.1 = (f32[512,768]{1,0:T(8,128)}, f32[10,768]{1,0:T(8,128)}, f32[10,768]{1,0:T(8,128)}, bf16[96,2304]{1,0:T(8,128)(2,1)}, f32[16,384]{1,0:T(8,128)}, /*inde...) custom-call(s32[1]{0:T(128)S(6)} %copy.35.length_ref, ...), custom_call_target="tpu_custom_call" | custom-call | tf_op jit(solution)/shard_map/back/pallas_call | solution.py:1316
  214.5 4.9 %finish.1 = (bf16[512,768]{1,0:T(8,128)(2,1)}, f32[512,768]{1,0:T(8,128)}, f32[10,768]{1,0:T(8,128)}, f32[10,768]{1,0:T(8,128)}, f32[96,2304]{1,0:T(8,128)}, /*i...) custom-call(bf16[512,768]{1,0:T(8,128)(2,1)} %get-tuple-element.68.o, ...), custom_call_target="tpu_custom_call" | custom-call | tf_op jit(solution)/shard_map/finish/pallas_call | solution.py:1663
  219.4 1.3 reduce
  220.7 1.4 copy.33
  222.1 1.4 copy.34

commit v7 on v6

--- a/solution.py
+++ b/solution.py
@@ -397,13 +397,13 @@
         else:
             pl.when(self.place.has(relation))(action)
 
-    def arrive_z(self, array, relation):
+    def arrive_z(self, array, relation, along=True, across=True):
         def action():
             if relation != OWN:
                 self.wait_z(array, relation)
-            for way, holds in self.z_ways(relation):
+            for way, holds in self.z_ways(relation) if along else ():
                 pl.when(holds)(lambda way=way: self.along_z(array, relation, way).start())
-            if array != OUT_W:
+            if array != OUT_W and across:
                 self.over_x(array, relation).start()
             if array != QKV_W and relation != OWN:
                 self.to_core(array, relation, 0).start()
@@ -543,21 +543,20 @@
         send_rows(half, 1).start()
         send_rows(half, 0).start()
     gather.cross_out()
-    gather.arrive_z(UP_W, OWN)
     for copy in own_copies():
         copy.start()
     for relation in (1, 4):
         gather.arrive_z(QKV_W, relation)
     gather.pair_out(own_copies()[2])
+    for relation in (2, 5):
+        gather.arrive_z(QKV_W, relation)
+    gather.arrive_z(UP_W, OWN, across=False)
     rows_from(0, 1).wait_recv()
     pass_rows(0, False).start()
-    for relation in (2, 5):
-        gather.arrive_z(QKV_W, relation)
-    gather.arrive_z(DOWN_W, OWN)
-    for relation in (1, 4):
-        gather.arrive_z(UP_W, relation)
     for relation in (3, 6):
         gather.arrive_z(QKV_W, relation)
+    gather.arrive_z(UP_W, OWN, along=False)
+    gather.arrive_z(DOWN_W, OWN)
     for relation in range(RELATIONS):
         gather.arrive_x(QKV_W, relation)
 
@@ -581,9 +580,11 @@
     project(2 * place.y + 1 - place.c)
     rows_from(1, 1).wait_recv()
     pass_rows(1, False).start()
+    for relation in (1, 4):
+        gather.arrive_z(UP_W, relation)
+        gather.arrive_z(OUT_W, relation)
     project(2 * (1 - place.y) + place.c)
     for relation in (1, 4):
-        gather.arrive_z(OUT_W, relation)
         gather.arrive_z(DOWN_W, relation)
 
     def scatter_vector(target, index, size, first):
@@ -620,49 +621,43 @@
         ]
 
     def chores(step):
-        if step == 0:
+        if step == 1:
+            gather.arrive_x(UP_W, OWN)
+        elif step == 2:
             for relation in (2, 5):
                 gather.arrive_z(UP_W, relation)
-        elif step == 1:
-            gather.arrive_x(UP_W, OWN)
             gather.arrive_x(DOWN_W, OWN)
         elif step == 3:
+            for relation in (1, 4):
+                gather.arrive_y(relation, 0)
+        elif step == 4:
             for relation in (2, 5):
                 gather.arrive_z(OUT_W, relation)
-                gather.arrive_z(DOWN_W, relation)
-        elif step == 4:
-            for relation in (1, 4):
-                gather.arrive_x(UP_W, relation)
-                gather.arrive_y(relation, 0)
             for save in head_saves(0):
                 save.start()
         elif step == 5:
+            for relation in (2, 5):
+                gather.arrive_z(DOWN_W, relation)
             gather.arrive_y(OWN, 1)
         elif step == 6:
-            for relation in (3, 6):
-                gather.arrive_z(UP_W, relation)
-        elif step == 7:
             for relation in (1, 4):
-                gather.arrive_x(DOWN_W, relation)
+                gather.arrive_x(UP_W, relation)
         elif step == 8:
             for relation in (2, 5):
-                gather.arrive_x(UP_W, relation)
+                gather.arrive_y(relation, 0)
             for save in head_saves(1):
                 save.start()
         elif step == 9:
             for relation in (3, 6):
+                gather.arrive_z(UP_W, relation)
+            for relation in (2, 5):
+                gather.arrive_x(UP_W, relation)
+        elif step == 11:
+            for relation in (3, 6):
                 gather.arrive_z(OUT_W, relation)
                 gather.arrive_z(DOWN_W, relation)
-            for relation in (2, 5):
-                gather.arrive_y(relation, 0)
-        elif step == 10:
-            for relation in (2, 5):
+            for relation in (1, 4):
                 gather.arrive_x(DOWN_W, relation)
-        elif step == 11:
-            for relation in (3, 6):
-                gather.arrive_x(UP_W, relation)
-            for relation in (1, 4):
-                gather.arrive_y(relation, 1)
 
     def send_mixed(h, turn, arriving=False):
         member = place.member(turn)
@@ -711,12 +706,16 @@
     for save in head_saves(2):
         save.start()
     for relation in (3, 6):
+        gather.arrive_x(UP_W, relation)
+    for relation in (2, 5):
         gather.arrive_x(DOWN_W, relation)
-    for relation in (2, 5):
+    for relation in (1, 4):
         gather.arrive_y(relation, 1)
-    for column in range(2):
-        for relation in (3, 6):
-            gather.arrive_y(relation, column)
+    for relation in (3, 6):
+        gather.arrive_y(relation, 0)
+        gather.arrive_x(DOWN_W, relation)
+    for relation in (2, 5, 3, 6):
+        gather.arrive_y(relation, 1)
     for array in (UP_W, OUT_W, DOWN_W, QKV_W):
         gather.finish(array)
     for copy in own_copies()[:2]:
@@ -1153,8 +1152,6 @@
         elif index == 11:
             take_x(DOWN_W, (1,))
             reduce.fling(DOWN_W, (1,))
-            reduce.settle(UP_W)
-            sum_y(UP_W).start()
 
     def step(index, carry):
         for when in range(1, 12):
@@ -1223,6 +1220,8 @@
         share_far(half).start()
     memory = Spread(place, memory_all, memory_own, share_send.at[DW_FIRST + heads], share_recv.at[DW_FIRST + heads])
     memory.start()
+    reduce.settle(UP_W)
+    sum_y(UP_W).start()
     take_x(first)
     reduce.fling(first)
     reduce.add_x(OUT_W, 0)
@@ -1635,11 +1634,12 @@
     output, input_out, read_out, write_out, qkv_out, qv_out, out_out, out_b, gain_one, shift_one, up_out, up_b,
     down_out, down_b, gain_two, shift_two,
 ):
-    shard = qkv_out.shape[0]
+    shard = out_b.shape[1]
     output[...] = output_in[...]
     input_out[...] = input_in[...]
-    read_out[...] = read_in[...]
-    write_out[...] = write_in[...]
+    for given, out in ((read_in, read_out), (write_in, write_out)):
+        for line in range(given.shape[0]):
+            out[line] = given[line : line + 1]
     for given, out in ((qkv_in, qkv_out), (up_in, up_out), (down_in, down_out), (out_in, out_out)):
         out[...] = given[...].astype(full)
     qv_out[...] = vector_in[0:1, : 2 * shard]
@@ -1660,12 +1660,31 @@
         return jax.ShapeDtypeStruct(shape, kind)
 
     line = shaped(1, shard)
+    steps = 2
+
+    def rows(array):
+        return pl.BlockSpec((array.shape[0] // steps,) + array.shape[1:], lambda i: (i, 0))
+
+    def once(*shape):
+        return pl.BlockSpec(shape, lambda i: (0,) * len(shape))
+
+    lone = once(1, shard)
+    memory = (grad_read.shape[0], 1, grad_read.shape[1])
     return pl.pallas_call(
         finish_kernel,
+        grid=(steps,),
+        in_specs=[
+            rows(output), rows(input_grad), rows(qkv_grad), once(*vectors.shape), rows(up_grad), rows(down_grad),
+            rows(out_grad), once(*grad_read.shape), once(*grad_write.shape),
+        ],
+        out_specs=[
+            rows(output), rows(input_grad), once(*memory), once(*memory), rows(qkv_grad), once(1, 2 * shard),
+            rows(out_grad), lone, lone, lone, rows(up_grad), once(1, 4 * shard), rows(down_grad), lone, lone, lone,
+        ],
         out_shape=[
-            shaped(*output.shape, kind=low), shaped(*input_grad.shape), shaped(*grad_read.shape),
-            shaped(*grad_write.shape), shaped(*qkv_grad.shape), shaped(1, 2 * shard), shaped(*out_grad.shape),
-            line, line, line, shaped(*up_grad.shape), shaped(1, 4 * shard), shaped(*down_grad.shape), line, line, line,
+            shaped(*output.shape, kind=low), shaped(*input_grad.shape), shaped(*memory), shaped(*memory),
+            shaped(*qkv_grad.shape), shaped(1, 2 * shard), shaped(*out_grad.shape), line, line, line,
+            shaped(*up_grad.shape), shaped(1, 4 * shard), shaped(*down_grad.shape), line, line, line,
         ],
         compiler_params=pltpu.CompilerParams(vmem_limit_bytes=VMEM_BYTES),
         name="finish",
@@ -1705,7 +1724,7 @@
     results = finish(
         output, input_grad, qkv_grad, vector_sum, up_grad, down_grad, out_grad, grad_read, grad_write
     )
-    shaped = [result[None] if index in (2, 3) else result for index, result in enumerate(results)]
+    shaped = [jnp.swapaxes(result, 0, 1) if index in (2, 3) else result for index, result in enumerate(results)]
     return tuple(result.reshape(-1) if result.shape[0] == 1 and result.ndim == 2 else result for result in shaped)
 
 

time: 224 us -> 217 us (0.969)
  Pallas kernels: 215 us -> 210 us
  local copies, waits for them, and re-layouts: 4.22 us -> 1.34 us
    pallas_call x1, Pallas kernels: 103 us -> 93.3 us  [back(): pl.pallas_call(back_kernel, in_specs=[pl.BlockSpec(memory_space=pltpu.SME...]
    pallas_call x1, Pallas kernels: 68.6 us -> 74.4 us  [front(): pl.pallas_call(front_kernel, in_specs=[pl.BlockSpec(memory_space=pltpu.SM...]
    unnamed x2 -> x0, local copies, waits for them, and re-layouts: 2.88 us -> none
where the time goes in v7:
time: 217 us; the launch traced here: 215 us
  Pallas kernels  210 us (97%)
  other arithmetic  2.68 us (1%)
    pallas_call x1, Pallas kernels, back(): pl.pallas_call(back_kernel, in_specs=[pl.BlockSpec(memory_space=pltpu.SME...  93.3 us
    pallas_call x1, Pallas kernels, front(): pl.pallas_call(front_kernel, in_specs=[pl.BlockSpec(memory_space=pltpu.SM...  74.4 us
    pallas_call x1, Pallas kernels, middle_part(): pl.pallas_call(middle_kernel, in_specs=[pl.BlockSpec(memory_space=pltpu.S...  37.6 us
    pallas_call x1, Pallas kernels, finish(): pl.pallas_call(finish_kernel, grid=(steps,), in_specs=[rows(output), rows...  4.46 us

profile of v7, /device:TPU:9, one launch (start us, length us, event | category | flops | bytes accessed | tf_op | source)
XLA Modules:
  0.0 215.1 jit_solution(2057244575289544541)
XLA Ops:
  1.3 0.7 reshape.88
  2.0 0.7 reshape.92
  2.6 1.4 convert_add_fusion.vectors_in
  4.0 74.4 %front.1 = (f32[8,768]{1,0:T(8,128)}, f32[8,3072]{1,0:T(8,128)}, bf16[2048,768]{1,0:T(8,128)(2,1)}, bf16[768,576]{1,0:T(8,128)(2,1)}, bf16[3,64,2048]{2,1,0:T(8,...) custom-call(s32[1]{0:T(128)S(6)} %copy.33.length_ref, ...), custom_call_target="tpu_custom_call" | custom-call | tf_op jit(solution)/shard_map/front/pallas_call | solution.py:755
  78.4 37.6 %middle.1 = (bf16[512,768]{1,0:T(8,128)(2,1)}, f32[512,768]{1,0:T(8,128)}, bf16[768,512]{1,0:T(8,128)(2,1)}, f32[8,16,384]{2,1,0:T(8,128)}, bf16[2,4,96,1536]{3,...) custom-call(s32[1]{0:T(128)S(6)} %copy.33.length_ref, ...), custom_call_target="tpu_custom_call" | custom-call | tf_op jit(solution)/shard_map/middle/pallas_call | solution.py:1609
  116.1 93.3 %back.1 = (f32[512,768]{1,0:T(8,128)}, f32[10,768]{1,0:T(8,128)}, f32[10,768]{1,0:T(8,128)}, bf16[96,2304]{1,0:T(8,128)(2,1)}, f32[16,384]{1,0:T(8,128)}, /*inde...) custom-call(s32[1]{0:T(128)S(6)} %copy.33.length_ref, ...), custom_call_target="tpu_custom_call" | custom-call | tf_op jit(solution)/shard_map/back/pallas_call | solution.py:1315
  209.4 4.5 %finish.1 = (bf16[512,768]{1,0:T(8,128)(2,1)}, f32[512,768]{1,0:T(8,128)}, f32[10,1,768]{2,1,0:T(1,128)}, f32[10,1,768]{2,1,0:T(1,128)}, f32[96,2304]{1,0:T(8,12...) custom-call(bf16[512,768]{1,0:T(8,128)(2,1)} %get-tuple-element.68.o, ...), custom_call_target="tpu_custom_call" | custom-call | tf_op jit(solution)/shard_map/finish/pallas_call | solution.py:1673
  213.8 1.3 reduce

commit v8 on v7

--- a/solution.py
+++ b/solution.py
@@ -789,10 +789,10 @@
 
 
 class Reduce:
-    def __init__(self, place, given, sums, from_y, from_x, from_z, sems):
+    def __init__(self, place, given, sums, across, from_y, from_x, from_z, last, sems):
+        self.across, self.last, self.far_up = across, last, last + 1
         self.place, self.given, self.sums = place, given, sums
         self.from_y, self.from_x, self.from_z = from_y, from_x, from_z
-        self.last = max(sums)
         self.y_send, self.y_recv, self.x_send, self.x_recv, self.z_send, self.z_recv = sems
 
     def dest(self, column, line):
@@ -800,7 +800,7 @@
         return 2 * line + (x if column == 0 else 1 - x)
 
     def slot(self, array, line, column=0):
-        if array >= DW_FIRST:
+        if DW_FIRST <= array <= self.last:
             rows = 4 * HEAD if array == self.last else 3 * HEAD
             return self.sums[array].at[self.dest(column, line), pl.ds(0, rows // 4)]
         return self.sums[array].at[line]
@@ -811,31 +811,29 @@
         return ref
 
     def load(self, array, column, line, sem):
-        source = self.given[array]
         if array == OUT_W:
-            return pltpu.make_async_copy(source.at[line], self.sums[array].at[line], sem)
-        source = source.at[column, line, 0] if array == DOWN_W else source.at[column, line]
-        return pltpu.make_async_copy(source, self.sums[array].at[line], sem)
-
-    def over_y(self, line):
+            return pltpu.make_async_copy(self.given[array].at[line, 0], self.sums[array].at[line], sem)
+        source = self.given[UP_W if array == self.far_up else array].at[column, line, 1 if array == self.far_up else 0]
+        target = self.across if column == 1 else self.sums[array]
+        return pltpu.make_async_copy(source, target.at[line], sem)
+
+    def over_y(self, array, line):
+        column, index = (1, 1) if array == UP_W else (0, 0)
         return remote(
-            self.given[DOWN_W].at[0, line, 1], self.from_y.at[line], self.y_send.at[line], self.y_recv.at[line],
-            self.place.across_y,
-        )
-
-    def add_y(self, line):
-        self.over_y(line).wait_recv()
-        slot = self.slot(DOWN_W, line)
-        slot[...] = add_low(slot[...], self.from_y[line])
+            self.given[array].at[column, line, 1], self.from_y.at[index, line], self.y_send.at[index, line],
+            self.y_recv.at[index, line], self.place.across_y,
+        )
+
+    def add_y(self, array, line):
+        self.over_y(array, line).wait_recv()
+        slot = self.across.at[line] if array == UP_W else self.slot(DOWN_W, line)
+        slot[...] = add_low(slot[...], self.from_y[1 if array == UP_W else 0, line])
 
     def over_x(self, array, line):
         if array == OUT_W:
-            here = self.sums[array].at[self.place.z]
-            return remote(
-                here.at[1], self.from_x[array], self.x_send.at[array, 0], self.x_recv.at[array, 0], self.place.across_x
-            )
-        if array == UP_W:
-            start = self.given[array].at[1, line]
+            start = self.given[array].at[line, 1]
+        elif array == UP_W:
+            start = self.across.at[line]
         elif array == DOWN_W:
             start = self.given[array].at[1, line, 0]
         else:
@@ -847,9 +845,8 @@
 
     def add_x(self, array, line):
         self.over_x(array, line).wait_recv()
-        slot = self.sums[array].at[self.place.z, 0] if array == OUT_W else self.slot(array, line)
-        came = self.from_x[array] if array == OUT_W else self.cut(array, self.from_x[array].at[line])
-        slot[...] = add_low(slot[...], came[...])
+        slot = self.slot(array, line)
+        slot[...] = add_low(slot[...], self.cut(array, self.from_x[array].at[line])[...])
 
     def along_z(self, array, way, line):
         return remote(
@@ -880,6 +877,9 @@
                         self.add_z(array, 1, line)
                     self.along_z(array, 1, line).start()
 
+    def direct(self, array):
+        return array != self.far_up
+
     def to_line(self, array, line):
         where = (2 * line + self.place.x, self.place.s)
         return remote(
@@ -892,7 +892,7 @@
             pl.when(self.place.z != line)(lambda line=line: self.to_line(array, line).start())
 
     def settle(self, array):
-        if array >= DOWN_W:
+        if self.direct(array):
             slot = self.slot(array, self.place.z)
             for line in range(4):
 
@@ -916,15 +916,15 @@
 
     def finish(self, array):
         for line in range(4):
-            if array != OUT_W or line == 0:
+            if array != self.far_up:
                 self.over_x(array, line).wait_send()
-            if array >= DOWN_W:
+            if self.direct(array):
                 pl.when(self.place.z != line)(lambda line=line: self.to_line(array, line).wait_send())
             else:
                 pl.when(self.place.z < line)(lambda line=line: self.along_z(array, 0, line).wait_send())
                 pl.when(self.place.z > line)(lambda line=line: self.along_z(array, 1, line).wait_send())
-            if array == DOWN_W:
-                self.over_y(line).wait_send()
+            if array in (UP_W, DOWN_W):
+                self.over_y(array, line).wait_send()
 
 
 class Spread:
@@ -965,10 +965,10 @@
     length_ref, grad_own, vectors_in, q_in, k_in, k_wide_in, v_wide_in, mixed_in, stats_in, rows_in, weight_in, resid_in, up_given, down_given, out_given,
     input_out, read_out, write_out, qkv_out, vector_out, up_out, down_out, out_out,
     q_x, k_t, k_wide, v_wide, mixed, row_stats, grad_t, q_here, do_x, grads, grad_k, grad_v, rows_ref, weight_ref, resid_ref,
-    up_sum, out_sum, down_sum, dw, down_y, up_x, out_x, down_x, dw_x, up_z, out_z, down_z, dw_z,
-    up_last, out_last, up_other, out_other, down_all, dw_all,
+    up_sum, out_sum, down_sum, far_sum_up, across_up, dw, both_y, up_x, out_x, down_x, dw_x, up_z, out_z, down_z, dw_z, far_z,
+    up_last, out_last, up_all, out_other, down_all, dw_all,
     near_send, near_recv, far_sum, far_recv, memory_all, memory_own,
-    mix_send, mix_recv, local_sem, saved_sem, mine_sem, share_send, share_recv, near_s, near_r, far_s, far_r,
+    mix_send, mix_recv, local_sem, saved_sem, mine_sem, share_send, share_recv, near_s, near_r, far_s, far_r, cross_s, cross_r,
     *sems,
 ):
     place = Place()
@@ -976,6 +976,7 @@
     width, local_rows = grad_own.shape
     head_cols = heads * HEAD
     last = DW_FIRST + heads - 1
+    far_up = last + 1
     given = {UP_W: up_given, OUT_W: out_given, DOWN_W: down_given}
     sums = {UP_W: up_sum, OUT_W: out_sum, DOWN_W: down_sum}
     from_x = {UP_W: up_x, OUT_W: out_x, DOWN_W: down_x}
@@ -983,7 +984,8 @@
     for h in range(heads):
         sums[DW_FIRST + h], from_x[DW_FIRST + h] = dw.at[h], dw_x.at[h]
         from_z[DW_FIRST + h] = dw_z.at[h]
-    reduce = Reduce(place, given, sums, down_y, from_x, from_z, sems)
+    sums[far_up], from_z[far_up] = far_sum_up, far_z
+    reduce = Reduce(place, given, sums, across_up, both_y, from_x, from_z, last, sems)
     greet(place, True)
 
     peers = (place.across_y, place.diagonal, place.core)
@@ -1009,11 +1011,15 @@
         return [pltpu.make_async_copy(src, dst, saved_sem.at[h, i]) for i, (src, dst) in enumerate(pairs)]
 
     def sum_loads(array):
-        return [reduce.load(array, 0, line, mine_sem.at[array, line]) for line in LINES]
+        index = array if array < DW_FIRST else DW_FIRST
+        return [reduce.load(array, 0, line, mine_sem.at[index, line]) for line in LINES]
+
+    def across_loads():
+        return [reduce.load(UP_W, 1, line, mine_sem.at[DW_FIRST + 1, line]) for line in LINES]
 
     for turn in range(3):
         send_grad(turn).start()
-    for load in sum_loads(OUT_W):
+    for load in sum_loads(far_up):
         load.start()
     for load in saved_loads(0):
         load.start()
@@ -1025,13 +1031,13 @@
         for line in lines:
             reduce.over_x(array, line).start()
 
-    send_x(UP_W)
-    for line in LINES:
-        reduce.over_y(line).start()
     send_x(DOWN_W)
-    for array in (UP_W, DOWN_W):
-        for load in sum_loads(array):
-            load.start()
+    send_x(OUT_W)
+    for array in (DOWN_W, UP_W):
+        for line in LINES:
+            reduce.over_y(array, line).start()
+    for load in across_loads() + sum_loads(UP_W) + sum_loads(OUT_W) + sum_loads(DOWN_W):
+        load.start()
     for load in loads:
         load.start()
 
@@ -1072,10 +1078,10 @@
                     ].astype(low)
         send_x(DW_FIRST + h)
 
-    share = {UP_W: (up_last, up_other), OUT_W: (out_last, out_other)}
+    share = {OUT_W: (out_last, out_other)}
 
     def settled(array):
-        return sums[array].at[place.z, 0] if array == OUT_W else sums[array].at[place.z]
+        return sums[array].at[place.z]
 
     def sum_y(array):
         mine_now = settled(array)
@@ -1086,13 +1092,26 @@
         return remote(mine_now, share[array][1], share_send.at[array, 1], share_recv.at[array, 1], place.core)
 
     def spread_of(array):
-        if array == DOWN_W:
-            return Spread(place, down_all, down_sum.at[place.z], share_send.at[2], share_recv.at[2])
+        if array in (UP_W, DOWN_W):
+            return Spread(
+                place, {UP_W: up_all, DOWN_W: down_all}[array], sums[array].at[place.z], share_send.at[array],
+                share_recv.at[array],
+            )
         h = array - DW_FIRST
         return Spread(
             place, dw_all.at[h, :, pl.ds(0, reduce.slot(array, 0).shape[0])], reduce.slot(array, place.z),
             share_send.at[array], share_recv.at[array],
         )
+
+    def cross_up():
+        return remote(far_sum_up.at[place.z], up_last, cross_s.at[0], cross_r.at[0], place.across_y)
+
+    def settle_up():
+        reduce.settle(UP_W)
+        cross_up().wait_recv()
+        slot = sums[UP_W].at[place.z]
+        slot[...] = add_low(slot[...], up_last[...])
+        spread_of(UP_W).start()
 
     def add_last(array):
         sum_y(array).wait()
@@ -1102,56 +1121,59 @@
 
     first, second = DW_FIRST, DW_FIRST + 1
 
+    def pass_up(lines):
+        for line in lines:
+            reduce.add_y(UP_W, line)
+            reduce.over_x(UP_W, line).start()
+
     def chores(index):
         if index == 1:
             send_grad(2, True).wait_recv()
+            for load in across_loads() + sum_loads(UP_W) + sum_loads(OUT_W) + sum_loads(DOWN_W):
+                load.wait()
         elif index == 2:
             send_grad(1, True).wait_recv()
-            for array in (UP_W, DOWN_W):
-                for load in sum_loads(array):
-                    load.wait()
-            take_x(UP_W, (3,))
-            reduce.hop(UP_W, 0, (3,))
-            reduce.hop(OUT_W, 1, (3, 0))
+            reduce.hop(far_up, 1, (3, 0))
         elif index == 3:
             send_grad(0, True).wait_recv()
-            reduce.hop(OUT_W, 1, (2, 1))
+            reduce.hop(far_up, 1, (2, 1))
         elif index == 4:
             for load in saved_loads(1):
                 load.wait()
             weight_part(0)
-            take_x(UP_W, (0,))
-            reduce.hop(UP_W, 0, (0,))
-            reduce.hop(OUT_W, 2)
+            reduce.hop(far_up, 2)
         elif index == 5:
-            reduce.hop(UP_W, 1, (3,))
+            take_x(DOWN_W)
+            for line in (3, 0):
+                reduce.add_y(DOWN_W, line)
+                reduce.fling(DOWN_W, (line,))
         elif index == 6:
-            for line in LINES:
-                reduce.add_y(line)
-            take_x(UP_W, (2,))
-            reduce.hop(UP_W, 0, (2,))
-            reduce.settle(OUT_W)
-            reduce.over_x(OUT_W, 0).start()
+            for line in (2, 1):
+                reduce.add_y(DOWN_W, line)
+                reduce.fling(DOWN_W, (line,))
+            take_x(OUT_W)
+            reduce.fling(OUT_W)
+            reduce.settle(far_up)
+            cross_up().start()
         elif index == 7:
-            reduce.hop(UP_W, 1, (0,))
-            take_x(UP_W, (1,))
-            reduce.hop(UP_W, 0, (1,))
+            take_x(first)
+            reduce.fling(first)
         elif index == 8:
             for load in saved_loads(2):
                 load.wait()
             weight_part(1)
-            reduce.hop(UP_W, 2, (3,))
+            pass_up((3, 0))
         elif index == 9:
-            reduce.hop(UP_W, 2, (0,))
-            reduce.hop(UP_W, 1, (2, 1))
-            take_x(DOWN_W, (3, 0))
-            reduce.fling(DOWN_W, (3, 0))
+            pass_up((2,))
         elif index == 10:
-            take_x(DOWN_W, (2,))
-            reduce.fling(DOWN_W, (2,))
+            pass_up((1,))
+            reduce.settle(DOWN_W)
+            spread_of(DOWN_W).start()
         elif index == 11:
-            take_x(DOWN_W, (1,))
-            reduce.fling(DOWN_W, (1,))
+            take_x(UP_W, (3, 0))
+            reduce.fling(UP_W, (3, 0))
+            take_x(second)
+            reduce.fling(second)
 
     def step(index, carry):
         for when in range(1, 12):
@@ -1170,14 +1192,13 @@
 
         return carry
 
-    for load in sum_loads(OUT_W):
+    for load in sum_loads(far_up):
         load.wait()
-    reduce.hop(OUT_W, 0)
+    reduce.hop(far_up, 0)
     for load in saved_loads(0):
         load.wait()
     lax.fori_loop(0, heads * turns, step, 0)
 
-    weight_part(heads - 1)
     loads[1].wait()
     loads[2].wait()
 
@@ -1207,56 +1228,59 @@
         return remote(far_sum.at[rows], far_recv.at[rows], far_s.at[half], far_r.at[half], place.across_y)
 
     for half in range(halves):
+        near_send[0, half * part : (half + 1) * part, :] = part_for(1, half).astype(low)
+        share_near(0, half).start()
+    for half in range(halves):
         rows = slice(half * part, (half + 1) * part)
-        near_send[0, rows, :] = part_for(1, half).astype(low)
-        share_near(0, half).start()
-        far_sum[rows, :] = part_for(0, half).astype(low)
-        if half == 0:
-            taken = mul(memory_pick(slot_rows, 0), grads[...], NT).astype(low)
-            own_part = mul(memory_pick(local_rows, place.s * local_rows), resid_ref[...].astype(low))
-            memory_own[...] = (mul(taken, weight_ref[...], NT) + own_part).astype(low)
+        far_part = part_for(0, half)
         share_near(0, half).wait_recv()
-        far_sum[rows, :] = add_low(far_sum[rows, :], near_recv[0, rows, :])
+        far_sum[rows, :] = (far_part + near_recv[0, rows, :].astype(full)).astype(low)
         share_far(half).start()
+    reduce.settle(OUT_W)
+    sum_y(OUT_W).start()
+    weight_part(heads - 1)
+    take_x(UP_W, (2, 1))
+    reduce.fling(UP_W, (2, 1))
+    taken = mul(memory_pick(slot_rows, 0), grads[...], NT).astype(low)
+    own_part = mul(memory_pick(local_rows, place.s * local_rows), resid_ref[...].astype(low))
+    memory_own[...] = (mul(taken, weight_ref[...], NT) + own_part).astype(low)
     memory = Spread(place, memory_all, memory_own, share_send.at[DW_FIRST + heads], share_recv.at[DW_FIRST + heads])
     memory.start()
-    reduce.settle(UP_W)
-    sum_y(UP_W).start()
-    take_x(first)
-    reduce.fling(first)
-    reduce.add_x(OUT_W, 0)
-    sum_y(OUT_W).start()
     for half in range(halves):
         rows = slice(half * part, (half + 1) * part)
         near_send[1, rows, :] = part_for(2, half).astype(low)
         share_near(1, half).start()
-    take_x(second)
-    reduce.fling(second)
-    reduce.settle(DOWN_W)
-    spread_of(DOWN_W).start()
+    for half in range(halves):
+        resid_ref[half * part : (half + 1) * part, :] += part_for(3, half)
     take_x(last)
     reduce.fling(last)
-    add_last(UP_W)
-    for half in range(halves):
-        resid_ref[half * part : (half + 1) * part, :] += part_for(3, half)
-    for array in (first, second, last):
-        reduce.settle(array)
-        spread_of(array).start()
+    reduce.settle(first)
+    spread_of(first).start()
     add_last(OUT_W)
+    reduce.settle(second)
+    spread_of(second).start()
+    settle_up()
+    reduce.settle(last)
+    spread_of(last).start()
     memory.pass_on()
     for h in (heads - 1, 0, 1):
         spread_of(DW_FIRST + h).pass_on()
-    spread_of(DOWN_W).pass_on()
-    for array, out in ((UP_W, up_out), (OUT_W, out_out)):
+    for array in (UP_W, DOWN_W):
+        spread_of(array).pass_on()
+    for array, out in ((OUT_W, out_out),):
         columns = out.shape[1] // 2
         out[:, pl.ds(pl.multiple_of(place.c * columns, columns), columns)] = settled(array)[...]
         half_to_core(array).wait()
         out[:, pl.ds(pl.multiple_of((1 - place.c) * columns, columns), columns)] = share[array][1][...]
     for h in range(heads):
         spread_of(DW_FIRST + h).finish()
+    spread_of(UP_W).finish()
     spread_of(DOWN_W).finish()
     quarter = down_out.shape[0] // 4
+    part_columns = up_out.shape[1] // 4
     for member in range(4):
+        start = (2 * (member % 2) + member // 2) * part_columns
+        up_out[:, start : start + part_columns] = up_all[member]
         down_out[member * quarter : (member + 1) * quarter, :] = down_all[member]
     half = qkv_out.shape[0] // 2
     for kind in range(3):
@@ -1286,8 +1310,9 @@
         rows_at = place.s * local_rows + half * part + lax.broadcasted_iota(jnp.int32, (part, 1), 0)
         in_write = (rows_at >= length - MEM) & (rows_at < length)
         input_out[rows, :] = jnp.where((rows_at < MEM) | in_write, 0.0, grad_layer)
-    for array in range(DW_FIRST + heads):
+    for array in range(DW_FIRST + heads + 1):
         reduce.finish(array)
+    cross_up().wait_send()
     for turn in range(3):
         send_grad(turn).wait_send()
     for half in range(halves):
@@ -1300,7 +1325,7 @@
     q_x, k_t, k_wide, v_wide, mixed, row_stats = saved
     heads, _, slot_rows = q_x.shape
     width, local_rows = grad_own.shape
-    hidden = 2 * up_given.shape[3]
+    hidden = 32 * up_given.shape[3]
     shard, head_cols = width // 8, heads * HEAD
     half, small, piece = hidden // 2, width // 2, hidden // 32
     vmem = pl.BlockSpec(memory_space=pltpu.VMEM)
@@ -1332,18 +1357,20 @@
             held(head_cols, slot_rows), held(WIDE, local_rows), held(WIDE, local_rows), held(3 * head_cols, slot_rows),
             held(HEAD, slot_rows, kind=full), held(HEAD, slot_rows, kind=full),
             held(slot_rows, width), held(width, 3 * head_cols), held(local_rows, width, kind=full),
-            held(4, shard, half), held(4, 2, shard, small), held(4, piece, width),
-            held(heads, 8, *tall), held(4, piece, width),
-            held(4, shard, half), held(shard, small), held(4, piece, width), held(heads, 4, *tall),
-            held(2, 4, shard, half), held(2, 4, 2, shard, small), held(4, piece, width), held(heads, 4, *tall),
-            held(shard, half), held(shard, small), held(shard, half), held(shard, small),
+            held(4, piece, width), held(4, shard, small), held(4, piece, width), held(4, piece, width),
+            held(4, piece, width), held(heads, 8, *tall), held(2, 4, piece, width),
+            held(4, piece, width), held(4, shard, small), held(4, piece, width), held(heads, 4, *tall),
+            held(4, piece, width), held(4, shard, small), held(4, piece, width), held(heads, 4, *tall),
+            held(2, 4, piece, width),
+            held(piece, width), held(shard, small), held(4, piece, width), held(shard, small),
             held(4, piece, width), held(heads, 4, *tall),
             held(2, local_rows, width), held(2, local_rows, width), held(local_rows, width),
             held(local_rows, width), held(4, 32, width), held(32, width),
-            dma((3,)), dma((3,)), dma((3,)), dma((heads, 6)), dma((3, 4)), dma((arrays + 1, 3)),
+            dma((3,)), dma((3,)), dma((3,)), dma((heads, 6)), dma((5, 4)), dma((arrays + 1, 3)),
             dma((arrays + 1, 3)), dma((2, 2)), dma((2, 2)), dma((2,)), dma((2,)),
-            dma((4,)), dma((4,)), dma((arrays, 4)), dma((arrays, 4)),
-            dma((arrays, 2, 4)), dma((arrays, 2, 4)),
+            dma((1,)), dma((1,)),
+            dma((2, 4)), dma((2, 4)), dma((arrays, 4)), dma((arrays, 4)),
+            dma((arrays + 1, 2, 4)), dma((arrays + 1, 2, 4)),
         ],
         compiler_params=pltpu.CompilerParams(
             vmem_limit_bytes=VMEM_BYTES, collective_id=1, has_side_effects=True
@@ -1486,9 +1513,18 @@
     def down_save(column, line):
         return pltpu.make_async_copy(down_sum.at[column, line], down_out.at[column, line], save_sem.at[2, column, line])
 
-    def side_save(array, column, line):
-        out = out_out.at[line, column] if array == 1 else up_out.at[column, line]
-        return pltpu.make_async_copy(side_slot(array, line, column), out, save_sem.at[array, column, line])
+    def side_saves(array, column, line):
+        if array == 1:
+            return [pltpu.make_async_copy(
+                side_slot(1, line, column), out_out.at[line, column], save_sem.at[1, column, line]
+            )]
+        return [
+            pltpu.make_async_copy(
+                up_sum.at[column, line, :, chunk_lanes(place.y if far == 0 else 1 - place.y)],
+                up_out.at[column, line, far], save_sem.at[3 * far, column, line],
+            )
+            for far in range(2)
+        ]
 
     def add_far(column, line):
         down_share(line, column, 1).wait_recv()
@@ -1499,12 +1535,20 @@
     def down_chunk(line, carry):
         lanes = chunk_lanes(line)
         down_grad[lanes, :] = mul(hidden[:, lanes], grad_down[...], TN).astype(low)
-        for column in range(2):
-            for far in range(2):
+        for far in (1, 0):
+            for column in (1, 0):
                 down_share(line, column, far).start()
+
+        @pl.when(line > 0)
+        def _():
+            add_far(1, line - 1)
+            over_y(line - 1).start()
+
         return carry
 
     lax.fori_loop(0, 4, down_chunk, 0)
+    add_far(1, 3)
+    over_y(3).start()
     grad_mid[...] = grad_two[...]
 
     def back_chunk(turn, carry):
@@ -1514,12 +1558,6 @@
         up_total[0:1, lanes] = column_total(grad_up.astype(full))
         up_grad[:, lanes] = mul(middle_low[...], grad_up, TN).astype(low)
         grad_mid[...] += mul(grad_up, up_w[:, lanes], NT)
-
-        @pl.when(turn == 0)
-        def _():
-            for line in LINES:
-                add_far(1, line)
-                over_y(line).start()
 
         @pl.when(turn == 1)
         def _():
@@ -1560,7 +1598,8 @@
         slot = side_slot(array, line, column)
         side_share(array, line, column).wait_recv()
         slot[...] = add_low(slot[...], side_piece((up_grad, out_grad)[array], line, column, place.c)[...])
-        side_save(array, column, line).start()
+        for save in side_saves(array, column, line):
+            save.start()
 
     for line in LINES:
         add_down(0, line)
@@ -1585,7 +1624,8 @@
         for line in range(4):
             for array in range(2):
                 side_share(array, line, column).wait_send()
-                side_save(array, column, line).wait()
+                for save in side_saves(array, column, line):
+                    save.wait()
             for far in range(2):
                 down_share(line, column, far).wait_send()
             down_save(column, line).wait()
@@ -1612,14 +1652,14 @@
         out_specs=[vmem] * 4 + [anywhere] * 3,
         out_shape=[
             shaped(rows, width), shaped(rows, width, kind=full), shaped(width, rows),
-            shaped(8, 16, 4 * shard, kind=full), shaped(*up_parts), shaped(*down_parts), shaped(*out_parts),
+            shaped(8, 16, 4 * shard, kind=full), shaped(*down_parts), shaped(*down_parts), shaped(*out_parts),
         ],
         scratch_shapes=[
             held(rows, width), held(width, rows), held(width, ff), held(ff, width), held(width, width), held(rows, ff), held(rows, ff, kind=full),
             held(rows, width, kind=full), held(rows, width), held(rows, width), held(rows, width, kind=full),
             held(rows, width, kind=full), held(8, width, kind=full), held(8, ff, kind=full),
             held(width, ff), held(ff, width), held(width, width), held(*up_parts), held(*down_parts),
-            held(*out_parts), held(4, ff // 32, width), dma((11,)), dma((3, 2, 4)), dma((4, 2, 4)),
+            held(*out_parts), held(4, ff // 32, width), dma((11,)), dma((4, 2, 4)), dma((4, 2, 4)),
             dma((4, 2, 4)), dma((4,)), dma((4,)),
         ],
         compiler_params=pltpu.CompilerParams(

time: 217 us -> 208 us (0.959)
  Pallas kernels: 210 us -> 202 us
    pallas_call x1, Pallas kernels: 93.3 us -> 87.1 us  [back(): pl.pallas_call(back_kernel, in_specs=[pl.BlockSpec(memory_space=pltpu.SME...]
where the time goes in v8:
time: 208 us; the launch traced here: 207 us
  Pallas kernels  202 us (97%)
  other arithmetic  2.68 us (1%)
    pallas_call x1, Pallas kernels, back(): pl.pallas_call(back_kernel, in_specs=[pl.BlockSpec(memory_space=pltpu.SME...  87.1 us
    pallas_call x1, Pallas kernels, front(): pl.pallas_call(front_kernel, in_specs=[pl.BlockSpec(memory_space=pltpu.SM...  74.4 us
    pallas_call x1, Pallas kernels, middle_part(): pl.pallas_call(middle_kernel, in_specs=[pl.BlockSpec(memory_space=pltpu.S...  36.1 us
    pallas_call x1, Pallas kernels, finish(): pl.pallas_call(finish_kernel, grid=(steps,), in_specs=[rows(output), rows...  4.46 us

profile of v8, /device:TPU:9, one launch (start us, length us, event | category | flops | bytes accessed | tf_op | source)
XLA Modules:
  0.0 207.3 jit_solution(10237999458873176696)
XLA Ops:
  1.3 0.7 reshape.88
  2.0 0.7 reshape.92
  2.6 1.4 convert_add_fusion.vectors_in
  4.0 74.4 %front.1 = (f32[8,768]{1,0:T(8,128)}, f32[8,3072]{1,0:T(8,128)}, bf16[2048,768]{1,0:T(8,128)(2,1)}, bf16[768,576]{1,0:T(8,128)(2,1)}, bf16[3,64,2048]{2,1,0:T(8,...) custom-call(s32[1]{0:T(128)S(6)} %copy.33.length_ref, ...), custom_call_target="tpu_custom_call" | custom-call | tf_op jit(solution)/shard_map/front/pallas_call | solution.py:755
  78.4 36.1 %middle.1 = (bf16[512,768]{1,0:T(8,128)(2,1)}, f32[512,768]{1,0:T(8,128)}, bf16[768,512]{1,0:T(8,128)(2,1)}, f32[8,16,384]{2,1,0:T(8,128)}, bf16[2,4,2,96,768]{4...) custom-call(s32[1]{0:T(128)S(6)} %copy.33.length_ref, ...), custom_call_target="tpu_custom_call" | custom-call | tf_op jit(solution)/shard_map/middle/pallas_call | solution.py:1649
  114.5 87.1 %back.1 = (f32[512,768]{1,0:T(8,128)}, f32[10,768]{1,0:T(8,128)}, f32[10,768]{1,0:T(8,128)}, bf16[96,2304]{1,0:T(8,128)(2,1)}, f32[16,384]{1,0:T(8,128)}, /*inde...) custom-call(s32[1]{0:T(128)S(6)} %copy.33.length_ref, ...), custom_call_target="tpu_custom_call" | custom-call | tf_op jit(solution)/shard_map/back/pallas_call | solution.py:1340
  201.6 4.5 %finish.1 = (bf16[512,768]{1,0:T(8,128)(2,1)}, f32[512,768]{1,0:T(8,128)}, f32[10,1,768]{2,1,0:T(1,128)}, f32[10,1,768]{2,1,0:T(1,128)}, f32[96,2304]{1,0:T(8,12...) custom-call(bf16[512,768]{1,0:T(8,128)(2,1)} %get-tuple-element.68.o, ...), custom_call_target="tpu_custom_call" | custom-call | tf_op jit(solution)/shard_map/finish/pallas_call | solution.py:1713
  206.1 1.3 reduce

commit v9 on v8

--- a/solution.py
+++ b/solution.py
@@ -547,18 +547,23 @@
         copy.start()
     for relation in (1, 4):
         gather.arrive_z(QKV_W, relation)
+    gather.arrive_z(DOWN_W, OWN, along=False)
     gather.pair_out(own_copies()[2])
     for relation in (2, 5):
         gather.arrive_z(QKV_W, relation)
-    gather.arrive_z(UP_W, OWN, across=False)
+    gather.arrive_z(DOWN_W, OWN, across=False)
+    gather.arrive_z(UP_W, OWN)
     rows_from(0, 1).wait_recv()
     pass_rows(0, False).start()
     for relation in (3, 6):
         gather.arrive_z(QKV_W, relation)
-    gather.arrive_z(UP_W, OWN, along=False)
-    gather.arrive_z(DOWN_W, OWN)
+    for relation in (1, 4):
+        gather.arrive_z(DOWN_W, relation)
     for relation in range(RELATIONS):
         gather.arrive_x(QKV_W, relation)
+    for relation in (1, 4):
+        gather.arrive_z(OUT_W, relation)
+        gather.arrive_z(UP_W, relation)
 
     for source in range(8):
         weight_ref[source * shard : (source + 1) * shard, :] = pieces[source, :, :columns]
@@ -580,12 +585,7 @@
     project(2 * place.y + 1 - place.c)
     rows_from(1, 1).wait_recv()
     pass_rows(1, False).start()
-    for relation in (1, 4):
-        gather.arrive_z(UP_W, relation)
-        gather.arrive_z(OUT_W, relation)
     project(2 * (1 - place.y) + place.c)
-    for relation in (1, 4):
-        gather.arrive_z(DOWN_W, relation)
 
     def scatter_vector(target, index, size, first):
         for source in range(8):
@@ -621,30 +621,39 @@
         ]
 
     def chores(step):
-        if step == 1:
+        if step == 0:
+            gather.arrive_x(DOWN_W, OWN)
+            for relation in (2, 5):
+                gather.arrive_z(DOWN_W, relation)
+        elif step == 1:
             gather.arrive_x(UP_W, OWN)
+            for relation in (2, 5):
+                gather.arrive_z(OUT_W, relation)
         elif step == 2:
-            for relation in (2, 5):
-                gather.arrive_z(UP_W, relation)
-            gather.arrive_x(DOWN_W, OWN)
-        elif step == 3:
             for relation in (1, 4):
+                gather.arrive_x(DOWN_W, relation)
                 gather.arrive_y(relation, 0)
         elif step == 4:
             for relation in (2, 5):
-                gather.arrive_z(OUT_W, relation)
+                gather.arrive_z(UP_W, relation)
+            gather.arrive_y(OWN, 1)
             for save in head_saves(0):
                 save.start()
         elif step == 5:
-            for relation in (2, 5):
-                gather.arrive_z(DOWN_W, relation)
-            gather.arrive_y(OWN, 1)
-        elif step == 6:
             for relation in (1, 4):
                 gather.arrive_x(UP_W, relation)
+            for relation in (3, 6):
+                gather.arrive_z(DOWN_W, relation)
+        elif step == 6:
+            for relation in (2, 5):
+                gather.arrive_x(DOWN_W, relation)
+                gather.arrive_y(relation, 0)
+        elif step == 7:
+            for relation in (3, 6):
+                gather.arrive_z(OUT_W, relation)
         elif step == 8:
-            for relation in (2, 5):
-                gather.arrive_y(relation, 0)
+            for relation in (1, 4):
+                gather.arrive_y(relation, 1)
             for save in head_saves(1):
                 save.start()
         elif step == 9:
@@ -652,12 +661,13 @@
                 gather.arrive_z(UP_W, relation)
             for relation in (2, 5):
                 gather.arrive_x(UP_W, relation)
+        elif step == 10:
+            for relation in (3, 6):
+                gather.arrive_x(DOWN_W, relation)
+                gather.arrive_y(relation, 0)
         elif step == 11:
-            for relation in (3, 6):
-                gather.arrive_z(OUT_W, relation)
-                gather.arrive_z(DOWN_W, relation)
-            for relation in (1, 4):
-                gather.arrive_x(DOWN_W, relation)
+            for relation in (2, 5):
+                gather.arrive_y(relation, 1)
 
     def send_mixed(h, turn, arriving=False):
         member = place.member(turn)
@@ -706,16 +716,9 @@
     for save in head_saves(2):
         save.start()
     for relation in (3, 6):
-        gather.arrive_x(UP_W, relation)
-    for relation in (2, 5):
-        gather.arrive_x(DOWN_W, relation)
-    for relation in (1, 4):
         gather.arrive_y(relation, 1)
     for relation in (3, 6):
-        gather.arrive_y(relation, 0)
-        gather.arrive_x(DOWN_W, relation)
-    for relation in (2, 5, 3, 6):
-        gather.arrive_y(relation, 1)
+        gather.arrive_x(UP_W, relation)
     for array in (UP_W, OUT_W, DOWN_W, QKV_W):
         gather.finish(array)
     for copy in own_copies()[:2]:
@@ -986,7 +989,6 @@
         from_z[DW_FIRST + h] = dw_z.at[h]
     sums[far_up], from_z[far_up] = far_sum_up, far_z
     reduce = Reduce(place, given, sums, across_up, both_y, from_x, from_z, last, sems)
-    greet(place, True)
 
     peers = (place.across_y, place.diagonal, place.core)
 
@@ -1017,12 +1019,13 @@
     def across_loads():
         return [reduce.load(UP_W, 1, line, mine_sem.at[DW_FIRST + 1, line]) for line in LINES]
 
-    for turn in range(3):
-        send_grad(turn).start()
     for load in sum_loads(far_up):
         load.start()
     for load in saved_loads(0):
         load.start()
+    greet(place, True)
+    for turn in (1, 0, 2):
+        send_grad(turn).start()
     loads = []
     for index, (src, dst) in enumerate(((rows_in, rows_ref), (weight_in, weight_ref), (resid_in, resid_ref))):
         loads.append(pltpu.make_async_copy(src, dst, local_sem.at[index]))
@@ -1223,9 +1226,9 @@
             place.core,
         )
 
-    def share_far(half):
-        rows = pl.ds(half * part, part)
-        return remote(far_sum.at[rows], far_recv.at[rows], far_s.at[half], far_r.at[half], place.across_y)
+    def share_far(quarter):
+        rows = pl.ds(quarter * (part // 2), part // 2)
+        return remote(far_sum.at[rows], far_recv.at[rows], far_s.at[quarter], far_r.at[quarter], place.across_y)
 
     for half in range(halves):
         near_send[0, half * part : (half + 1) * part, :] = part_for(1, half).astype(low)
@@ -1235,10 +1238,12 @@
         far_part = part_for(0, half)
         share_near(0, half).wait_recv()
         far_sum[rows, :] = (far_part + near_recv[0, rows, :].astype(full)).astype(low)
-        share_far(half).start()
+        share_far(2 * half).start()
+        if half == 0:
+            share_far(1).start()
+    weight_part(heads - 1)
     reduce.settle(OUT_W)
     sum_y(OUT_W).start()
-    weight_part(heads - 1)
     take_x(UP_W, (2, 1))
     reduce.fling(UP_W, (2, 1))
     taken = mul(memory_pick(slot_rows, 0), grads[...], NT).astype(low)
@@ -1262,6 +1267,7 @@
     settle_up()
     reduce.settle(last)
     spread_of(last).start()
+    share_far(3).start()
     memory.pass_on()
     for h in (heads - 1, 0, 1):
         spread_of(DW_FIRST + h).pass_on()
@@ -1305,7 +1311,8 @@
     for half in range(halves):
         rows = slice(half * part, (half + 1) * part)
         share_near(1, half).wait_recv()
-        share_far(half).wait_recv()
+        for quarter in (2 * half, 2 * half + 1):
+            share_far(quarter).wait_recv()
         grad_layer = resid_ref[rows, :] + near_recv[1, rows, :].astype(full) + far_recv[rows, :].astype(full)
         rows_at = place.s * local_rows + half * part + lax.broadcasted_iota(jnp.int32, (part, 1), 0)
         in_write = (rows_at >= length - MEM) & (rows_at < length)
@@ -1318,7 +1325,8 @@
     for half in range(halves):
         for index in range(2):
             share_near(index, half).wait_send()
-        share_far(half).wait_send()
+        for quarter in (2 * half, 2 * half + 1):
+            share_far(quarter).wait_send()
 
 
 def back(lengths, grad_own, saved, vectors, rows, weight, resid, up_given, down_given, out_given):
@@ -1367,7 +1375,7 @@
             held(2, local_rows, width), held(2, local_rows, width), held(local_rows, width),
             held(local_rows, width), held(4, 32, width), held(32, width),
             dma((3,)), dma((3,)), dma((3,)), dma((heads, 6)), dma((5, 4)), dma((arrays + 1, 3)),
-            dma((arrays + 1, 3)), dma((2, 2)), dma((2, 2)), dma((2,)), dma((2,)),
+            dma((arrays + 1, 3)), dma((2, 2)), dma((2, 2)), dma((4,)), dma((4,)),
             dma((1,)), dma((1,)),
             dma((2, 4)), dma((2, 4)), dma((arrays, 4)), dma((arrays, 4)),
             dma((arrays + 1, 2, 4)), dma((arrays + 1, 2, 4)),

time: 208 us -> 200 us (0.962)
  Pallas kernels: 202 us -> 193 us
    pallas_call x1, Pallas kernels: 74.4 us -> 67.6 us  [front(): pl.pallas_call(front_kernel, in_specs=[pl.BlockSpec(memory_space=pltpu.SM...]
    pallas_call x1, Pallas kernels: 87.1 us -> 84.5 us  [back(): pl.pallas_call(back_kernel, in_specs=[pl.BlockSpec(memory_space=pltpu.SME...]
where the time goes in v9:
time: 200 us; the launch traced here: 198 us
  Pallas kernels  193 us (96%)
  other arithmetic  2.68 us (1%)
    pallas_call x1, Pallas kernels, back(): pl.pallas_call(back_kernel, in_specs=[pl.BlockSpec(memory_space=pltpu.SME...  84.5 us
    pallas_call x1, Pallas kernels, front(): pl.pallas_call(front_kernel, in_specs=[pl.BlockSpec(memory_space=pltpu.SM...  67.6 us
    pallas_call x1, Pallas kernels, middle_part(): pl.pallas_call(middle_kernel, in_specs=[pl.BlockSpec(memory_space=pltpu.S...  36.1 us
    pallas_call x1, Pallas kernels, finish(): pl.pallas_call(finish_kernel, grid=(steps,), in_specs=[rows(output), rows...  4.46 us

profile of v9, /device:TPU:9, one launch (start us, length us, event | category | flops | bytes accessed | tf_op | source)
XLA Modules:
  0.0 198.0 jit_solution(11297319094367078112)
XLA Ops:
  1.3 0.7 reshape.88
  2.0 0.7 reshape.92
  2.6 1.4 convert_add_fusion.vectors_in
  4.0 67.6 %front.1 = (f32[8,768]{1,0:T(8,128)}, f32[8,3072]{1,0:T(8,128)}, bf16[2048,768]{1,0:T(8,128)(2,1)}, bf16[768,576]{1,0:T(8,128)(2,1)}, bf16[3,64,2048]{2,1,0:T(8,...) custom-call(s32[1]{0:T(128)S(6)} %copy.33.length_ref, ...), custom_call_target="tpu_custom_call" | custom-call | tf_op jit(solution)/shard_map/front/pallas_call | solution.py:758
  71.7 36.1 %middle.1 = (bf16[512,768]{1,0:T(8,128)(2,1)}, f32[512,768]{1,0:T(8,128)}, bf16[768,512]{1,0:T(8,128)(2,1)}, f32[8,16,384]{2,1,0:T(8,128)}, bf16[2,4,2,96,768]{4...) custom-call(s32[1]{0:T(128)S(6)} %copy.33.length_ref, ...), custom_call_target="tpu_custom_call" | custom-call | tf_op jit(solution)/shard_map/middle/pallas_call | solution.py:1657
  107.7 84.5 %back.1 = (f32[512,768]{1,0:T(8,128)}, f32[10,768]{1,0:T(8,128)}, f32[10,768]{1,0:T(8,128)}, bf16[96,2304]{1,0:T(8,128)(2,1)}, f32[16,384]{1,0:T(8,128)}, /*inde...) custom-call(s32[1]{0:T(128)S(6)} %copy.33.length_ref, ...), custom_call_target="tpu_custom_call" | custom-call | tf_op jit(solution)/shard_map/back/pallas_call | solution.py:1348
  192.2 4.5 %finish.1 = (bf16[512,768]{1,0:T(8,128)(2,1)}, f32[512,768]{1,0:T(8,128)}, f32[10,1,768]{2,1,0:T(1,128)}, f32[10,1,768]{2,1,0:T(1,128)}, f32[96,2304]{1,0:T(8,12...) custom-call(bf16[512,768]{1,0:T(8,128)(2,1)} %get-tuple-element.68.o, ...), custom_call_target="tpu_custom_call" | custom-call | tf_op jit(solution)/shard_map/finish/pallas_call | solution.py:1721
  196.7 1.3 reduce

commit v10 on v9

--- a/solution.py
+++ b/solution.py
@@ -140,10 +140,16 @@
     parts = [part.astype(full) for part in three_parts(-row_stats[h, 0:1, lanes])]
     q_here[:HEAD, :] = q_x[h, :HEAD, lanes]
     q_here[HEAD:, :] = stack_rows([jnp.ones((1, columns), full)] + parts, columns)
-    probs = jnp.exp(mul(k_wide[h], q_here[...]))
-    grad_scores = (probs * mul(v_wide[h], do_x[...])).astype(low)
-    value_part = mul(grad, probs.astype(low), NT)
-    key_part = mul(q_here[:HEAD, :], grad_scores, NT)
+    value_part, key_part, query_parts = None, None, []
+    for start in range(0, columns, columns // 2):
+        side = slice(start, start + columns // 2)
+        probs = jnp.exp(mul(k_wide[h], q_here[:, side]))
+        grad_scores = (probs * mul(v_wide[h], do_x[:, side])).astype(low)
+        value_more = mul(do_x[:HEAD, side], probs.astype(low), NT)
+        key_more = mul(q_here[:HEAD, side], grad_scores, NT)
+        value_part = value_more if value_part is None else value_part + value_more
+        key_part = key_more if key_part is None else key_part + key_more
+        query_parts.append(mul(k_t[own, :], grad_scores) * HEAD**-0.5)
 
     @pl.when(first)
     def _():
@@ -155,7 +161,7 @@
         grad_v[...] += value_part
         grad_k[...] += key_part
 
-    query_part = mul(k_t[own, :], grad_scores) * HEAD**-0.5
+    query_part = jnp.concatenate(query_parts, axis=1)
     grads[pl.ds(pl.multiple_of(3 * h * HEAD, HEAD), HEAD), lanes] = query_part.astype(low)
 
 
@@ -1147,11 +1153,8 @@
             reduce.hop(far_up, 2)
         elif index == 5:
             take_x(DOWN_W)
-            for line in (3, 0):
-                reduce.add_y(DOWN_W, line)
-                reduce.fling(DOWN_W, (line,))
         elif index == 6:
-            for line in (2, 1):
+            for line in LINES:
                 reduce.add_y(DOWN_W, line)
                 reduce.fling(DOWN_W, (line,))
             take_x(OUT_W)
@@ -1170,13 +1173,11 @@
             pass_up((2,))
         elif index == 10:
             pass_up((1,))
+        elif index == 11:
+            take_x(second)
+            reduce.fling(second)
             reduce.settle(DOWN_W)
             spread_of(DOWN_W).start()
-        elif index == 11:
-            take_x(UP_W, (3, 0))
-            reduce.fling(UP_W, (3, 0))
-            take_x(second)
-            reduce.fling(second)
 
     def step(index, carry):
         for when in range(1, 12):
@@ -1241,11 +1242,11 @@
         share_far(2 * half).start()
         if half == 0:
             share_far(1).start()
+    take_x(UP_W)
+    reduce.fling(UP_W)
     weight_part(heads - 1)
     reduce.settle(OUT_W)
     sum_y(OUT_W).start()
-    take_x(UP_W, (2, 1))
-    reduce.fling(UP_W, (2, 1))
     taken = mul(memory_pick(slot_rows, 0), grads[...], NT).astype(low)
     own_part = mul(memory_pick(local_rows, place.s * local_rows), resid_ref[...].astype(low))
     memory_own[...] = (mul(taken, weight_ref[...], NT) + own_part).astype(low)

time: 200 us -> 197 us (0.985)
  Pallas kernels: 193 us -> 190 us
    pallas_call x1, Pallas kernels: 84.5 us -> 81.5 us  [back(): pl.pallas_call(back_kernel, in_specs=[pl.BlockSpec(memory_space=pltpu.SME...]
where the time goes in v10:
time: 197 us; the launch traced here: 195 us
  Pallas kernels  190 us (96%)
  other arithmetic  2.68 us (1%)
    pallas_call x1, Pallas kernels, back(): pl.pallas_call(back_kernel, in_specs=[pl.BlockSpec(memory_space=pltpu.SME...  81.5 us
    pallas_call x1, Pallas kernels, front(): pl.pallas_call(front_kernel, in_specs=[pl.BlockSpec(memory_space=pltpu.SM...  67.6 us
    pallas_call x1, Pallas kernels, middle_part(): pl.pallas_call(middle_kernel, in_specs=[pl.BlockSpec(memory_space=pltpu.S...  36.1 us
    pallas_call x1, Pallas kernels, finish(): pl.pallas_call(finish_kernel, grid=(steps,), in_specs=[rows(output), rows...  4.46 us

profile of v10, /device:TPU:9, one launch (start us, length us, event | category | flops | bytes accessed | tf_op | source)
XLA Modules:
  0.0 194.9 jit_solution(13212810510822613575)
XLA Ops:
  1.3 0.7 reshape.88
  2.0 0.7 reshape.92
  2.6 1.4 convert_add_fusion.vectors_in
  4.0 67.6 %front.1 = (f32[8,768]{1,0:T(8,128)}, f32[8,3072]{1,0:T(8,128)}, bf16[2048,768]{1,0:T(8,128)(2,1)}, bf16[768,576]{1,0:T(8,128)(2,1)}, bf16[3,64,2048]{2,1,0:T(8,...) custom-call(s32[1]{0:T(128)S(6)} %copy.33.length_ref, ...), custom_call_target="tpu_custom_call" | custom-call | tf_op jit(solution)/shard_map/front/pallas_call | solution.py:764
  71.7 36.1 %middle.1 = (bf16[512,768]{1,0:T(8,128)(2,1)}, f32[512,768]{1,0:T(8,128)}, bf16[768,512]{1,0:T(8,128)(2,1)}, f32[8,16,384]{2,1,0:T(8,128)}, bf16[2,4,2,96,768]{4...) custom-call(s32[1]{0:T(128)S(6)} %copy.33.length_ref, ...), custom_call_target="tpu_custom_call" | custom-call | tf_op jit(solution)/shard_map/middle/pallas_call | solution.py:1658
  107.7 81.5 %back.1 = (f32[512,768]{1,0:T(8,128)}, f32[10,768]{1,0:T(8,128)}, f32[10,768]{1,0:T(8,128)}, bf16[96,2304]{1,0:T(8,128)(2,1)}, f32[16,384]{1,0:T(8,128)}, /*inde...) custom-call(s32[1]{0:T(128)S(6)} %copy.33.length_ref, ...), custom_call_target="tpu_custom_call" | custom-call | tf_op jit(solution)/shard_map/back/pallas_call | solution.py:1349
  189.2 4.5 %finish.1 = (bf16[512,768]{1,0:T(8,128)(2,1)}, f32[512,768]{1,0:T(8,128)}, f32[10,1,768]{2,1,0:T(1,128)}, f32[10,1,768]{2,1,0:T(1,128)}, f32[96,2304]{1,0:T(8,12...) custom-call(bf16[512,768]{1,0:T(8,128)(2,1)} %get-tuple-element.68.o, ...), custom_call_target="tpu_custom_call" | custom-call | tf_op jit(solution)/shard_map/finish/pallas_call | solution.py:1722
  193.6 1.3 reduce

commit v11 on v10

--- a/solution.py
+++ b/solution.py
@@ -1239,8 +1239,8 @@
         far_part = part_for(0, half)
         share_near(0, half).wait_recv()
         far_sum[rows, :] = (far_part + near_recv[0, rows, :].astype(full)).astype(low)
-        share_far(2 * half).start()
         if half == 0:
+            share_far(0).start()
             share_far(1).start()
     take_x(UP_W)
     reduce.fling(UP_W)
@@ -1262,13 +1262,14 @@
     reduce.fling(last)
     reduce.settle(first)
     spread_of(first).start()
-    add_last(OUT_W)
     reduce.settle(second)
     spread_of(second).start()
+    share_far(2).start()
     settle_up()
     reduce.settle(last)
     spread_of(last).start()
     share_far(3).start()
+    add_last(OUT_W)
     memory.pass_on()
     for h in (heads - 1, 0, 1):
         spread_of(DW_FIRST + h).pass_on()

time: 197 us -> 197 us (level)
  no operation moved by 1% of the time
where the time goes in v11:
time: 197 us; the launch traced here: 195 us
  Pallas kernels  190 us (96%)
  other arithmetic  2.68 us (1%)
    pallas_call x1, Pallas kernels, back(): pl.pallas_call(back_kernel, in_specs=[pl.BlockSpec(memory_space=pltpu.SME...  81.5 us
    pallas_call x1, Pallas kernels, front(): pl.pallas_call(front_kernel, in_specs=[pl.BlockSpec(memory_space=pltpu.SM...  67.6 us
    pallas_call x1, Pallas kernels, middle_part(): pl.pallas_call(middle_kernel, in_specs=[pl.BlockSpec(memory_space=pltpu.S...  36.1 us
    pallas_call x1, Pallas kernels, finish(): pl.pallas_call(finish_kernel, grid=(steps,), in_specs=[rows(output), rows...  4.46 us

profile of v11, /device:TPU:9, one launch (start us, length us, event | category | flops | bytes accessed | tf_op | source)
XLA Modules:
  0.0 194.9 jit_solution(16112808281827287058)
XLA Ops:
  1.3 0.7 reshape.88
  2.0 0.7 reshape.92
  2.6 1.4 convert_add_fusion.vectors_in
  4.0 67.6 %front.1 = (f32[8,768]{1,0:T(8,128)}, f32[8,3072]{1,0:T(8,128)}, bf16[2048,768]{1,0:T(8,128)(2,1)}, bf16[768,576]{1,0:T(8,128)(2,1)}, bf16[3,64,2048]{2,1,0:T(8,...) custom-call(s32[1]{0:T(128)S(6)} %copy.33.length_ref, ...), custom_call_target="tpu_custom_call" | custom-call | tf_op jit(solution)/shard_map/front/pallas_call | solution.py:764
  71.7 36.1 %middle.1 = (bf16[512,768]{1,0:T(8,128)(2,1)}, f32[512,768]{1,0:T(8,128)}, bf16[768,512]{1,0:T(8,128)(2,1)}, f32[8,16,384]{2,1,0:T(8,128)}, bf16[2,4,2,96,768]{4...) custom-call(s32[1]{0:T(128)S(6)} %copy.33.length_ref, ...), custom_call_target="tpu_custom_call" | custom-call | tf_op jit(solution)/shard_map/middle/pallas_call | solution.py:1659
  107.7 81.5 %back.1 = (f32[512,768]{1,0:T(8,128)}, f32[10,768]{1,0:T(8,128)}, f32[10,768]{1,0:T(8,128)}, bf16[96,2304]{1,0:T(8,128)(2,1)}, f32[16,384]{1,0:T(8,128)}, /*inde...) custom-call(s32[1]{0:T(128)S(6)} %copy.33.length_ref, ...), custom_call_target="tpu_custom_call" | custom-call | tf_op jit(solution)/shard_map/back/pallas_call | solution.py:1350
  189.2 4.5 %finish.1 = (bf16[512,768]{1,0:T(8,128)(2,1)}, f32[512,768]{1,0:T(8,128)}, f32[10,1,768]{2,1,0:T(1,128)}, f32[10,1,768]{2,1,0:T(1,128)}, f32[96,2304]{1,0:T(8,12...) custom-call(bf16[512,768]{1,0:T(8,128)(2,1)} %get-tuple-element.68.o, ...), custom_call_target="tpu_custom_call" | custom-call | tf_op jit(solution)/shard_map/finish/pallas_call | solution.py:1723
  193.6 1.3 reduce
